TPU v7x, 32 devices: a whole 2x2x4 slice. The times are simulated.
32 devices in a mesh: groups: 2 (over x), tile: 16 (over z, y, core).
Axes of the slice: x: 2, y: 2, z: 4, core: 2. Of those that a mesh axis runs over, the one named last changes fastest.
Arguments:
- frame_one: bfloat16 [256, 128, 128], P(('groups', 'tile')), parts along dimension 0, may hold values from -6 to 6
- frame_two: bfloat16 [256, 128, 128], P(('groups', 'tile')), parts along dimension 0, may hold values from -6 to 6
- conv_weight: bfloat16 [3, 3, 128, 256], replicated, may hold values from -0.1875 to 0.1875
- partners: int32 [32, 4], P(('groups', 'tile')), parts along dimension 0, may hold values from 0 to 15, as said below
- counts: int32 [32], P(('groups', 'tile')), parts along dimension 0, may hold values from 3 to 4
- targets: int32 [256, 128], P(('groups', 'tile')), parts along dimension 0, may hold values from 0 to 4095, as said below
Outputs:
- grad_one: bfloat16 [256, 128, 128], P(('groups', 'tile')), parts along dimension 0
- grad_two: bfloat16 [256, 128, 128], P(('groups', 'tile')), parts along dimension 0
There are 2 independent parts, one for each index of `groups`. A program takes and returns all parts, laid end to end along the dimension named above; an argument that names none is the same for every part. Nothing has to cross between parts.
Inputs may be any that keep to these rules, and one draw needn't show every extreme that they name: `partners`: row t holds counts[t] distinct tiles within 2 of t, then copies of t. `targets`: A pixel's slot v // 1024 is below counts of its tile.
All inputs are finite; a program needn't handle non-finite values.
Results may differ from a plain program's by a relative error of at most 0.005.
Values may be sent and summed in bfloat16 or wider, within the bound.
No kernel may reach another device: no remote copies, remote signals or barrier semaphores. Data moves between devices by JAX's collectives and lax.ppermute only.
A program may use at most 64 MiB of HBM per device.

v0:
```python
import math

import jax
import jax.numpy as jnp
from jax import lax
from jax.sharding import PartitionSpec as P

LEVELS = 4
RADIUS = 2
SLOTS = 4


score_shift = 2.0


def extended(cells, sides, width):
    for axis, dim in sides:
        count = lax.axis_size(axis)
        ends = count - 1
        head = lax.slice_in_dim(cells, 0, width, axis=dim)
        tail = lax.slice_in_dim(cells, cells.shape[dim] - width, cells.shape[dim], axis=dim)
        cells = jnp.concatenate(
            [
                lax.ppermute(tail, axis, [(i, (i + 1) % count) for i in range(ends)]),
                cells,
                lax.ppermute(head, axis, [((i + 1) % count, i) for i in range(ends)]),
            ],
            axis=dim,
        )
    return cells


def from_behind(block, axis, distance):
    devices = range(lax.axis_size(axis))
    route = [(i - distance, i) for i in devices if i - distance in devices]
    return lax.ppermute(block, axis, route)


def pool_levels(features):
    num_rows, num_cols, channels = features.shape
    widened = features.astype(jnp.float32)
    stacked = []
    for level_idx in range(LEVELS):
        stride = 2**level_idx
        pooled = widened.reshape(
            num_rows // stride, stride, num_cols // stride, stride, channels
        ).mean(axis=(1, 3))
        stacked.append(pooled.reshape(-1, channels))
    return jnp.concatenate(stacked, 0).astype(jnp.bfloat16)


def unpool_levels(summed, num_rows, num_cols):
    channels = summed.shape[1]
    result = jnp.zeros((num_rows, num_cols, channels), jnp.float32)
    offset = 0
    for level_idx in range(LEVELS):
        stride = 2**level_idx
        cells = num_rows // stride * (num_cols // stride)
        piece = summed[offset : offset + cells].reshape(
            num_rows // stride, 1, num_cols // stride, 1, channels
        )
        piece = jnp.broadcast_to(
            piece, (num_rows // stride, stride, num_cols // stride, stride, channels)
        )
        result = result + piece.reshape(num_rows, num_cols, channels) / float(stride * stride)
        offset += cells
    return result.reshape(num_rows * num_cols, channels)


def column_scales(num_rows, num_cols, channels):
    pieces = []
    for level_idx in range(LEVELS):
        stride = 2**level_idx
        cells = num_rows // stride * (num_cols // stride)
        pieces.append(jnp.full((cells,), 2.0**level_idx / math.sqrt(channels), jnp.float32))
    return jnp.concatenate(pieces, 0)


def label_columns(target_row, num_rows, num_cols):
    pixels = num_rows * num_cols
    slot_ids = target_row // pixels
    inside = target_row % pixels
    row_ids = inside // num_cols
    col_ids = inside % num_cols
    columns = []
    offset = 0
    for level_idx in range(LEVELS):
        stride = 2**level_idx
        columns.append(offset + row_ids // stride * (num_cols // stride) + col_ids // stride)
        offset += num_rows // stride * (num_cols // stride)
    return (slot_ids, jnp.stack(columns, 1))


def slot_gradient(scores_raw, scales, columns, is_slot, usable):
    scores = scores_raw * scales[None, :]
    positions = jnp.arange(scales.shape[0], dtype=jnp.int32)
    matched = jnp.zeros(scores.shape, jnp.float32)
    for level_idx in range(LEVELS):
        matched = matched + (positions[None, :] == columns[:, level_idx : level_idx + 1]).astype(
            jnp.float32
        )
    matched = matched * is_slot[:, None]
    return (scales[None, :] * (jax.nn.sigmoid(scores - score_shift) - matched) * usable).astype(
        jnp.bfloat16
    )


def on_device(frame_one, frame_two, conv_weight, partners, counts, targets):
    num_rows, num_cols, in_depth = frame_one.shape
    pixels = num_rows * num_cols
    channels = conv_weight.shape[3]
    stacked = jnp.stack([frame_one, frame_two])
    with_rim = extended(stacked, (("tile", 1),), 1)
    with_rim = jnp.pad(with_rim, ((0, 0), (0, 0), (1, 1), (0, 0)))
    summed = jnp.zeros((2 * pixels, channels), jnp.float32)
    for row_tap in range(3):
        for col_tap in range(3):
            window = with_rim[
                :, row_tap : row_tap + num_rows, col_tap : col_tap + num_cols
            ].reshape(2 * pixels, in_depth)
            summed = summed + jnp.dot(
                window, conv_weight[row_tap, col_tap], preferred_element_type=jnp.float32
            )
    features = summed.astype(jnp.bfloat16).reshape(2, pixels, channels)
    feat_one = features[0]
    feat_two = features[1]
    dev_index = lax.axis_index("tile")
    offsets = dev_index - partners[0]
    candidate = []
    own_levels = pool_levels(feat_two.reshape(num_rows, num_cols, channels))
    for offset in range(-RADIUS, RADIUS + 1):
        if offset == 0:
            candidate.append(own_levels)
        else:
            candidate.append(from_behind(own_levels, "tile", offset))
    candidate = jnp.stack(candidate)
    chosen = jnp.take(candidate, offsets + RADIUS, axis=0)
    cells_all = chosen.shape[1]
    scales = column_scales(num_rows, num_cols, channels)
    slot_ids, columns = label_columns(targets.reshape(pixels), num_rows, num_cols)
    block_rows = min(512, pixels)
    level_grads = [jnp.zeros((cells_all, channels), jnp.float32) for slot_idx in range(SLOTS)]
    grad_blocks = []
    for row_start in range(0, pixels, block_rows):
        rows_feat = feat_one[row_start : row_start + block_rows]
        grad_rows = jnp.zeros((block_rows, channels), jnp.float32)
        for slot_idx in range(SLOTS):
            scores_raw = jnp.einsum(
                "pc,qc->pq", rows_feat, chosen[slot_idx], preferred_element_type=jnp.float32
            )
            usable = (slot_idx < counts[0]).astype(jnp.float32)
            is_slot = (slot_ids[row_start : row_start + block_rows] == slot_idx).astype(jnp.float32)
            dscore = slot_gradient(
                scores_raw, scales, columns[row_start : row_start + block_rows], is_slot, usable
            )
            grad_rows = grad_rows + jnp.dot(
                dscore, chosen[slot_idx], preferred_element_type=jnp.float32
            )
            level_grads[slot_idx] = level_grads[slot_idx] + jnp.einsum(
                "pq,pc->qc", dscore, rows_feat, preferred_element_type=jnp.float32
            )
        grad_blocks.append(grad_rows)
    grad_one = jnp.concatenate(grad_blocks, 0).astype(jnp.bfloat16)
    own_sum = jnp.zeros((cells_all, channels), jnp.float32)
    for slot_idx in range(SLOTS):
        own_sum = own_sum + jnp.where(offsets[slot_idx] == 0, level_grads[slot_idx], 0.0)
    for offset in range(-RADIUS, RADIUS + 1):
        if offset != 0:
            outgoing = jnp.zeros((cells_all, channels), jnp.float32)
            for slot_idx in range(SLOTS):
                outgoing = jnp.where(offsets[slot_idx] == offset, level_grads[slot_idx], outgoing)
            returned = from_behind(outgoing, "tile", -offset)
            own_sum = own_sum + returned
    grad_two = unpool_levels(own_sum, num_rows, num_cols).astype(jnp.bfloat16)
    grad_stack = jnp.stack([grad_one, grad_two]).reshape(2, num_rows, num_cols, channels)
    grad_edges = extended(grad_stack, (("tile", 1),), 1)
    grad_edges = jnp.pad(grad_edges, ((0, 0), (0, 0), (1, 1), (0, 0)))
    input_grads = jnp.zeros((2 * pixels, in_depth), jnp.float32)
    for row_tap in range(3):
        for col_tap in range(3):
            window = grad_edges[
                :, 2 - row_tap : 2 - row_tap + num_rows, 2 - col_tap : 2 - col_tap + num_cols
            ].reshape(2 * pixels, channels)
            input_grads = input_grads + jnp.einsum(
                "nc,ic->ni",
                window,
                conv_weight[row_tap, col_tap],
                preferred_element_type=jnp.float32,
            )
    input_grads = input_grads.astype(jnp.bfloat16).reshape(2, num_rows, num_cols, in_depth)
    return (input_grads[0], input_grads[1])


def solution(mesh):
    return jax.shard_map(
        on_device,
        mesh=mesh,
        in_specs=(
            P(("groups", "tile"), None, None),
            P(("groups", "tile"), None, None),
            P(),
            P(("groups", "tile"), None),
            P(("groups", "tile")),
            P(("groups", "tile"), None),
        ),
        out_specs=(P(("groups", "tile"), None, None), P(("groups", "tile"), None, None)),
        check_vma=False,
    )
```

profile of v0, /device:TPU:9, one launch (start us, length us, event | category | flops | bytes accessed | tf_op | source)
XLA Modules:
  0.0 227.6 jit_solution(2738266725022276316)
XLA Ops:
  1.5 3.7 %collective-permute-start = (bf16[2,1,128,128]{3,2,1,0:T(8,128)(2,1)S(1)}, bf16[2,1,128,128]{3,2,1,0:T(8,128)(2,1)S(1)}, u32[]{:S(2)}, u32[]{:S(2)}) collective-permute-start(bf16[2,1,128,128]{3,2,1,0:T(8,128)(2,1)S(1)} %get-tuple-element.37), channel_id=1, source_target_pairs={{0,1},{1,2},{2,3},{3,4},{4,5},{5,6},{6,7},{7,8},{8,9},{9,10},{10,1... | collective-permute-start | bytes 196616 | tf_op jit(solution)/shard_map/ppermute | solution.py:24
  22.5 3.9 %collective-permute-start.2 = (bf16[1360,256]{1,0:T(8,128)(2,1)S(1)}, bf16[1360,256]{1,0:T(8,128)(2,1)S(1)}, u32[]{:S(2)}, u32[]{:S(2)}) collective-permute-start(bf16[1360,256]{1,0:T(8,128)(2,1)S(1)} %pad_maximum_fusion.5), channel_id=1, source_target_pairs={{2,0},{3,1},{4,2},{5,3},{6,4},{7,5},{8,6},{9,7},{10,8},{11,9},{12,... | collective-permute-start | bytes 2088968 | tf_op jit(solution)/shard_map/ppermute | solution.py:36
  40.2 2.0 collective-permute-start.5
  42.2 3.7 %collective-permute-start.4 = (bf16[1360,256]{1,0:T(8,128)(2,1)S(1)}, bf16[1360,256]{1,0:T(8,128)(2,1)S(1)}, u32[]{:S(2)}, u32[]{:S(2)}) collective-permute-start(bf16[1360,256]{1,0:T(8,128)(2,1)S(1)} %pad_maximum_fusion.5), channel_id=1, source_target_pairs={{0,1},{1,2},{2,3},{3,4},{4,5},{5,6},{6,7},{7,8},{8,9},{9,10},{10,1... | collective-permute-start | bytes 2088968 | tf_op jit(solution)/shard_map/ppermute | solution.py:36
  46.0 2.1 collective-permute-start.3
  49.0 26.0 %collective-permute-done.3 = bf16[1360,256]{1,0:T(8,128)(2,1)S(1)} collective-permute-done((bf16[1360,256]{1,0:T(8,128)(2,1)S(1)}, bf16[1360,256]{1,0:T(8,128)(2,1)S(1)}, u32[]{:S(2)}, u32[]{:S(2)}) %collective-permute-start.3) | collective-permute-done | bytes 696352 | tf_op jit(solution)/shard_map/ppermute | solution.py:36
  78.6 4.3 %gather_fusion = bf16[4,1360,256]{2,1,0:T(8,128)(2,1)} fusion(bf16[5,1360,256]{2,1,0:T(8,128)(2,1)} %bitcast_dynamic-update-slice_fusion, s32[1024]{0:T(1024)S(1)} %pad_clamp_fusion), kind=kCustom, calls=%fused_computation | custom fusion | bytes 5570576 | tf_op jit(solution)/shard_map/jit(_take)/gather | solution.py:137
  82.9 2.1 broadcast_select_fusion
  85.1 2.3 %fusion.71 = bf16[512,1360]{0,1:T(8,128)(2,1)S(1)} fusion(f32[512]{0:T(512)S(1)} %get-tuple-element.47, s32[512]{0:T(512)S(1)} %bitcast.263, s32[512]{0:T(512)S(1)} %bitcast.279, s32[512]{0:T(512)S(1)} %bitcast.275, s32[512]{0:T(512)S(1)} %bitcast.255, f32[]{:T(128)} %bitcast.49, f32[1360]{0:T(1024)S(1)} %copy-done.6, ...), kind=kOutput, calls=%fused_computation.82 | convolution fusion | flops 371138560 | bytes 2369540 | tf_op jit(solution)/shard_map/pc,qc->pq/dot_general | solution.py:148
  87.4 2.3 %fusion.70 = bf16[512,1360]{0,1:T(8,128)(2,1)S(1)} fusion(f32[512]{0:T(512)S(1)} %get-tuple-element.46, s32[512]{0:T(512)S(1)} %bitcast.264, s32[512]{0:T(512)S(1)} %bitcast.280, s32[512]{0:T(512)S(1)} %bitcast.276, s32[512]{0:T(512)S(1)} %bitcast.256, f32[]{:T(128)} %bitcast.47, f32[1360]{0:T(1024)S(1)} %copy-done.6, ...), kind=kOutput, calls=%fused_computation.81 | convolution fusion | flops 371138560 | bytes 2369540 | tf_op jit(solution)/shard_map/pc,qc->pq/dot_general | solution.py:148
  89.7 2.3 %fusion.67 = bf16[512,1360]{0,1:T(8,128)(2,1)S(1)} fusion(f32[]{:T(128)} %bitcast.49, f32[512]{0:T(512)S(1)} %get-tuple-element.42, s32[512]{0:T(512)S(1)} %bitcast.259, s32[512]{0:T(512)S(1)} %bitcast.271, s32[512]{0:T(512)S(1)} %bitcast.267, s32[512]{0:T(512)S(1)} %bitcast.251, f32[1360]{0:T(1024)S(1)} %copy-done.6, ...), kind=kOutput, calls=%fused_computation.78 | convolution fusion | flops 371138560 | bytes 2369540 | tf_op jit(solution)/shard_map/pc,qc->pq/dot_general | solution.py:148
  92.1 2.3 %fusion.66 = bf16[512,1360]{0,1:T(8,128)(2,1)S(1)} fusion(f32[]{:T(128)} %bitcast.47, f32[512]{0:T(512)S(1)} %get-tuple-element.44, s32[512]{0:T(512)S(1)} %bitcast.260, s32[512]{0:T(512)S(1)} %bitcast.272, s32[512]{0:T(512)S(1)} %bitcast.268, s32[512]{0:T(512)S(1)} %bitcast.252, f32[1360]{0:T(1024)S(1)} %copy-done.6, ...), kind=kOutput, calls=%fused_computation.77 | convolution fusion | flops 371138560 | bytes 2369540 | tf_op jit(solution)/shard_map/pc,qc->pq/dot_general | solution.py:148
  94.4 2.3 %fusion.68 = bf16[512,1360]{0,1:T(8,128)(2,1)S(1)} fusion(f32[512]{0:T(512)S(1)} %get-tuple-element.48, s32[512]{0:T(512)S(1)} %bitcast.265, s32[512]{0:T(512)S(1)} %bitcast.281, s32[512]{0:T(512)S(1)} %bitcast.277, s32[512]{0:T(512)S(1)} %bitcast.257, f32[]{:T(128)} %bitcast.43, f32[1360]{0:T(1024)S(1)} %copy-done.6, ...), kind=kOutput, calls=%fused_computation.79 | convolution fusion | flops 371138560 | bytes 2369540 | tf_op jit(solution)/shard_map/pc,qc->pq/dot_general | solution.py:148
  97.3 2.3 %fusion.64 = bf16[512,1360]{0,1:T(8,128)(2,1)S(1)} fusion(f32[]{:T(128)} %bitcast.43, f32[512]{0:T(512)S(1)} %get-tuple-element.49, s32[512]{0:T(512)S(1)} %bitcast.261, s32[512]{0:T(512)S(1)} %bitcast.273, s32[512]{0:T(512)S(1)} %bitcast.269, s32[512]{0:T(512)S(1)} %bitcast.253, f32[1360]{0:T(1024)S(1)} %copy-done.6, ...), kind=kOutput, calls=%fused_computation.75 | convolution fusion | flops 371138560 | bytes 2369540 | tf_op jit(solution)/shard_map/pc,qc->pq/dot_general | solution.py:148
  100.7 2.3 %fusion.69 = bf16[512,1360]{0,1:T(8,128)(2,1)S(1)} fusion(f32[512]{0:T(512)S(1)} %get-tuple-element.45, s32[512]{0:T(512)S(1)} %bitcast.266, s32[512]{0:T(512)S(1)} %bitcast.282, s32[512]{0:T(512)S(1)} %bitcast.278, s32[512]{0:T(512)S(1)} %bitcast.258, f32[]{:T(128)} %bitcast.45, f32[1360]{0:T(1024)S(1)} %copy-done.6, ...), kind=kOutput, calls=%fused_computation.80 | convolution fusion | flops 371138560 | bytes 2369540 | tf_op jit(solution)/shard_map/pc,qc->pq/dot_general | solution.py:148
  103.0 2.5 %fusion.65 = bf16[512,1360]{0,1:T(8,128)(2,1)S(1)} fusion(f32[]{:T(128)} %bitcast.45, f32[512]{0:T(512)S(1)} %get-tuple-element.43, s32[512]{0:T(512)S(1)} %bitcast.262, s32[512]{0:T(512)S(1)} %bitcast.274, s32[512]{0:T(512)S(1)} %bitcast.270, s32[512]{0:T(512)S(1)} %bitcast.254, f32[1360]{0:T(1024)S(1)} %copy-done.6, ...), kind=kOutput, calls=%fused_computation.76 | convolution fusion | flops 371138560 | bytes 2369540 | tf_op jit(solution)/shard_map/pc,qc->pq/dot_general | solution.py:148
  114.6 4.3 %collective-permute-start.9 = (f32[1360,256]{1,0:T(8,128)S(1)}, f32[1360,256]{1,0:T(8,128)S(1)}, u32[]{:S(2)}, u32[]{:S(2)}) collective-permute-start(f32[1360,256]{1,0:T(8,128)S(1)} %get-tuple-element.10), channel_id=1, source_target_pairs={{2,0},{3,1},{4,2},{5,3},{6,4},{7,5},{8,6},{9,7},{10,8},{11,9},{12,... | collective-permute-start | bytes 4177928 | tf_op jit(solution)/shard_map/ppermute | solution.py:36
  118.9 3.0 %collective-permute-start.8 = (f32[1360,256]{1,0:T(8,128)S(1)}, f32[1360,256]{1,0:T(8,128)S(1)}, u32[]{:S(2)}, u32[]{:S(2)}) collective-permute-start(f32[1360,256]{1,0:T(8,128)S(1)} %get-tuple-element.11), channel_id=1, source_target_pairs={{1,0},{2,1},{3,2},{4,3},{5,4},{6,5},{7,6},{8,7},{9,8},{10,9},{11,1... | collective-permute-start | bytes 4177928 | tf_op jit(solution)/shard_map/ppermute | solution.py:36
  125.1 60.1 %collective-permute-done.7 = f32[1360,256]{1,0:T(8,128)S(1)} collective-permute-done((f32[1360,256]{1,0:T(8,128)S(1)}, f32[1360,256]{1,0:T(8,128)S(1)}, u32[]{:S(2)}, u32[]{:S(2)}) %collective-permute-start.7) | collective-permute-done | bytes 1392672 | tf_op jit(solution)/shard_map/ppermute | solution.py:36
  185.1 17.6 %collective-permute-done.6 = f32[1360,256]{1,0:T(8,128)S(1)} collective-permute-done((f32[1360,256]{1,0:T(8,128)S(1)}, f32[1360,256]{1,0:T(8,128)S(1)}, u32[]{:S(2)}, u32[]{:S(2)}) %collective-permute-start.6) | collective-permute-done | bytes 1392672 | tf_op jit(solution)/shard_map/ppermute | solution.py:36
  204.8 1.9 div.196
  207.9 2.5 %div.200 = f32[1024,256]{1,0:T(8,128)} reshape(f32[2,4,32,4,256]{4,3,2,1,0:T(4,128)} %broadcast_in_dim.26) | data formatting | bytes 2097152 | tf_op jit(solution)/shard_map/div | solution.py:65
  213.8 2.7 %collective-permute-start.11 = (bf16[2,1,128,256]{3,2,1,0:T(8,128)(2,1)S(1)}, bf16[2,1,128,256]{3,2,1,0:T(8,128)(2,1)S(1)}, u32[]{:S(2)}, u32[]{:S(2)}) collective-permute-start(bf16[2,1,128,256]{3,2,1,0:T(8,128)(2,1)S(1)} %get-tuple-element.22), channel_id=1, source_target_pairs={{1,0},{2,1},{3,2},{4,3},{5,4},{6,5},{7,6},{8,7},{9,8},{10,9},{11,1... | collective-permute-start | bytes 393224 | tf_op jit(solution)/shard_map/ppermute | solution.py:26
  216.5 4.2 %collective-permute-done.11 = bf16[2,1,128,256]{3,2,1,0:T(8,128)(2,1)S(1)} collective-permute-done((bf16[2,1,128,256]{3,2,1,0:T(8,128)(2,1)S(1)}, bf16[2,1,128,256]{3,2,1,0:T(8,128)(2,1)S(1)}, u32[]{:S(2)}, u32[]{:S(2)}) %collective-permute-start.11) | collective-permute-done | bytes 131104 | tf_op jit(solution)/shard_map/ppermute | solution.py:26
  (106 shorter events, 49.7 us)
Async XLA Ops:
  1.5 8.6 %collective-permute-start = (bf16[2,1,128,128]{3,2,1,0:T(8,128)(2,1)S(1)}, bf16[2,1,128,128]{3,2,1,0:T(8,128)(2,1)S(1)}, u32[]{:S(2)}, u32[]{:S(2)}) collective-permute-start(bf16[2,1,128,128]{3,2,1,0:T(8,128)(2,1)S(1)} %get-tuple-element.37), channel_id=1, source_target_pairs={{0,1},{1,2},{2,3},{3,4},{4,5},{5,6},{6,7},{7,8},{8,9},{9,10},{10,1... | collective-permute-start | bytes 196616 | tf_op jit(solution)/shard_map/ppermute | solution.py:24
  5.2 5.6 %collective-permute-start.1 = (bf16[2,1,128,128]{3,2,1,0:T(8,128)(2,1)S(1)}, bf16[2,1,128,128]{3,2,1,0:T(8,128)(2,1)S(1)}, u32[]{:S(2)}, u32[]{:S(2)}) collective-permute-start(bf16[2,1,128,128]{3,2,1,0:T(8,128)(2,1)S(1)} %get-tuple-element.38), channel_id=1, source_target_pairs={{1,0},{2,1},{3,2},{4,3},{5,4},{6,5},{7,6},{8,7},{9,8},{10,9},{11,1... | collective-permute-start | bytes 196616 | tf_op jit(solution)/shard_map/ppermute | solution.py:26
  12.0 1.1 copy-start
  12.7 1.2 copy-start.2
  12.7 1.2 copy-start.3
  20.1 2.3 %copy-start.5 = (bf16[1024,256]{1,0:T(8,128)(2,1)S(1)}, bf16[1024,256]{1,0:T(8,128)(2,1)}, u32[]{:S(2)}) copy-start(bf16[1024,256]{1,0:T(8,128)(2,1)} %get-tuple-element.25) | copy-start | bytes 1572868
  21.7 54.3 %copy-start.4 = (bf16[1,1024,256]{2,1,0:T(8,128)(2,1)S(1)}, bf16[1,1024,256]{2,1,0:T(8,128)(2,1)}, u32[]{:S(2)}) copy-start(bf16[1,1024,256]{2,1,0:T(8,128)(2,1)} %get-tuple-element.23) | copy-start | bytes 1572868
  22.5 25.6 %collective-permute-start.2 = (bf16[1360,256]{1,0:T(8,128)(2,1)S(1)}, bf16[1360,256]{1,0:T(8,128)(2,1)S(1)}, u32[]{:S(2)}, u32[]{:S(2)}) collective-permute-start(bf16[1360,256]{1,0:T(8,128)(2,1)S(1)} %pad_maximum_fusion.5), channel_id=1, source_target_pairs={{2,0},{3,1},{4,2},{5,3},{6,4},{7,5},{8,6},{9,7},{10,8},{11,9},{12,... | collective-permute-start | bytes 2088968 | tf_op jit(solution)/shard_map/ppermute | solution.py:36
  40.2 37.6 %collective-permute-start.5 = (bf16[1360,256]{1,0:T(8,128)(2,1)S(1)}, bf16[1360,256]{1,0:T(8,128)(2,1)S(1)}, u32[]{:S(2)}, u32[]{:S(2)}) collective-permute-start(bf16[1360,256]{1,0:T(8,128)(2,1)S(1)} %pad_maximum_fusion.5), channel_id=1, source_target_pairs={{0,2},{1,3},{2,4},{3,5},{4,6},{5,7},{6,8},{7,9},{8,10},{9,11},{10,... | collective-permute-start | bytes 2088968 | tf_op jit(solution)/shard_map/ppermute | solution.py:36
  42.2 34.6 %collective-permute-start.4 = (bf16[1360,256]{1,0:T(8,128)(2,1)S(1)}, bf16[1360,256]{1,0:T(8,128)(2,1)S(1)}, u32[]{:S(2)}, u32[]{:S(2)}) collective-permute-start(bf16[1360,256]{1,0:T(8,128)(2,1)S(1)} %pad_maximum_fusion.5), channel_id=1, source_target_pairs={{0,1},{1,2},{2,3},{3,4},{4,5},{5,6},{6,7},{7,8},{8,9},{9,10},{10,1... | collective-permute-start | bytes 2088968 | tf_op jit(solution)/shard_map/ppermute | solution.py:36
  46.0 29.0 %collective-permute-start.3 = (bf16[1360,256]{1,0:T(8,128)(2,1)S(1)}, bf16[1360,256]{1,0:T(8,128)(2,1)S(1)}, u32[]{:S(2)}, u32[]{:S(2)}) collective-permute-start(bf16[1360,256]{1,0:T(8,128)(2,1)S(1)} %pad_maximum_fusion.5), channel_id=1, source_target_pairs={{1,0},{2,1},{3,2},{4,3},{5,4},{6,5},{7,6},{8,7},{9,8},{10,9},{11,1... | collective-permute-start | bytes 2088968 | tf_op jit(solution)/shard_map/ppermute | solution.py:36
  82.9 2.1 copy-start.6
  110.8 74.3 %collective-permute-start.7 = (f32[1360,256]{1,0:T(8,128)S(1)}, f32[1360,256]{1,0:T(8,128)S(1)}, u32[]{:S(2)}, u32[]{:S(2)}) collective-permute-start(f32[1360,256]{1,0:T(8,128)S(1)} %select_select_fusion.2), channel_id=1, source_target_pairs={{0,1},{1,2},{2,3},{3,4},{4,5},{5,6},{6,7},{7,8},{8,9},{9,10},{10,1... | collective-permute-start | bytes 4177928 | tf_op jit(solution)/shard_map/ppermute | solution.py:36
  112.7 90.0 %collective-permute-start.6 = (f32[1360,256]{1,0:T(8,128)S(1)}, f32[1360,256]{1,0:T(8,128)S(1)}, u32[]{:S(2)}, u32[]{:S(2)}) collective-permute-start(f32[1360,256]{1,0:T(8,128)S(1)} %get-tuple-element.9), channel_id=1, source_target_pairs={{0,2},{1,3},{2,4},{3,5},{4,6},{5,7},{6,8},{7,9},{8,10},{9,11},{10,... | collective-permute-start | bytes 4177928 | tf_op jit(solution)/shard_map/ppermute | solution.py:36
  114.6 88.1 %collective-permute-start.9 = (f32[1360,256]{1,0:T(8,128)S(1)}, f32[1360,256]{1,0:T(8,128)S(1)}, u32[]{:S(2)}, u32[]{:S(2)}) collective-permute-start(f32[1360,256]{1,0:T(8,128)S(1)} %get-tuple-element.10), channel_id=1, source_target_pairs={{2,0},{3,1},{4,2},{5,3},{6,4},{7,5},{8,6},{9,7},{10,8},{11,9},{12,... | collective-permute-start | bytes 4177928 | tf_op jit(solution)/shard_map/ppermute | solution.py:36
  118.9 83.8 %collective-permute-start.8 = (f32[1360,256]{1,0:T(8,128)S(1)}, f32[1360,256]{1,0:T(8,128)S(1)}, u32[]{:S(2)}, u32[]{:S(2)}) collective-permute-start(f32[1360,256]{1,0:T(8,128)S(1)} %get-tuple-element.11), channel_id=1, source_target_pairs={{1,0},{2,1},{3,2},{4,3},{5,4},{6,5},{7,6},{8,7},{9,8},{10,9},{11,1... | collective-permute-start | bytes 4177928 | tf_op jit(solution)/shard_map/ppermute | solution.py:36
  211.9 4.6 %collective-permute-start.10 = (bf16[2,1,128,256]{3,2,1,0:T(8,128)(2,1)S(1)}, bf16[2,1,128,256]{3,2,1,0:T(8,128)(2,1)S(1)}, u32[]{:S(2)}, u32[]{:S(2)}) collective-permute-start(bf16[2,1,128,256]{3,2,1,0:T(8,128)(2,1)S(1)} %get-tuple-element.21), channel_id=1, source_target_pairs={{0,1},{1,2},{2,3},{3,4},{4,5},{5,6},{6,7},{7,8},{8,9},{9,10},{10,1... | collective-permute-start | bytes 393224 | tf_op jit(solution)/shard_map/ppermute | solution.py:24
  213.8 6.8 %collective-permute-start.11 = (bf16[2,1,128,256]{3,2,1,0:T(8,128)(2,1)S(1)}, bf16[2,1,128,256]{3,2,1,0:T(8,128)(2,1)S(1)}, u32[]{:S(2)}, u32[]{:S(2)}) collective-permute-start(bf16[2,1,128,256]{3,2,1,0:T(8,128)(2,1)S(1)} %get-tuple-element.22), channel_id=1, source_target_pairs={{1,0},{2,1},{3,2},{4,3},{5,4},{6,5},{7,6},{8,7},{9,8},{10,9},{11,1... | collective-permute-start | bytes 393224 | tf_op jit(solution)/shard_map/ppermute | solution.py:26
  221.4 1.2 copy-start.1
where the time goes:
time: 230 us; the launch traced here: 228 us
  waiting for transfers between devices  109 us (47%)
  matrix products  36 us (16%)
  starting transfers between devices  33.1 us (14%)
  local copies, waits for them, and re-layouts  20.5 us (9%)
  between operations  15 us (7%)
  other arithmetic  14.6 us (6%)
    ppermute x8, waiting for transfers between devices, from_behind(): return lax.ppermute(block, axis, route)  104 us
    ppermute x8, starting transfers between devices, from_behind(): return lax.ppermute(block, axis, route)  22.9 us
    dot_general x8, matrix products, on_device(): jnp.einsum('pc,qc->pq', rows_feat, chosen[slot_idx], preferred_element_ty...  18.8 us
    ppermute x2, starting transfers between devices, extended(): lax.ppermute(tail, axis, [(i, (i + 1) % count) for i in range(ends)])  5.63 us
    dot_general x8, matrix products, on_device(): jnp.dot(dscore, chosen[slot_idx], preferred_element_type=jnp.float32)  4.94 us
    ppermute x2, waiting for transfers between devices, extended(): lax.ppermute(head, axis, [((i + 1) % count, i) for i in range(ends)])  4.87 us
  transfers between devices with their start and end apart: 12, of which 5 were waited for; matrix products, arithmetic and copies ran while one was open for 4% of the time, Pallas kernels for 0%

commit v1 on v0

v1 whole, which is shorter than its diff:
```python
import functools

import jax
import jax.numpy as jnp
import numpy as np
from jax import lax
from jax.experimental import pallas as pl
from jax.experimental.pallas import tpu as pltpu
from jax.sharding import PartitionSpec as P

LEVELS = 4
RADIUS = 2
SLOTS = 4
TR = 8
TC = 128
PIX = TR * TC
CIN = 128
CH = 256
POOLED = PIX // 4 + PIX // 16 + PIX // 64
PAD = 384
CELLS = PIX + PAD
WIN = 2 * RADIUS * TR + TR + 2

NN = (((1,), (0,)), ((), ()))
NT = (((1,), (1,)), ((), ()))
TN = (((0,), (0,)), ((), ()))


def matmul(a, b, dims):
    return lax.dot_general(a, b, dims, preferred_element_type=jnp.float32)


def routes(count):
    side = [1 - 2 * (i % 2) for i in range(count)]

    def keep(pairs):
        return [(a, b) for a, b in pairs if 0 <= b < count]

    return dict(
        swap=[(i, i + side[i]) for i in range(count)],
        ahead=keep((i, i + 2 * side[i]) for i in range(count)),
        behind=keep((i, i - 2 * side[i]) for i in range(count)),
        far=keep((i, i - 3 * side[i]) for i in range(count)),
    )


def shifted(block):
    n = block.shape[0]
    column = lax.broadcasted_iota(jnp.int32, block.shape, 0)
    down = jnp.where(column == 0, 0.0, pltpu.roll(block, 1, 0))
    up = jnp.where(column == n - 1, 0.0, pltpu.roll(block, n - 1, 0))
    return down, up


def spread_columns(source, row, target, at):
    middle = source[row]
    down, up = shifted(middle.astype(jnp.float32))
    where = pl.ds(pl.multiple_of(at * TC, TC), TC)
    target[where, 0:CIN] = down.astype(jnp.bfloat16)
    target[where, CIN : 2 * CIN] = middle
    target[where, 2 * CIN : 3 * CIN] = up.astype(jnp.bfloat16)


def convolve(spread, at, weight):
    parts = [
        spread[pl.ds(pl.multiple_of((at + a) * TC, TC), PIX), :] for a in range(3)
    ]
    total = matmul(jnp.concatenate(parts, 1), weight[...], NN)
    return total.astype(jnp.bfloat16)


def convolve_back(gradient, weight_back, moved, total, at):
    for r in range(TR):
        block = gradient[r * TC : (r + 1) * TC, :]
        down, up = shifted(block)
        rows = slice(r * TC, (r + 1) * TC)
        moved[rows, 0:CH] = up.astype(jnp.bfloat16)
        moved[rows, CH : 2 * CH] = block.astype(jnp.bfloat16)
        moved[rows, 2 * CH : 3 * CH] = down.astype(jnp.bfloat16)
    for a in range(3):
        part = matmul(moved[...], weight_back[a * CIN : (a + 1) * CIN, :], NT)
        where = pl.ds(pl.multiple_of((at + a) * TC, TC), PIX)
        total[where, :] += part


def pool_matrix():
    cell = lax.broadcasted_iota(jnp.int32, (PAD, PIX), 0)
    pixel = lax.broadcasted_iota(jnp.int32, (PAD, PIX), 1)
    row, column = pixel // TC, pixel % TC
    offset = 0
    inside = jnp.zeros((PAD, PIX), jnp.bool_)
    for level in range(1, LEVELS):
        cells = PIX >> (2 * level)
        own = offset + (row >> level) * (TC >> level) + (column >> level)
        inside = inside | ((cell >= offset) & (cell < offset + cells) & (cell == own))
        offset += cells
    return jnp.where(inside, 1.0, 0.0).astype(jnp.bfloat16)


def per_level(values, fill):
    cell = lax.broadcasted_iota(jnp.int32, (PAD, 1), 0)
    result = jnp.full((PAD, 1), fill, jnp.float32)
    offset = 0
    for level in range(1, LEVELS):
        result = jnp.where(cell >= offset, values[level], result)
        offset += PIX >> (2 * level)
    return jnp.where(cell >= offset, fill, result)


def work_kernel(
    plan,
    own_one,
    own_two,
    near,
    direct,
    far,
    from_sibling,
    weight,
    labels,
    to_sibling,
    ahead,
    behind,
    far_out,
    sum_one,
    sum_two,
    window,
    spread_two,
    window_one,
    spread_one,
    weight_back,
    pool,
    feat_one,
    pyramid,
    dscore,
    level_grad,
    grad_rows,
    moved,
    total_two,
    total_one,
):
    side = plan[5]
    count = plan[4]

    def at(offset):
        return 1 + TR * (offset + RADIUS)

    def edge(sign):
        return jnp.where(sign > 0, WIN - 1, 0)

    for r in range(TR):
        window[at(0) + r] = own_two[r]
        window[at(2 * side) + r] = near[r]
        window[at(-2 * side) + r] = direct[r]
        window[at(side) + r] = from_sibling[r]
        window[at(-side) + r] = from_sibling[TR + r]
        window_one[1 + r] = own_one[r]
    window[edge(side)] = from_sibling[2 * TR + 2]
    window[edge(-side)] = far[0]
    window_one[jnp.where(side > 0, TR + 1, 0)] = from_sibling[2 * TR + 1]
    window_one[jnp.where(side > 0, 0, TR + 1)] = from_sibling[2 * TR]

    def spread(r, carry):
        spread_columns(window, r, spread_two, r)
        return carry

    lax.fori_loop(0, WIN, spread, 0)
    for r in range(TR + 2):
        spread_columns(window_one, r, spread_one, r)
    for a in range(3):
        for b in range(3):
            weight_back[a * CIN : (a + 1) * CIN, b * CH : (b + 1) * CH] = weight[
                (3 * a + b) * CIN : (3 * a + b + 1) * CIN, :
            ]
    pool[...] = pool_matrix()
    feat_one[...] = convolve(spread_one, 0, weight)
    grad_rows[...] = jnp.zeros_like(grad_rows)
    total_two[...] = jnp.zeros_like(total_two)
    total_one[...] = jnp.zeros_like(total_one)

    def slot(k, carry):
        @pl.when(k < count)
        def _():
            first = TR * (plan[k] + RADIUS)
            feat_two = convolve(spread_two, first, weight)
            pyramid[0:PIX, :] = feat_two * jnp.bfloat16(2.0**-5)
            means = matmul(pool[...], feat_two, NN) * per_level(
                [4.0**-level for level in range(LEVELS)], 0.0
            )
            scale = per_level([2.0 ** (level - 5) for level in range(LEVELS)], 0.0)
            pyramid[PIX:CELLS, :] = (
                means.astype(jnp.bfloat16).astype(jnp.float32) * scale
            ).astype(jnp.bfloat16)
            features = feat_one[...]
            here = labels[4:5, :] == k
            columns = [jnp.where(here, labels[n : n + 1, :], -1) for n in range(LEVELS)]
            for start in range(0, CELLS, 256):
                size = min(256, CELLS - start)
                half_score = matmul(pyramid[start : start + size, :], features, NT)
                position = lax.broadcasted_iota(jnp.int32, half_score.shape, 0) + start
                if start < PIX:
                    hit = position == columns[0]
                elif start < PIX + PIX // 4:
                    hit = position == columns[1]
                else:
                    hit = (position == columns[2]) | (position == columns[3])
                value = jnp.tanh(half_score - 1.0) + jnp.where(hit, -1.0, 1.0)
                dscore[start : start + size, :] = value.astype(jnp.bfloat16)
            level_grad[...] = matmul(dscore[...], features, NN)
            grad_rows[...] += matmul(dscore[...], pyramid[...], TN)
            coarse = level_grad[PIX:CELLS, :] * per_level(
                [2.0 ** (-level - 5) for level in range(LEVELS)], 0.0
            )
            high = coarse.astype(jnp.bfloat16)
            low = (coarse - high.astype(jnp.float32)).astype(jnp.bfloat16)
            gradient = level_grad[0:PIX, :] * 2.0**-5
            gradient = gradient + matmul(pool[...], high, TN)
            gradient = gradient + matmul(pool[...], low, TN)
            convolve_back(gradient, weight_back, moved, total_two, first)

        return carry

    lax.fori_loop(0, SLOTS, slot, 0)
    convolve_back(grad_rows[...], weight_back, moved, total_one, 0)

    def rows(total, row, size=1):
        return total[pl.ds(pl.multiple_of(row * TC, TC), size * TC), :].reshape(size, TC, CIN)

    to_sibling[0:TR] = rows(total_two, at(side), TR).astype(jnp.bfloat16)
    to_sibling[TR : 2 * TR] = rows(total_two, at(-side), TR).astype(jnp.bfloat16)
    to_sibling[2 * TR : 2 * TR + 1] = rows(total_two, edge(side)).astype(jnp.bfloat16)
    to_sibling[2 * TR + 1 : 2 * TR + 2] = rows(
        total_one, jnp.where(side > 0, TR + 1, 0)
    ).astype(jnp.bfloat16)
    to_sibling[2 * TR + 2 : 2 * TR + 3] = rows(
        total_one, jnp.where(side > 0, 0, TR + 1)
    ).astype(jnp.bfloat16)
    ahead[...] = rows(total_two, at(2 * side), TR)
    behind[...] = rows(total_two, at(-2 * side), TR)
    far_out[...] = rows(total_two, edge(-side)).astype(jnp.bfloat16)
    sum_two[...] = rows(total_two, at(0), TR)
    sum_one[...] = rows(total_one, 1, TR)


def join_kernel(plan, ahead, behind, from_sibling, ahead_out, behind_out, held):
    side = plan[5]
    for r in range(TR):
        ahead_out[r] = (ahead[r] + from_sibling[TR + r].astype(jnp.float32)).astype(jnp.bfloat16)
    ahead_out[TR] = from_sibling[2 * TR + 2]
    held[...] = behind[...]
    row = jnp.where(side > 0, TR - 1, 0)
    held[row] = held[row] + from_sibling[2 * TR].astype(jnp.float32)
    behind_out[...] = held[...].astype(jnp.bfloat16)


def final_kernel(plan, sum_one, sum_two, from_sibling, ahead, behind, far, one, two, held_one, held_two):
    side = plan[5]
    facing = jnp.where(side > 0, TR - 1, 0)
    outer = jnp.where(side > 0, 0, TR - 1)
    held_one[...] = sum_one[...]
    held_one[facing] = held_one[facing] + from_sibling[2 * TR + 1].astype(jnp.float32)
    held_one[outer] = held_one[outer] + ahead[TR].astype(jnp.float32)
    one[...] = held_one[...].astype(jnp.bfloat16)
    for r in range(TR):
        held_two[r] = (
            sum_two[r]
            + from_sibling[r].astype(jnp.float32)
            + ahead[r].astype(jnp.float32)
            + behind[r].astype(jnp.float32)
        )
    held_two[outer] = held_two[outer] + far[0].astype(jnp.float32)
    two[...] = held_two[...].astype(jnp.bfloat16)


def call(kernel, outs, scratch, args, name):
    smem = pl.BlockSpec(memory_space=pltpu.SMEM)
    vmem = pl.BlockSpec(memory_space=pltpu.VMEM)
    return pl.pallas_call(
        kernel,
        in_specs=[smem] + [vmem] * (len(args) - 1),
        out_specs=[vmem] * len(outs),
        out_shape=[jax.ShapeDtypeStruct(*out) for out in outs],
        scratch_shapes=[pltpu.VMEM(*item) for item in scratch],
        compiler_params=pltpu.CompilerParams(vmem_limit_bytes=56 << 20),
        name=name,
    )(*args)


def label_rows(targets):
    value = targets.reshape(PIX)
    inside = value % PIX
    row, column = inside // TC, inside % TC
    rows = []
    offset = 0
    for level in range(LEVELS):
        rows.append(offset + (row >> level) * (TC >> level) + (column >> level))
        offset += PIX >> (2 * level)
    rows.append(value // PIX)
    rows += [rows[-1]] * 3
    return jnp.stack(rows).astype(jnp.int32)


def on_device(frame_one, frame_two, conv_weight, partners, counts, targets):
    route = routes(lax.axis_size("tile"))
    index = lax.axis_index("tile")
    side = 1 - 2 * (index % 2)
    f32, bf16 = jnp.float32, jnp.bfloat16

    def send(block, name):
        return lax.ppermute(block, "tile", route[name])

    def row_of(frame, first):
        return lax.dynamic_slice_in_dim(frame, jnp.where(first, 0, TR - 1), 1, 0)

    plan = jnp.concatenate(
        [partners[0] - index, counts, side[None], jnp.zeros((2,), jnp.int32)]
    ).astype(jnp.int32)
    labels = label_rows(targets)
    weight = conv_weight.reshape(9 * CIN, CH)
    outward = row_of(frame_one, side > 0)
    near = send(jnp.concatenate([frame_two, outward]), "behind")
    direct = send(frame_two, "ahead")
    far = send(row_of(frame_two, side > 0), "far")
    inward = row_of(frame_one, side < 0)
    payload = jnp.concatenate([frame_two, near, inward, row_of(direct, side < 0)])
    from_sibling = send(payload, "swap")

    tile = (TR, TC, CIN)
    pack = (2 * TR + 3, TC, CIN)
    to_sibling, ahead, behind, far_out, sum_one, sum_two = call(
        work_kernel,
        [(pack, bf16), (tile, f32), (tile, f32), ((1, TC, CIN), bf16), (tile, f32), (tile, f32)],
        [
            ((WIN, TC, CIN), bf16),
            ((WIN * TC, 3 * CIN), bf16),
            ((TR + 2, TC, CIN), bf16),
            (((TR + 2) * TC, 3 * CIN), bf16),
            ((3 * CIN, 3 * CH), bf16),
            ((PAD, PIX), bf16),
            ((PIX, CH), bf16),
            ((CELLS, CH), bf16),
            ((CELLS, PIX), bf16),
            ((CELLS, CH), f32),
            ((PIX, CH), f32),
            ((PIX, 3 * CH), bf16),
            ((WIN * TC, CIN), f32),
            (((TR + 2) * TC, CIN), f32),
        ],
        [plan, frame_one, frame_two, near, direct, far, from_sibling, weight, labels],
        "work",
    )
    back_sibling = send(to_sibling, "swap")
    ahead_out, behind_out = call(
        join_kernel,
        [((TR + 1, TC, CIN), bf16), (tile, bf16)],
        [(tile, f32)],
        [plan, ahead, behind, back_sibling],
        "join",
    )
    back_ahead = send(ahead_out, "ahead")
    back_behind = send(behind_out, "behind")
    back_far = send(far_out, "far")
    return call(
        final_kernel,
        [(tile, bf16), (tile, bf16)],
        [(tile, f32), (tile, f32)],
        [plan, sum_one, sum_two, back_sibling, back_ahead, back_behind, back_far],
        "final",
    )


def solution(mesh):
    return jax.shard_map(
        on_device,
        mesh=mesh,
        in_specs=(
            P(("groups", "tile"), None, None),
            P(("groups", "tile"), None, None),
            P(),
            P(("groups", "tile"), None),
            P(("groups", "tile")),
            P(("groups", "tile"), None),
        ),
        out_specs=(P(("groups", "tile"), None, None), P(("groups", "tile"), None, None)),
        check_vma=False,
    )
```

time: 230 us -> 91.7 us (0.40)
  waiting for transfers between devices: 109 us -> 15.5 us
  Pallas kernels: 0 us -> 45 us
  matrix products: 36 us -> 0 us
  local copies, waits for them, and re-layouts: 20.5 us -> 5.38 us
  between operations: 15 us -> 1.47 us
  other arithmetic: 14.6 us -> 1.88 us
  starting transfers between devices: 33.1 us -> 20.9 us
    ppermute x12 -> x8, waiting for transfers between devices: 109 us -> 15.5 us  [send(): return lax.ppermute(block, 'tile', route[name])]
    pallas_call x0 -> x3, Pallas kernels: none -> 45 us  [call(): pl.pallas_call(kernel, in_specs=[smem] + [vmem] * (len(args) - 1), out_sp...]
    dot_general x42 -> x0, matrix products: 36 us -> none  [the longest x8 18.8 us: on_device(): jnp.einsum('pc,qc->pq', rows_feat, chosen[slot_idx], preferred_element_ty...]
    ppermute x12 -> x8, starting transfers between devices: 33.1 us -> 20.9 us  [send(): return lax.ppermute(block, 'tile', route[name])]
    div x2 -> x0, local copies, waits for them, and re-layouts: 4.49 us -> none  [unpool_levels(): piece.reshape(num_rows, num_cols, channels) / float(stride * stride)]
    gather x1 -> x0, local copies, waits for them, and re-layouts: 4.27 us -> none  [on_device(): chosen = jnp.take(candidate, offsets + RADIUS, axis=0)]
    slice x7 -> x0, local copies, waits for them, and re-layouts: 3.35 us -> none  [the longest x1 1.13 us: on_device(): grad_edges[:, 2 - row_tap:2 - row_tap + num_rows, 2 - col_tap:2 - col_tap...]
    select_n x4 -> x1, other arithmetic: 3.19 us -> 0.02 us  [label_rows(): rows.append(value // PIX)]
  transfers between devices with their start and end apart: 12 -> 8, of which waited for: 5 -> 4; matrix products, arithmetic and copies ran while one was open for 4% -> 5% of each run, Pallas kernels for 0% -> 0%
where the time goes in v1:
time: 91.7 us; the launch traced here: 90.1 us
  Pallas kernels  45 us (49%)
  starting transfers between devices  20.9 us (23%)
  waiting for transfers between devices  15.5 us (17%)
  local copies, waits for them, and re-layouts  5.38 us (6%)
  other arithmetic  1.88 us (2%)
  between operations  1.47 us (2%)
    pallas_call x3, Pallas kernels, call(): pl.pallas_call(kernel, in_specs=[smem] + [vmem] * (len(args) - 1), out_sp...  45 us
    ppermute x8, starting transfers between devices, send(): return lax.ppermute(block, 'tile', route[name])  20.9 us
    ppermute x8, waiting for transfers between devices, send(): return lax.ppermute(block, 'tile', route[name])  15.5 us
    unnamed x24, local copies, waits for them, and re-layouts  3.14 us
  transfers between devices with their start and end apart: 8, of which 4 were waited for; matrix products, arithmetic and copies ran while one was open for 5% of the time, Pallas kernels for 0%

profile of v1, /device:TPU:9, one launch (start us, length us, event | category | flops | bytes accessed | tf_op | source)
XLA Modules:
  0.0 90.1 jit_solution(4394797555566368549)
XLA Ops:
  0.6 3.0 %collective-permute-start.1 = (bf16[8,128,128]{2,1,0:T(8,128)(2,1)}, bf16[8,128,128]{2,1,0:T(8,128)(2,1)S(1)}, u32[]{:S(2)}, u32[]{:S(2)}) collective-permute-start(bf16[8,128,128]{2,1,0:T(8,128)(2,1)} %own_two.1), channel_id=1, source_target_pairs={{0,2},{2,4},{3,1},{4,6},{5,3},{6,8},{7,5},{8,10},{9,7},{10,12},{11... | collective-permute-start | bytes 786440 | tf_op jit(solution)/shard_map/ppermute | solution.py:309
  3.7 0.8 constant_dynamic-slice_fusion.2
  4.5 4.1 %collective-permute-start.2 = (bf16[1,128,128]{2,1,0:T(8,128)(2,1)S(1)}, bf16[1,128,128]{2,1,0:T(8,128)(2,1)S(1)}, u32[]{:S(2)}, u32[]{:S(2)}) collective-permute-start(bf16[1,128,128]{2,1,0:T(8,128)(2,1)S(1)} %constant_dynamic-slice_fusion.2), channel_id=1, source_target_pairs={{1,4},{3,6},{4,1},{5,8},{6,3},{7,10},{8,5},{9,12},{10,7},{11,14},{... | collective-permute-start | bytes 98312 | tf_op jit(solution)/shard_map/ppermute | solution.py:309
  8.6 0.8 constant_dynamic-slice_fusion.1
  9.4 1.0 %pad_maximum_fusion.1 = bf16[9,128,128]{2,1,0:T(8,128)(2,1)S(1)} fusion(bf16[1,128,128]{2,1,0:T(8,128)(2,1)S(1)} %get-tuple-element.24, bf16[8,128,128]{2,1,0:T(8,128)(2,1)} %own_two.1), kind=kLoop, calls=%fused_computation.1 | loop fusion | flops 147456 | bytes 589824 | tf_op jit(solution)/shard_map/concatenate | solution.py:320
  10.5 3.1 %collective-permute-start = (bf16[9,128,128]{2,1,0:T(8,128)(2,1)S(1)}, bf16[9,128,128]{2,1,0:T(8,128)(2,1)S(1)}, u32[]{:S(2)}, u32[]{:S(2)}) collective-permute-start(bf16[9,128,128]{2,1,0:T(8,128)(2,1)S(1)} %pad_maximum_fusion.1), channel_id=1, source_target_pairs={{1,3},{2,0},{3,5},{4,2},{5,7},{6,4},{7,9},{8,6},{9,11},{10,8},{11,... | collective-permute-start | bytes 884744 | tf_op jit(solution)/shard_map/ppermute | solution.py:309
  13.7 6.7 %collective-permute-done.near = bf16[9,128,128]{2,1,0:T(8,128)(2,1)S(1)} collective-permute-done((bf16[9,128,128]{2,1,0:T(8,128)(2,1)S(1)}, bf16[9,128,128]{2,1,0:T(8,128)(2,1)S(1)}, u32[]{:S(2)}, u32[]{:S(2)}) %collective-permute-start) | collective-permute-done | bytes 294944 | tf_op jit(solution)/shard_map/ppermute | solution.py:309
  20.6 0.6 copy-done.2
  21.2 0.6 collective-permute-start.3
  22.6 0.6 pad_add_fusion.plan
  23.2 0.7 stack.2.labels
  23.9 0.6 copy-done.7
  24.5 0.3 copy-done.3
  24.7 40.2 %work.1 = (bf16[19,128,128]{2,1,0:T(8,128)(2,1)}, f32[8,128,128]{2,1,0:T(8,128)}, f32[8,128,128]{2,1,0:T(8,128)}, bf16[1,128,128]{2,1,0:T(8,128)(2,1)}, f32[8,128,128]{2,1,0:T(8,128)}, /*index=5*/f32[8,128,128]{2,1,0:T(8,128)}) custom-call(s32[8]{0:T(128)} %pad_add_fusion.plan, bf16[8,128,128]{2,1,0:T(8,128)(2,1)} %own_one.1, bf16[8,128,128]{2,1,0:T(8,128)(2,1)} %own_two.1, ...), custom_call_target="tpu_custom_call" | custom-call | tf_op jit(solution)/shard_map/work/pallas_call | solution.py:277
  65.0 2.3 %collective-permute-done.4.from_sibling = bf16[19,128,128]{2,1,0:T(8,128)(2,1)S(1)} collective-permute-done((bf16[19,128,128]{2,1,0:T(8,128)(2,1)}, bf16[19,128,128]{2,1,0:T(8,128)(2,1)S(1)}, u32[]{:S(2)}, u32[]{:S(2)}) %collective-permute-start.4) | collective-permute-done | bytes 622624 | tf_op jit(solution)/shard_map/ppermute | solution.py:309
  67.2 0.9 copy-done.1
  68.1 2.3 %join.1 = (bf16[9,128,128]{2,1,0:T(8,128)(2,1)}, bf16[8,128,128]{2,1,0:T(8,128)(2,1)}) custom-call(s32[8]{0:T(128)} %pad_add_fusion.plan, f32[8,128,128]{2,1,0:T(8,128)} %get-tuple-element.13.ahead, f32[8,128,128]{2,1,0:T(8,128)} %get-tuple-element.14.behind, bf16[19,128,128]{2,1,0:T(8,128)(2,1)} %copy-done.1), custom_call_target="tpu_custom_call" | custom-call | tf_op jit(solution)/shard_map/join/pallas_call | solution.py:277
  70.4 2.1 %collective-permute-start.5 = (bf16[9,128,128]{2,1,0:T(8,128)(2,1)}, bf16[9,128,128]{2,1,0:T(8,128)(2,1)S(1)}, u32[]{:S(2)}, u32[]{:S(2)}) collective-permute-start(bf16[9,128,128]{2,1,0:T(8,128)(2,1)} %get-tuple-element.15), channel_id=1, source_target_pairs={{0,2},{2,4},{3,1},{4,6},{5,3},{6,8},{7,5},{8,10},{9,7},{10,12},{11... | collective-permute-start | bytes 884744 | tf_op jit(solution)/shard_map/ppermute | solution.py:309
  72.5 3.2 %collective-permute-start.6 = (bf16[8,128,128]{2,1,0:T(8,128)(2,1)}, bf16[8,128,128]{2,1,0:T(8,128)(2,1)S(1)}, u32[]{:S(2)}, u32[]{:S(2)}) collective-permute-start(bf16[8,128,128]{2,1,0:T(8,128)(2,1)} %get-tuple-element.16), channel_id=1, source_target_pairs={{1,3},{2,0},{3,5},{4,2},{5,7},{6,4},{7,9},{8,6},{9,11},{10,8},{11,... | collective-permute-start | bytes 786440 | tf_op jit(solution)/shard_map/ppermute | solution.py:309
  75.7 4.7 %collective-permute-start.7 = (bf16[1,128,128]{2,1,0:T(8,128)(2,1)S(1)}, bf16[1,128,128]{2,1,0:T(8,128)(2,1)S(1)}, u32[]{:S(2)}, u32[]{:S(2)}) collective-permute-start(bf16[1,128,128]{2,1,0:T(8,128)(2,1)S(1)} %copy-done.10), channel_id=1, source_target_pairs={{1,4},{3,6},{4,1},{5,8},{6,3},{7,10},{8,5},{9,12},{10,7},{11,14},{... | collective-permute-start | bytes 98312 | tf_op jit(solution)/shard_map/ppermute | solution.py:309
  80.3 3.0 %collective-permute-done.7.far = bf16[1,128,128]{2,1,0:T(8,128)(2,1)S(1)} collective-permute-done((bf16[1,128,128]{2,1,0:T(8,128)(2,1)S(1)}, bf16[1,128,128]{2,1,0:T(8,128)(2,1)S(1)}, u32[]{:S(2)}, u32[]{:S(2)}) %collective-permute-start.7) | collective-permute-done | bytes 32800 | tf_op jit(solution)/shard_map/ppermute | solution.py:309
  83.4 3.5 %collective-permute-done.6.behind = bf16[8,128,128]{2,1,0:T(8,128)(2,1)S(1)} collective-permute-done((bf16[8,128,128]{2,1,0:T(8,128)(2,1)}, bf16[8,128,128]{2,1,0:T(8,128)(2,1)S(1)}, u32[]{:S(2)}, u32[]{:S(2)}) %collective-permute-start.6) | collective-permute-done | bytes 262176 | tf_op jit(solution)/shard_map/ppermute | solution.py:309
  86.9 0.7 copy-done.6
  87.7 2.5 %final.1 = (bf16[8,128,128]{2,1,0:T(8,128)(2,1)}, bf16[8,128,128]{2,1,0:T(8,128)(2,1)}) custom-call(s32[8]{0:T(128)} %pad_add_fusion.plan, f32[8,128,128]{2,1,0:T(8,128)} %get-tuple-element.10.sum_one, f32[8,128,128]{2,1,0:T(8,128)} %get-tuple-element.11.sum_two, bf16[19,128,128]{2,1,0:T(8,128)(2,1)} %copy-done.1, bf16[9,128,128]{2,1,0:T(8,128)(2,1)} %copy-done.5, ...), custom_call_target="tpu_custom_call" | custom-call | tf_op jit(solution)/shard_map/final/pallas_call | solution.py:277
  (31 shorter events, 0.4 us)
Async XLA Ops:
  0.6 13.1 %collective-permute-start.1 = (bf16[8,128,128]{2,1,0:T(8,128)(2,1)}, bf16[8,128,128]{2,1,0:T(8,128)(2,1)S(1)}, u32[]{:S(2)}, u32[]{:S(2)}) collective-permute-start(bf16[8,128,128]{2,1,0:T(8,128)(2,1)} %own_two.1), channel_id=1, source_target_pairs={{0,2},{2,4},{3,1},{4,6},{5,3},{6,8},{7,5},{8,10},{9,7},{10,12},{11... | collective-permute-start | bytes 786440 | tf_op jit(solution)/shard_map/ppermute | solution.py:309
  4.5 19.4 %collective-permute-start.2 = (bf16[1,128,128]{2,1,0:T(8,128)(2,1)S(1)}, bf16[1,128,128]{2,1,0:T(8,128)(2,1)S(1)}, u32[]{:S(2)}, u32[]{:S(2)}) collective-permute-start(bf16[1,128,128]{2,1,0:T(8,128)(2,1)S(1)} %constant_dynamic-slice_fusion.2), channel_id=1, source_target_pairs={{1,4},{3,6},{4,1},{5,8},{6,3},{7,10},{8,5},{9,12},{10,7},{11,14},{... | collective-permute-start | bytes 98312 | tf_op jit(solution)/shard_map/ppermute | solution.py:309
  9.4 4.2 %copy-start.9 = (s32[8,128]{1,0:T(8,128)S(1)}, s32[8,128]{1,0:T(8,128)}, u32[]{:S(2)}) copy-start(s32[8,128]{1,0:T(8,128)} %param.11) | copy-start | bytes 12292
  9.4 11.0 %copy-start = (bf16[8,128,128]{2,1,0:T(8,128)(2,1)S(1)}, bf16[8,128,128]{2,1,0:T(8,128)(2,1)}, u32[]{:S(2)}) copy-start(bf16[8,128,128]{2,1,0:T(8,128)(2,1)} %own_two.1) | copy-start | bytes 786436
  10.5 10.0 %collective-permute-start = (bf16[9,128,128]{2,1,0:T(8,128)(2,1)S(1)}, bf16[9,128,128]{2,1,0:T(8,128)(2,1)S(1)}, u32[]{:S(2)}, u32[]{:S(2)}) collective-permute-start(bf16[9,128,128]{2,1,0:T(8,128)(2,1)S(1)} %pad_maximum_fusion.1), channel_id=1, source_target_pairs={{1,3},{2,0},{3,5},{4,2},{5,7},{6,4},{7,9},{8,6},{9,11},{10,8},{11,... | collective-permute-start | bytes 884744 | tf_op jit(solution)/shard_map/ppermute | solution.py:309
  13.7 6.9 %copy-start.4 = (bf16[8,128,128]{2,1,0:T(8,128)(2,1)}, bf16[8,128,128]{2,1,0:T(8,128)(2,1)S(1)}, u32[]{:S(2)}) copy-start(bf16[8,128,128]{2,1,0:T(8,128)(2,1)S(1)} %collective-permute-done.1.direct) | copy-start | bytes 786436
  20.5 0.7 copy-start.2
  20.5 1.4 %copy-start.11 = (s32[1,4]{1,0:T(1,128)S(1)}, s32[1,4]{1,0:T(1,128)}, u32[]{:S(2)}) copy-start(s32[1,4]{1,0:T(1,128)} %param.9) | copy-start | bytes 52
  21.2 2.7 %collective-permute-start.3 = (bf16[19,128,128]{2,1,0:T(8,128)(2,1)S(1)}, bf16[19,128,128]{2,1,0:T(8,128)(2,1)S(1)}, u32[]{:S(2)}, u32[]{:S(2)}) collective-permute-start(bf16[19,128,128]{2,1,0:T(8,128)(2,1)S(1)} %pad_maximum_fusion), channel_id=1, source_target_pairs={{0,1},{1,0},{2,3},{3,2},{4,5},{5,4},{6,7},{7,6},{8,9},{9,8},{10,11... | collective-permute-start | bytes 1867784 | tf_op jit(solution)/shard_map/ppermute | solution.py:309
  23.9 0.6 copy-start.7
  23.9 0.9 copy-start.3
  65.0 2.3 %collective-permute-start.4 = (bf16[19,128,128]{2,1,0:T(8,128)(2,1)}, bf16[19,128,128]{2,1,0:T(8,128)(2,1)S(1)}, u32[]{:S(2)}, u32[]{:S(2)}) collective-permute-start(bf16[19,128,128]{2,1,0:T(8,128)(2,1)} %get-tuple-element.12), channel_id=1, source_target_pairs={{0,1},{1,0},{2,3},{3,2},{4,5},{5,4},{6,7},{7,6},{8,9},{9,8},{10,11... | collective-permute-start | bytes 1867784 | tf_op jit(solution)/shard_map/ppermute | solution.py:309
  67.2 0.9 copy-start.1
  68.1 7.6 %copy-start.10 = (bf16[1,128,128]{2,1,0:T(8,128)(2,1)S(1)}, bf16[1,128,128]{2,1,0:T(8,128)(2,1)}, u32[]{:S(2)}) copy-start(bf16[1,128,128]{2,1,0:T(8,128)(2,1)} %get-tuple-element.17) | copy-start | bytes 98308
  70.4 16.5 %collective-permute-start.5 = (bf16[9,128,128]{2,1,0:T(8,128)(2,1)}, bf16[9,128,128]{2,1,0:T(8,128)(2,1)S(1)}, u32[]{:S(2)}, u32[]{:S(2)}) collective-permute-start(bf16[9,128,128]{2,1,0:T(8,128)(2,1)} %get-tuple-element.15), channel_id=1, source_target_pairs={{0,2},{2,4},{3,1},{4,6},{5,3},{6,8},{7,5},{8,10},{9,7},{10,12},{11... | collective-permute-start | bytes 884744 | tf_op jit(solution)/shard_map/ppermute | solution.py:309
  72.5 14.4 %collective-permute-start.6 = (bf16[8,128,128]{2,1,0:T(8,128)(2,1)}, bf16[8,128,128]{2,1,0:T(8,128)(2,1)S(1)}, u32[]{:S(2)}, u32[]{:S(2)}) collective-permute-start(bf16[8,128,128]{2,1,0:T(8,128)(2,1)} %get-tuple-element.16), channel_id=1, source_target_pairs={{1,3},{2,0},{3,5},{4,2},{5,7},{6,4},{7,9},{8,6},{9,11},{10,8},{11,... | collective-permute-start | bytes 786440 | tf_op jit(solution)/shard_map/ppermute | solution.py:309
  75.7 7.7 %collective-permute-start.7 = (bf16[1,128,128]{2,1,0:T(8,128)(2,1)S(1)}, bf16[1,128,128]{2,1,0:T(8,128)(2,1)S(1)}, u32[]{:S(2)}, u32[]{:S(2)}) collective-permute-start(bf16[1,128,128]{2,1,0:T(8,128)(2,1)S(1)} %copy-done.10), channel_id=1, source_target_pairs={{1,4},{3,6},{4,1},{5,8},{6,3},{7,10},{8,5},{9,12},{10,7},{11,14},{... | collective-permute-start | bytes 98312 | tf_op jit(solution)/shard_map/ppermute | solution.py:309
  83.3 3.5 %copy-start.8 = (bf16[1,128,128]{2,1,0:T(8,128)(2,1)}, bf16[1,128,128]{2,1,0:T(8,128)(2,1)S(1)}, u32[]{:S(2)}) copy-start(bf16[1,128,128]{2,1,0:T(8,128)(2,1)S(1)} %collective-permute-done.7.far) | copy-start | bytes 98308
  86.9 0.7 copy-start.6
  86.9 0.8 copy-start.5

commit v2 on v1

--- a/solution.py
+++ b/solution.py
@@ -19,6 +19,7 @@
 POOLED = PIX // 4 + PIX // 16 + PIX // 64
 PAD = 384
 CELLS = PIX + PAD
+LIMIT = 56
 WIN = 2 * RADIUS * TR + TR + 2
 
 NN = (((1,), (0,)), ((), ()))
@@ -77,24 +78,23 @@
         moved[rows, 0:CH] = up.astype(jnp.bfloat16)
         moved[rows, CH : 2 * CH] = block.astype(jnp.bfloat16)
         moved[rows, 2 * CH : 3 * CH] = down.astype(jnp.bfloat16)
+    parts = matmul(moved[...], weight_back[...], NT)
     for a in range(3):
-        part = matmul(moved[...], weight_back[a * CIN : (a + 1) * CIN, :], NT)
         where = pl.ds(pl.multiple_of((at + a) * TC, TC), PIX)
-        total[where, :] += part
-
-
-def pool_matrix():
-    cell = lax.broadcasted_iota(jnp.int32, (PAD, PIX), 0)
-    pixel = lax.broadcasted_iota(jnp.int32, (PAD, PIX), 1)
+        total[where, :] += parts[:, a * CIN : (a + 1) * CIN]
+
+
+def pool_matrix(shape, cell_axis, values):
+    cell = lax.broadcasted_iota(jnp.int32, shape, cell_axis)
+    pixel = lax.broadcasted_iota(jnp.int32, shape, 1 - cell_axis)
     row, column = pixel // TC, pixel % TC
     offset = 0
-    inside = jnp.zeros((PAD, PIX), jnp.bool_)
+    result = jnp.zeros(shape, jnp.float32)
     for level in range(1, LEVELS):
-        cells = PIX >> (2 * level)
         own = offset + (row >> level) * (TC >> level) + (column >> level)
-        inside = inside | ((cell >= offset) & (cell < offset + cells) & (cell == own))
-        offset += cells
-    return jnp.where(inside, 1.0, 0.0).astype(jnp.bfloat16)
+        result = jnp.where(cell == own, values[level], result)
+        offset += PIX >> (2 * level)
+    return result.astype(jnp.bfloat16)
 
 
 def per_level(values, fill):
@@ -105,6 +105,16 @@
         result = jnp.where(cell >= offset, values[level], result)
         offset += PIX >> (2 * level)
     return jnp.where(cell >= offset, fill, result)
+
+
+def tables_kernel(weight, weight_back, pool, unpool):
+    for a in range(3):
+        for b in range(3):
+            weight_back[a * CIN : (a + 1) * CIN, b * CH : (b + 1) * CH] = weight[
+                (3 * a + b) * CIN : (3 * a + b + 1) * CIN, :
+            ]
+    pool[...] = pool_matrix((PAD, PIX), 0, [1.0] * LEVELS)
+    unpool[...] = pool_matrix((PIX, PAD), 1, [2.0**-level for level in range(LEVELS)])
 
 
 def work_kernel(
@@ -116,6 +126,9 @@
     far,
     from_sibling,
     weight,
+    weight_back,
+    pool,
+    unpool,
     labels,
     to_sibling,
     ahead,
@@ -127,8 +140,6 @@
     spread_two,
     window_one,
     spread_one,
-    weight_back,
-    pool,
     feat_one,
     pyramid,
     dscore,
@@ -166,12 +177,6 @@
     lax.fori_loop(0, WIN, spread, 0)
     for r in range(TR + 2):
         spread_columns(window_one, r, spread_one, r)
-    for a in range(3):
-        for b in range(3):
-            weight_back[a * CIN : (a + 1) * CIN, b * CH : (b + 1) * CH] = weight[
-                (3 * a + b) * CIN : (3 * a + b + 1) * CIN, :
-            ]
-    pool[...] = pool_matrix()
     feat_one[...] = convolve(spread_one, 0, weight)
     grad_rows[...] = jnp.zeros_like(grad_rows)
     total_two[...] = jnp.zeros_like(total_two)
@@ -207,14 +212,9 @@
                 dscore[start : start + size, :] = value.astype(jnp.bfloat16)
             level_grad[...] = matmul(dscore[...], features, NN)
             grad_rows[...] += matmul(dscore[...], pyramid[...], TN)
-            coarse = level_grad[PIX:CELLS, :] * per_level(
-                [2.0 ** (-level - 5) for level in range(LEVELS)], 0.0
-            )
-            high = coarse.astype(jnp.bfloat16)
-            low = (coarse - high.astype(jnp.float32)).astype(jnp.bfloat16)
-            gradient = level_grad[0:PIX, :] * 2.0**-5
-            gradient = gradient + matmul(pool[...], high, TN)
-            gradient = gradient + matmul(pool[...], low, TN)
+            coarse = level_grad[PIX:CELLS, :].astype(jnp.bfloat16)
+            gradient = level_grad[0:PIX, :] + matmul(unpool[...], coarse, NN)
+            gradient = gradient * 2.0**-5
             convolve_back(gradient, weight_back, moved, total_two, first)
 
         return carry
@@ -235,52 +235,22 @@
         total_one, jnp.where(side > 0, 0, TR + 1)
     ).astype(jnp.bfloat16)
     ahead[...] = rows(total_two, at(2 * side), TR)
-    behind[...] = rows(total_two, at(-2 * side), TR)
+    behind[...] = rows(total_two, at(-2 * side), TR).astype(jnp.bfloat16)
     far_out[...] = rows(total_two, edge(-side)).astype(jnp.bfloat16)
     sum_two[...] = rows(total_two, at(0), TR)
     sum_one[...] = rows(total_one, 1, TR)
 
 
-def join_kernel(plan, ahead, behind, from_sibling, ahead_out, behind_out, held):
-    side = plan[5]
-    for r in range(TR):
-        ahead_out[r] = (ahead[r] + from_sibling[TR + r].astype(jnp.float32)).astype(jnp.bfloat16)
-    ahead_out[TR] = from_sibling[2 * TR + 2]
-    held[...] = behind[...]
-    row = jnp.where(side > 0, TR - 1, 0)
-    held[row] = held[row] + from_sibling[2 * TR].astype(jnp.float32)
-    behind_out[...] = held[...].astype(jnp.bfloat16)
-
-
-def final_kernel(plan, sum_one, sum_two, from_sibling, ahead, behind, far, one, two, held_one, held_two):
-    side = plan[5]
-    facing = jnp.where(side > 0, TR - 1, 0)
-    outer = jnp.where(side > 0, 0, TR - 1)
-    held_one[...] = sum_one[...]
-    held_one[facing] = held_one[facing] + from_sibling[2 * TR + 1].astype(jnp.float32)
-    held_one[outer] = held_one[outer] + ahead[TR].astype(jnp.float32)
-    one[...] = held_one[...].astype(jnp.bfloat16)
-    for r in range(TR):
-        held_two[r] = (
-            sum_two[r]
-            + from_sibling[r].astype(jnp.float32)
-            + ahead[r].astype(jnp.float32)
-            + behind[r].astype(jnp.float32)
-        )
-    held_two[outer] = held_two[outer] + far[0].astype(jnp.float32)
-    two[...] = held_two[...].astype(jnp.bfloat16)
-
-
-def call(kernel, outs, scratch, args, name):
+def call(kernel, outs, scratch, args, name, scalars=1, limit=LIMIT):
     smem = pl.BlockSpec(memory_space=pltpu.SMEM)
     vmem = pl.BlockSpec(memory_space=pltpu.VMEM)
     return pl.pallas_call(
         kernel,
-        in_specs=[smem] + [vmem] * (len(args) - 1),
+        in_specs=[smem] * scalars + [vmem] * (len(args) - scalars),
         out_specs=[vmem] * len(outs),
         out_shape=[jax.ShapeDtypeStruct(*out) for out in outs],
         scratch_shapes=[pltpu.VMEM(*item) for item in scratch],
-        compiler_params=pltpu.CompilerParams(vmem_limit_bytes=56 << 20),
+        compiler_params=pltpu.CompilerParams(vmem_limit_bytes=limit << 20),
         name=name,
     )(*args)
 
@@ -316,26 +286,34 @@
     ).astype(jnp.int32)
     labels = label_rows(targets)
     weight = conv_weight.reshape(9 * CIN, CH)
-    outward = row_of(frame_one, side > 0)
-    near = send(jnp.concatenate([frame_two, outward]), "behind")
     direct = send(frame_two, "ahead")
-    far = send(row_of(frame_two, side > 0), "far")
+    near_in = jnp.concatenate([frame_two, row_of(frame_one, side > 0)])
+    near = send(near_in, "behind")
+    tables = call(
+        tables_kernel,
+        [((3 * CIN, 3 * CH), bf16), ((PAD, PIX), bf16), ((PIX, PAD), bf16)],
+        [],
+        [weight],
+        "tables",
+        scalars=0,
+    )
     inward = row_of(frame_one, side < 0)
+    far_in, direct = lax.optimization_barrier((row_of(frame_two, side > 0), direct))
+    far = send(far_in, "far")
     payload = jnp.concatenate([frame_two, near, inward, row_of(direct, side < 0)])
+    payload, tables, labels, plan = lax.optimization_barrier((payload, tables, labels, plan))
     from_sibling = send(payload, "swap")
 
     tile = (TR, TC, CIN)
     pack = (2 * TR + 3, TC, CIN)
     to_sibling, ahead, behind, far_out, sum_one, sum_two = call(
         work_kernel,
-        [(pack, bf16), (tile, f32), (tile, f32), ((1, TC, CIN), bf16), (tile, f32), (tile, f32)],
+        [(pack, bf16), (tile, f32), (tile, bf16), ((1, TC, CIN), bf16), (tile, f32), (tile, f32)],
         [
             ((WIN, TC, CIN), bf16),
             ((WIN * TC, 3 * CIN), bf16),
             ((TR + 2, TC, CIN), bf16),
             (((TR + 2) * TC, 3 * CIN), bf16),
-            ((3 * CIN, 3 * CH), bf16),
-            ((PAD, PIX), bf16),
             ((PIX, CH), bf16),
             ((CELLS, CH), bf16),
             ((CELLS, PIX), bf16),
@@ -345,27 +323,33 @@
             ((WIN * TC, CIN), f32),
             (((TR + 2) * TC, CIN), f32),
         ],
-        [plan, frame_one, frame_two, near, direct, far, from_sibling, weight, labels],
+        [plan, frame_one, frame_two, near, direct, far, from_sibling, weight, *tables, labels],
         "work",
     )
+    back_behind = send(behind, "behind")
     back_sibling = send(to_sibling, "swap")
-    ahead_out, behind_out = call(
-        join_kernel,
-        [((TR + 1, TC, CIN), bf16), (tile, bf16)],
-        [(tile, f32)],
-        [plan, ahead, behind, back_sibling],
-        "join",
-    )
-    back_ahead = send(ahead_out, "ahead")
-    back_behind = send(behind_out, "behind")
+    joined = (ahead + back_sibling[TR : 2 * TR].astype(f32)).astype(bf16)
+    ahead_in = jnp.concatenate([joined, back_sibling[2 * TR + 2 :]])
+    far_out, edge, ahead_in = lax.optimization_barrier(
+        (far_out, back_sibling[2 * TR : 2 * TR + 1], ahead_in)
+    )
+    back_ahead = send(ahead_in, "ahead")
     back_far = send(far_out, "far")
-    return call(
-        final_kernel,
-        [(tile, bf16), (tile, bf16)],
-        [(tile, f32), (tile, f32)],
-        [plan, sum_one, sum_two, back_sibling, back_ahead, back_behind, back_far],
-        "final",
-    )
+    back_edge = send(edge, "behind")
+
+    row = lax.broadcasted_iota(jnp.int32, (TR, 1, 1), 0)
+    facing = row == jnp.where(side > 0, TR - 1, 0)
+    outer = row == jnp.where(side > 0, 0, TR - 1)
+
+    def place(where, block):
+        return jnp.where(where, block.astype(f32), 0.0)
+
+    grad_one = sum_one + place(facing, back_sibling[2 * TR + 1 : 2 * TR + 2])
+    grad_one = grad_one + place(outer, back_ahead[TR:])
+    grad_two = sum_two + back_sibling[:TR].astype(f32) + back_ahead[:TR].astype(f32)
+    grad_two = grad_two + back_behind.astype(f32)
+    grad_two = grad_two + place(outer, back_far) + place(facing, back_edge)
+    return grad_one.astype(bf16), grad_two.astype(bf16)
 
 
 def solution(mesh):

time: 91.7 us -> 80.3 us (0.88)
  Pallas kernels: 45 us -> 31.5 us
  other arithmetic: 1.88 us -> 4.14 us
  starting transfers between devices: 20.9 us -> 22 us
    pallas_call x3 -> x2, Pallas kernels: 45 us -> 31.5 us  [call(): pl.pallas_call(kernel, in_specs=[smem] * scalars + [vmem] * (len(args) -...]
    convert_element_type x0 -> x2, other arithmetic: none -> 2.27 us  [the longest x1 1.17 us: on_device(): joined = (ahead + back_sibling[TR:2 * TR].astype(f32)).astype(bf16)]
    ppermute x8 -> x9, starting transfers between devices: 20.9 us -> 22 us  [send(): return lax.ppermute(block, 'tile', route[name])]
    ppermute x8 -> x9, waiting for transfers between devices: 15.5 us -> 14.9 us  [send(): return lax.ppermute(block, 'tile', route[name])]
    unnamed x24 -> x22, local copies, waits for them, and re-layouts: 3.14 us -> 3.47 us
  transfers between devices with their start and end apart: 8 -> 9, of which waited for: 4 -> 5; matrix products, arithmetic and copies ran while one was open for 5% -> 4% of each run, Pallas kernels for 0% -> 4%
where the time goes in v2:
time: 80.3 us; the launch traced here: 79 us
  Pallas kernels  31.5 us (39%)
  starting transfers between devices  22 us (27%)
  waiting for transfers between devices  14.9 us (19%)
  local copies, waits for them, and re-layouts  4.94 us (6%)
  other arithmetic  4.14 us (5%)
  between operations  1.55 us (2%)
    pallas_call x2, Pallas kernels, call(): pl.pallas_call(kernel, in_specs=[smem] * scalars + [vmem] * (len(args) -...  31.5 us
    ppermute x9, starting transfers between devices, send(): return lax.ppermute(block, 'tile', route[name])  22 us
    ppermute x9, waiting for transfers between devices, send(): return lax.ppermute(block, 'tile', route[name])  14.9 us
    unnamed x22, local copies, waits for them, and re-layouts  3.47 us
  transfers between devices with their start and end apart: 9, of which 5 were waited for; matrix products, arithmetic and copies ran while one was open for 4% of the time, Pallas kernels for 4%

profile of v2, /device:TPU:9, one launch (start us, length us, event | category | flops | bytes accessed | tf_op | source)
XLA Modules:
  0.0 79.0 jit_solution(4366909457363410034)
XLA Ops:
  0.6 3.0 %collective-permute-start.1 = (bf16[8,128,128]{2,1,0:T(8,128)(2,1)}, bf16[8,128,128]{2,1,0:T(8,128)(2,1)S(1)}, u32[]{:S(2)}, u32[]{:S(2)}) collective-permute-start(bf16[8,128,128]{2,1,0:T(8,128)(2,1)} %own_two.1), channel_id=1, source_target_pairs={{0,2},{2,4},{3,1},{4,6},{5,3},{6,8},{7,5},{8,10},{9,7},{10,12},{11... | collective-permute-start | bytes 786440 | tf_op jit(solution)/shard_map/ppermute | solution.py:279
  3.7 0.8 constant_dynamic-slice_fusion.3
  4.5 1.0 %pad_maximum_fusion.1 = bf16[9,128,128]{2,1,0:T(8,128)(2,1)S(1)} fusion(bf16[1,128,128]{2,1,0:T(8,128)(2,1)S(1)} %get-tuple-element.50, bf16[8,128,128]{2,1,0:T(8,128)(2,1)} %own_two.1), kind=kLoop, calls=%fused_computation.4 | loop fusion | flops 147456 | bytes 589824 | tf_op jit(solution)/shard_map/concatenate | solution.py:290
  5.5 2.2 %collective-permute-start = (bf16[9,128,128]{2,1,0:T(8,128)(2,1)S(1)}, bf16[9,128,128]{2,1,0:T(8,128)(2,1)S(1)}, u32[]{:S(2)}, u32[]{:S(2)}) collective-permute-start(bf16[9,128,128]{2,1,0:T(8,128)(2,1)S(1)} %pad_maximum_fusion.1), channel_id=1, source_target_pairs={{1,3},{2,0},{3,5},{4,2},{5,7},{6,4},{7,9},{8,6},{9,11},{10,8},{11,... | collective-permute-start | bytes 884744 | tf_op jit(solution)/shard_map/ppermute | solution.py:279
  7.9 0.6 copy-done.10
  9.2 3.0 %tables.1 = (bf16[384,768]{1,0:T(8,128)(2,1)}, bf16[384,1024]{1,0:T(8,128)(2,1)}, bf16[1024,384]{1,0:T(8,128)(2,1)}) custom-call(bf16[1152,256]{1,0:T(8,128)(2,1)} %bitcast.21), custom_call_target="tpu_custom_call" | custom-call | tf_op jit(solution)/shard_map/tables/pallas_call | solution.py:247
  12.2 0.7 stack.2.labels
  12.8 0.6 pad_add_fusion.plan
  13.5 3.8 %collective-permute-done.near = bf16[9,128,128]{2,1,0:T(8,128)(2,1)S(1)} collective-permute-done((bf16[9,128,128]{2,1,0:T(8,128)(2,1)S(1)}, bf16[9,128,128]{2,1,0:T(8,128)(2,1)S(1)}, u32[]{:S(2)}, u32[]{:S(2)}) %collective-permute-start) | collective-permute-done | bytes 294944 | tf_op jit(solution)/shard_map/ppermute | solution.py:279
  17.4 0.6 copy-done.1
  18.5 3.1 %collective-permute-start.2 = (bf16[1,128,128]{2,1,0:T(8,128)(2,1)S(1)}, bf16[1,128,128]{2,1,0:T(8,128)(2,1)S(1)}, u32[]{:S(2)}, u32[]{:S(2)}) collective-permute-start(bf16[1,128,128]{2,1,0:T(8,128)(2,1)S(1)} %constant_dynamic-slice_fusion.1), channel_id=1, source_target_pairs={{1,4},{3,6},{4,1},{5,8},{6,3},{7,10},{8,5},{9,12},{10,7},{11,14},{... | collective-permute-start | bytes 98312 | tf_op jit(solution)/shard_map/ppermute | solution.py:279
  21.7 2.1 %collective-permute-done.2.far = bf16[1,128,128]{2,1,0:T(8,128)(2,1)S(1)} collective-permute-done((bf16[1,128,128]{2,1,0:T(8,128)(2,1)S(1)}, bf16[1,128,128]{2,1,0:T(8,128)(2,1)S(1)}, u32[]{:S(2)}, u32[]{:S(2)}) %collective-permute-start.2) | collective-permute-done | bytes 32800 | tf_op jit(solution)/shard_map/ppermute | solution.py:279
  24.3 0.8 %copy-done.2 = bf16[19,128,128]{2,1,0:T(8,128)(2,1)} copy-done((bf16[19,128,128]{2,1,0:T(8,128)(2,1)}, bf16[19,128,128]{2,1,0:T(8,128)(2,1)S(1)}, u32[]{:S(2)}) %copy-start.2) | copy-done | bytes 622616
  25.2 28.4 %work.1 = (bf16[19,128,128]{2,1,0:T(8,128)(2,1)}, f32[8,128,128]{2,1,0:T(8,128)}, bf16[8,128,128]{2,1,0:T(8,128)(2,1)}, bf16[1,128,128]{2,1,0:T(8,128)(2,1)}, f3...) custom-call(s32[8]{0:T(128)} %pad_add_fusion.plan, bf16[8,128,128]{2,1,0:T(8,128)(2,1)} %own_one.1, ...), custom_call_target="tpu_custom_call" | custom-call | tf_op jit(solution)/shard_map/work/pallas_call | solution.py:247
  53.7 2.2 %collective-permute-done.4 = bf16[19,128,128]{2,1,0:T(8,128)(2,1)S(1)} collective-permute-done((bf16[19,128,128]{2,1,0:T(8,128)(2,1)}, bf16[19,128,128]{2,1,0:T(8,128)(2,1)S(1)}, u32[]{:S(2)}, u32[]{:S(2)}) %collective-permute-start.4) | collective-permute-done | bytes 622624 | tf_op jit(solution)/shard_map/ppermute | solution.py:279
  55.9 1.2 %add_convert_fusion.2 = bf16[8,128,128]{2,1,0:T(8,128)(2,1)S(1)} fusion(f32[8,128,128]{2,1,0:T(8,128)} %get-tuple-element.36, bf16[19,128,128]{2,1,0:T(8,128)(2,1)S(1)} %collective-permute-done.4), kind=kLoop, calls=%fused_computation.3 | loop fusion | flops 393216 | bytes 1048576 | tf_op jit(solution)/shard_map/convert_element_type | solution.py:331
  57.1 0.8 copy-done.9
  57.9 3.2 %collective-permute-start.7 = (bf16[1,128,128]{2,1,0:T(8,128)(2,1)S(1)}, bf16[1,128,128]{2,1,0:T(8,128)(2,1)S(1)}, u32[]{:S(2)}, u32[]{:S(2)}) collective-permute-start(bf16[1,128,128]{2,1,0:T(8,128)(2,1)S(1)} %copy-done.9), channel_id=1, source_target_pairs={{1,4},{3,6},{4,1},{5,8},{6,3},{7,10},{8,5},{9,12},{10,7},{11,14},{... | collective-permute-start | bytes 98312 | tf_op jit(solution)/shard_map/ppermute | solution.py:279
  61.2 3.7 %collective-permute-start.6 = (bf16[8,128,128]{2,1,0:T(8,128)(2,1)S(1)}, bf16[8,128,128]{2,1,0:T(8,128)(2,1)S(1)}, u32[]{:S(2)}, u32[]{:S(2)}) collective-permute-start(bf16[8,128,128]{2,1,0:T(8,128)(2,1)S(1)} %copy-done.8), channel_id=1, source_target_pairs={{1,3},{2,0},{3,5},{4,2},{5,7},{6,4},{7,9},{8,6},{9,11},{10,8},{11,... | collective-permute-start | bytes 786440 | tf_op jit(solution)/shard_map/ppermute | solution.py:279
  64.8 2.5 %collective-permute-start.8 = (bf16[1,128,128]{2,1,0:T(8,128)(2,1)S(1)}, bf16[1,128,128]{2,1,0:T(8,128)(2,1)S(1)}, u32[]{:S(2)}, u32[]{:S(2)}) collective-permute-start(bf16[1,128,128]{2,1,0:T(8,128)(2,1)S(1)} %get-tuple-element.41), channel_id=1, source_target_pairs={{1,3},{2,0},{3,5},{4,2},{5,7},{6,4},{7,9},{8,6},{9,11},{10,8},{11,... | collective-permute-start | bytes 98312 | tf_op jit(solution)/shard_map/ppermute | solution.py:279
  67.3 3.7 %collective-permute-start.5 = (bf16[9,128,128]{2,1,0:T(8,128)(2,1)S(1)}, bf16[9,128,128]{2,1,0:T(8,128)(2,1)S(1)}, u32[]{:S(2)}, u32[]{:S(2)}) collective-permute-start(bf16[9,128,128]{2,1,0:T(8,128)(2,1)S(1)} %pad_maximum_fusion.2), channel_id=1, source_target_pairs={{0,2},{2,4},{3,1},{4,6},{5,3},{6,8},{7,5},{8,10},{9,7},{10,12},{11... | collective-permute-start | bytes 884744 | tf_op jit(solution)/shard_map/ppermute | solution.py:279
  71.1 6.1 %collective-permute-done.8 = bf16[1,128,128]{2,1,0:T(8,128)(2,1)S(1)} collective-permute-done((bf16[1,128,128]{2,1,0:T(8,128)(2,1)S(1)}, bf16[1,128,128]{2,1,0:T(8,128)(2,1)S(1)}, u32[]{:S(2)}, u32[]{:S(2)}) %collective-permute-start.8) | collective-permute-done | bytes 32800 | tf_op jit(solution)/shard_map/ppermute | solution.py:279
  77.2 0.7 collective-permute-done.5
  77.9 1.1 %add_convert_fusion = (bf16[8,128,128]{2,1,0:T(8,128)(2,1)}, bf16[8,128,128]{2,1,0:T(8,128)(2,1)}) fusion(bf16[8,128,128]{2,1,0:T(8,128)(2,1)S(1)} %collective-permute-done.6, f32[8,128,128]{2,1,0:T(8,128)S(1)} %copy-done.4, bf16[9,128,128]{2,1,0:T(8,128)(2,1)S(1)} %collective-permute-done.5, bf16[19,128,128]{2,1,0:T(8,128)(2,1)S(1)} %collective-permute-done.4, ...), kind=kLoop, calls=%fused_computation.1 | loop fusion | flops 2097152 | bytes 2621456 | tf_op jit(solution)/shard_map/convert_element_type | solution.py:352
  (38 shorter events, 1.4 us)
Async XLA Ops:
  0.6 12.8 %collective-permute-start.1 = (bf16[8,128,128]{2,1,0:T(8,128)(2,1)}, bf16[8,128,128]{2,1,0:T(8,128)(2,1)S(1)}, u32[]{:S(2)}, u32[]{:S(2)}) collective-permute-start(bf16[8,128,128]{2,1,0:T(8,128)(2,1)} %own_two.1), channel_id=1, source_target_pairs={{0,2},{2,4},{3,1},{4,6},{5,3},{6,8},{7,5},{8,10},{9,7},{10,12},{11... | collective-permute-start | bytes 786440 | tf_op jit(solution)/shard_map/ppermute | solution.py:279
  4.5 3.3 %copy-start.7 = (s32[8,128]{1,0:T(8,128)S(1)}, s32[8,128]{1,0:T(8,128)}, u32[]{:S(2)}) copy-start(s32[8,128]{1,0:T(8,128)} %param.11) | copy-start | bytes 12292
  5.5 11.8 %collective-permute-start = (bf16[9,128,128]{2,1,0:T(8,128)(2,1)S(1)}, bf16[9,128,128]{2,1,0:T(8,128)(2,1)S(1)}, u32[]{:S(2)}, u32[]{:S(2)}) collective-permute-start(bf16[9,128,128]{2,1,0:T(8,128)(2,1)S(1)} %pad_maximum_fusion.1), channel_id=1, source_target_pairs={{1,3},{2,0},{3,5},{4,2},{5,7},{6,4},{7,9},{8,6},{9,11},{10,8},{11,... | collective-permute-start | bytes 884744 | tf_op jit(solution)/shard_map/ppermute | solution.py:279
  7.8 0.7 copy-start.10
  9.1 4.3 %copy-start = (bf16[8,128,128]{2,1,0:T(8,128)(2,1)S(1)}, bf16[8,128,128]{2,1,0:T(8,128)(2,1)}, u32[]{:S(2)}) copy-start(bf16[8,128,128]{2,1,0:T(8,128)(2,1)} %own_two.1) | copy-start | bytes 786436
  13.5 4.0 %copy-start.5 = (bf16[8,128,128]{2,1,0:T(8,128)(2,1)}, bf16[8,128,128]{2,1,0:T(8,128)(2,1)S(1)}, u32[]{:S(2)}) copy-start(bf16[8,128,128]{2,1,0:T(8,128)(2,1)S(1)} %collective-permute-done.1.direct) | copy-start | bytes 786436
  17.3 0.7 copy-start.1
  18.1 5.7 %collective-permute-start.3 = (bf16[19,128,128]{2,1,0:T(8,128)(2,1)S(1)}, bf16[19,128,128]{2,1,0:T(8,128)(2,1)S(1)}, u32[]{:S(2)}, u32[]{:S(2)}) collective-permute-start(bf16[19,128,128]{2,1,0:T(8,128)(2,1)S(1)} %pad_maximum_fusion), channel_id=1, source_target_pairs={{0,1},{1,0},{2,3},{3,2},{4,5},{5,4},{6,7},{7,6},{8,9},{9,8},{10,11... | collective-permute-start | bytes 1867784 | tf_op jit(solution)/shard_map/ppermute | solution.py:279
  18.5 5.2 %collective-permute-start.2 = (bf16[1,128,128]{2,1,0:T(8,128)(2,1)S(1)}, bf16[1,128,128]{2,1,0:T(8,128)(2,1)S(1)}, u32[]{:S(2)}, u32[]{:S(2)}) collective-permute-start(bf16[1,128,128]{2,1,0:T(8,128)(2,1)S(1)} %constant_dynamic-slice_fusion.1), channel_id=1, source_target_pairs={{1,4},{3,6},{4,1},{5,8},{6,3},{7,10},{8,5},{9,12},{10,7},{11,14},{... | collective-permute-start | bytes 98312 | tf_op jit(solution)/shard_map/ppermute | solution.py:279
  23.7 0.6 copy-start.6
  24.3 0.8 %copy-start.2 = (bf16[19,128,128]{2,1,0:T(8,128)(2,1)}, bf16[19,128,128]{2,1,0:T(8,128)(2,1)S(1)}, u32[]{:S(2)}) copy-start(bf16[19,128,128]{2,1,0:T(8,128)(2,1)S(1)} %collective-permute-done.3.from_sibling) | copy-start | bytes 1867780
  53.6 2.3 %collective-permute-start.4 = (bf16[19,128,128]{2,1,0:T(8,128)(2,1)}, bf16[19,128,128]{2,1,0:T(8,128)(2,1)S(1)}, u32[]{:S(2)}, u32[]{:S(2)}) collective-permute-start(bf16[19,128,128]{2,1,0:T(8,128)(2,1)} %get-tuple-element.34), channel_id=1, source_target_pairs={{0,1},{1,0},{2,3},{3,2},{4,5},{5,4},{6,7},{7,6},{8,9},{9,8},{10,11... | collective-permute-start | bytes 1867784 | tf_op jit(solution)/shard_map/ppermute | solution.py:279
  55.9 5.3 %copy-start.8 = (bf16[8,128,128]{2,1,0:T(8,128)(2,1)S(1)}, bf16[8,128,128]{2,1,0:T(8,128)(2,1)}, u32[]{:S(2)}) copy-start(bf16[8,128,128]{2,1,0:T(8,128)(2,1)} %get-tuple-element.39) | copy-start | bytes 786436
  55.9 22.0 %copy-start.4 = (f32[8,128,128]{2,1,0:T(8,128)S(1)}, f32[8,128,128]{2,1,0:T(8,128)}, u32[]{:S(2)}) copy-start(f32[8,128,128]{2,1,0:T(8,128)} %get-tuple-element.38) | copy-start | bytes 1572868
  57.1 20.8 %copy-start.3 = (f32[8,128,128]{2,1,0:T(8,128)S(1)}, f32[8,128,128]{2,1,0:T(8,128)}, u32[]{:S(2)}) copy-start(f32[8,128,128]{2,1,0:T(8,128)} %get-tuple-element.33) | copy-start | bytes 1572868
  57.1 0.8 %copy-start.9 = (bf16[1,128,128]{2,1,0:T(8,128)(2,1)S(1)}, bf16[1,128,128]{2,1,0:T(8,128)(2,1)}, u32[]{:S(2)}) copy-start(bf16[1,128,128]{2,1,0:T(8,128)(2,1)} %get-tuple-element.40) | copy-start | bytes 98308
  57.9 13.1 %collective-permute-start.7 = (bf16[1,128,128]{2,1,0:T(8,128)(2,1)S(1)}, bf16[1,128,128]{2,1,0:T(8,128)(2,1)S(1)}, u32[]{:S(2)}, u32[]{:S(2)}) collective-permute-start(bf16[1,128,128]{2,1,0:T(8,128)(2,1)S(1)} %copy-done.9), channel_id=1, source_target_pairs={{1,4},{3,6},{4,1},{5,8},{6,3},{7,10},{8,5},{9,12},{10,7},{11,14},{... | collective-permute-start | bytes 98312 | tf_op jit(solution)/shard_map/ppermute | solution.py:279
  61.2 16.7 %collective-permute-start.6 = (bf16[8,128,128]{2,1,0:T(8,128)(2,1)S(1)}, bf16[8,128,128]{2,1,0:T(8,128)(2,1)S(1)}, u32[]{:S(2)}, u32[]{:S(2)}) collective-permute-start(bf16[8,128,128]{2,1,0:T(8,128)(2,1)S(1)} %copy-done.8), channel_id=1, source_target_pairs={{1,3},{2,0},{3,5},{4,2},{5,7},{6,4},{7,9},{8,6},{9,11},{10,8},{11,... | collective-permute-start | bytes 786440 | tf_op jit(solution)/shard_map/ppermute | solution.py:279
  64.8 12.3 %collective-permute-start.8 = (bf16[1,128,128]{2,1,0:T(8,128)(2,1)S(1)}, bf16[1,128,128]{2,1,0:T(8,128)(2,1)S(1)}, u32[]{:S(2)}, u32[]{:S(2)}) collective-permute-start(bf16[1,128,128]{2,1,0:T(8,128)(2,1)S(1)} %get-tuple-element.41), channel_id=1, source_target_pairs={{1,3},{2,0},{3,5},{4,2},{5,7},{6,4},{7,9},{8,6},{9,11},{10,8},{11,... | collective-permute-start | bytes 98312 | tf_op jit(solution)/shard_map/ppermute | solution.py:279
  67.3 10.5 %collective-permute-start.5 = (bf16[9,128,128]{2,1,0:T(8,128)(2,1)S(1)}, bf16[9,128,128]{2,1,0:T(8,128)(2,1)S(1)}, u32[]{:S(2)}, u32[]{:S(2)}) collective-permute-start(bf16[9,128,128]{2,1,0:T(8,128)(2,1)S(1)} %pad_maximum_fusion.2), channel_id=1, source_target_pairs={{0,2},{2,4},{3,1},{4,6},{5,3},{6,8},{7,5},{8,10},{9,7},{10,12},{11... | collective-permute-start | bytes 884744 | tf_op jit(solution)/shard_map/ppermute | solution.py:279

commit v3 on v2

--- a/solution.py
+++ b/solution.py
@@ -19,7 +19,7 @@
 POOLED = PIX // 4 + PIX // 16 + PIX // 64
 PAD = 384
 CELLS = PIX + PAD
-LIMIT = 56
+LIMIT = 40
 WIN = 2 * RADIUS * TR + TR + 2
 
 NN = (((1,), (0,)), ((), ()))
@@ -42,6 +42,7 @@
         ahead=keep((i, i + 2 * side[i]) for i in range(count)),
         behind=keep((i, i - 2 * side[i]) for i in range(count)),
         far=keep((i, i - 3 * side[i]) for i in range(count)),
+        cross=keep((i, i - side[i]) for i in range(count)),
     )
 
 
@@ -107,12 +108,7 @@
     return jnp.where(cell >= offset, fill, result)
 
 
-def tables_kernel(weight, weight_back, pool, unpool):
-    for a in range(3):
-        for b in range(3):
-            weight_back[a * CIN : (a + 1) * CIN, b * CH : (b + 1) * CH] = weight[
-                (3 * a + b) * CIN : (3 * a + b + 1) * CIN, :
-            ]
+def tables_kernel(pool, unpool):
     pool[...] = pool_matrix((PAD, PIX), 0, [1.0] * LEVELS)
     unpool[...] = pool_matrix((PIX, PAD), 1, [2.0**-level for level in range(LEVELS)])
 
@@ -124,18 +120,26 @@
     near,
     direct,
     far,
+    cross,
     from_sibling,
     weight,
-    weight_back,
     pool,
     unpool,
     labels,
+    to_sibling_hbm,
+    ahead_hbm,
+    behind_hbm,
+    far_hbm,
+    sum_one_hbm,
+    sum_two_hbm,
     to_sibling,
     ahead,
     behind,
     far_out,
     sum_one,
     sum_two,
+    sems,
+    weight_back,
     window,
     spread_two,
     window_one,
@@ -165,10 +169,16 @@
         window[at(side) + r] = from_sibling[r]
         window[at(-side) + r] = from_sibling[TR + r]
         window_one[1 + r] = own_one[r]
-    window[edge(side)] = from_sibling[2 * TR + 2]
+    window[edge(side)] = from_sibling[2 * TR + 1]
     window[edge(-side)] = far[0]
-    window_one[jnp.where(side > 0, TR + 1, 0)] = from_sibling[2 * TR + 1]
-    window_one[jnp.where(side > 0, 0, TR + 1)] = from_sibling[2 * TR]
+    window_one[jnp.where(side > 0, TR + 1, 0)] = from_sibling[2 * TR]
+    window_one[jnp.where(side > 0, 0, TR + 1)] = cross[0]
+
+    for a in range(3):
+        for b in range(3):
+            weight_back[a * CIN : (a + 1) * CIN, b * CH : (b + 1) * CH] = weight[
+                (3 * a + b) * CIN : (3 * a + b + 1) * CIN, :
+            ]
 
     def spread(r, carry):
         spread_columns(window, r, spread_two, r)
@@ -220,37 +230,50 @@
         return carry
 
     lax.fori_loop(0, SLOTS, slot, 0)
-    convolve_back(grad_rows[...], weight_back, moved, total_one, 0)
 
     def rows(total, row, size=1):
         return total[pl.ds(pl.multiple_of(row * TC, TC), size * TC), :].reshape(size, TC, CIN)
 
+    def out(n, block, target):
+        return pltpu.make_async_copy(block, target, sems.at[n])
+
+    behind[...] = rows(total_two, at(-2 * side), TR).astype(jnp.bfloat16)
+    out(0, behind, behind_hbm).start()
+    far_out[...] = rows(total_two, edge(-side)).astype(jnp.bfloat16)
+    out(1, far_out, far_hbm).start()
+    ahead[...] = rows(total_two, at(2 * side), TR)
+    out(2, ahead, ahead_hbm).start()
+    sum_two[...] = rows(total_two, at(0), TR)
+    out(3, sum_two, sum_two_hbm).start()
     to_sibling[0:TR] = rows(total_two, at(side), TR).astype(jnp.bfloat16)
     to_sibling[TR : 2 * TR] = rows(total_two, at(-side), TR).astype(jnp.bfloat16)
     to_sibling[2 * TR : 2 * TR + 1] = rows(total_two, edge(side)).astype(jnp.bfloat16)
-    to_sibling[2 * TR + 1 : 2 * TR + 2] = rows(
-        total_one, jnp.where(side > 0, TR + 1, 0)
-    ).astype(jnp.bfloat16)
-    to_sibling[2 * TR + 2 : 2 * TR + 3] = rows(
-        total_one, jnp.where(side > 0, 0, TR + 1)
-    ).astype(jnp.bfloat16)
-    ahead[...] = rows(total_two, at(2 * side), TR)
-    behind[...] = rows(total_two, at(-2 * side), TR).astype(jnp.bfloat16)
-    far_out[...] = rows(total_two, edge(-side)).astype(jnp.bfloat16)
-    sum_two[...] = rows(total_two, at(0), TR)
+    convolve_back(grad_rows[...], weight_back, moved, total_one, 0)
+    facing = jnp.where(side > 0, TR + 1, 0)
+    outer = jnp.where(side > 0, 0, TR + 1)
+    to_sibling[2 * TR + 1 : 2 * TR + 2] = rows(total_one, facing).astype(jnp.bfloat16)
+    to_sibling[2 * TR + 2 : 2 * TR + 3] = rows(total_one, outer).astype(jnp.bfloat16)
+    out(4, to_sibling, to_sibling_hbm).start()
     sum_one[...] = rows(total_one, 1, TR)
-
-
-def call(kernel, outs, scratch, args, name, scalars=1, limit=LIMIT):
+    out(5, sum_one, sum_one_hbm).start()
+    out(0, behind, behind_hbm).wait()
+    out(1, far_out, far_hbm).wait()
+    out(2, ahead, ahead_hbm).wait()
+    out(3, sum_two, sum_two_hbm).wait()
+    out(4, to_sibling, to_sibling_hbm).wait()
+    out(5, sum_one, sum_one_hbm).wait()
+
+
+def call(kernel, outs, scratch, args, name, scalars, space):
     smem = pl.BlockSpec(memory_space=pltpu.SMEM)
     vmem = pl.BlockSpec(memory_space=pltpu.VMEM)
     return pl.pallas_call(
         kernel,
         in_specs=[smem] * scalars + [vmem] * (len(args) - scalars),
-        out_specs=[vmem] * len(outs),
+        out_specs=[pl.BlockSpec(memory_space=space)] * len(outs),
         out_shape=[jax.ShapeDtypeStruct(*out) for out in outs],
-        scratch_shapes=[pltpu.VMEM(*item) for item in scratch],
-        compiler_params=pltpu.CompilerParams(vmem_limit_bytes=limit << 20),
+        scratch_shapes=scratch,
+        compiler_params=pltpu.CompilerParams(vmem_limit_bytes=LIMIT << 20),
         name=name,
     )(*args)
 
@@ -286,56 +309,70 @@
     ).astype(jnp.int32)
     labels = label_rows(targets)
     weight = conv_weight.reshape(9 * CIN, CH)
+    near = send(frame_two, "behind")
     direct = send(frame_two, "ahead")
-    near_in = jnp.concatenate([frame_two, row_of(frame_one, side > 0)])
-    near = send(near_in, "behind")
     tables = call(
         tables_kernel,
-        [((3 * CIN, 3 * CH), bf16), ((PAD, PIX), bf16), ((PIX, PAD), bf16)],
+        [((PAD, PIX), bf16), ((PIX, PAD), bf16)],
         [],
-        [weight],
+        [],
         "tables",
-        scalars=0,
+        0,
+        pltpu.VMEM,
     )
+    rims = row_of(frame_two, side > 0), row_of(frame_one, side > 0)
+    tables, labels, plan, rims = lax.optimization_barrier((tables, labels, plan, rims))
+    far = send(rims[0], "far")
+    cross = send(rims[1], "cross")
     inward = row_of(frame_one, side < 0)
-    far_in, direct = lax.optimization_barrier((row_of(frame_two, side > 0), direct))
-    far = send(far_in, "far")
+    inward, far, cross = lax.optimization_barrier((inward, far, cross))
     payload = jnp.concatenate([frame_two, near, inward, row_of(direct, side < 0)])
-    payload, tables, labels, plan = lax.optimization_barrier((payload, tables, labels, plan))
     from_sibling = send(payload, "swap")
 
     tile = (TR, TC, CIN)
     pack = (2 * TR + 3, TC, CIN)
+    outs = [
+        (pack, bf16),
+        (tile, f32),
+        (tile, bf16),
+        ((1, TC, CIN), bf16),
+        (tile, f32),
+        (tile, f32),
+    ]
+    scratch = [
+        ((3 * CIN, 3 * CH), bf16),
+        ((WIN, TC, CIN), bf16),
+        ((WIN * TC, 3 * CIN), bf16),
+        ((TR + 2, TC, CIN), bf16),
+        (((TR + 2) * TC, 3 * CIN), bf16),
+        ((PIX, CH), bf16),
+        ((CELLS, CH), bf16),
+        ((CELLS, PIX), bf16),
+        ((CELLS, CH), f32),
+        ((PIX, CH), f32),
+        ((PIX, 3 * CH), bf16),
+        ((WIN * TC, CIN), f32),
+        (((TR + 2) * TC, CIN), f32),
+    ]
     to_sibling, ahead, behind, far_out, sum_one, sum_two = call(
         work_kernel,
-        [(pack, bf16), (tile, f32), (tile, bf16), ((1, TC, CIN), bf16), (tile, f32), (tile, f32)],
-        [
-            ((WIN, TC, CIN), bf16),
-            ((WIN * TC, 3 * CIN), bf16),
-            ((TR + 2, TC, CIN), bf16),
-            (((TR + 2) * TC, 3 * CIN), bf16),
-            ((PIX, CH), bf16),
-            ((CELLS, CH), bf16),
-            ((CELLS, PIX), bf16),
-            ((CELLS, CH), f32),
-            ((PIX, CH), f32),
-            ((PIX, 3 * CH), bf16),
-            ((WIN * TC, CIN), f32),
-            (((TR + 2) * TC, CIN), f32),
-        ],
-        [plan, frame_one, frame_two, near, direct, far, from_sibling, weight, *tables, labels],
+        outs,
+        [pltpu.VMEM(*out) for out in outs]
+        + [pltpu.SemaphoreType.DMA((len(outs),))]
+        + [pltpu.VMEM(*item) for item in scratch],
+        [plan, frame_one, frame_two, near, direct, far, cross]
+        + [from_sibling, weight, *tables, labels],
         "work",
+        1,
+        pltpu.HBM,
     )
     back_behind = send(behind, "behind")
     back_sibling = send(to_sibling, "swap")
     joined = (ahead + back_sibling[TR : 2 * TR].astype(f32)).astype(bf16)
     ahead_in = jnp.concatenate([joined, back_sibling[2 * TR + 2 :]])
-    far_out, edge, ahead_in = lax.optimization_barrier(
-        (far_out, back_sibling[2 * TR : 2 * TR + 1], ahead_in)
-    )
     back_ahead = send(ahead_in, "ahead")
     back_far = send(far_out, "far")
-    back_edge = send(edge, "behind")
+    back_edge = send(back_sibling[2 * TR : 2 * TR + 1], "behind")
 
     row = lax.broadcasted_iota(jnp.int32, (TR, 1, 1), 0)
     facing = row == jnp.where(side > 0, TR - 1, 0)

time: 80.3 us -> 74 us (0.922)
  Pallas kernels: 31.5 us -> 22.1 us
  starting transfers between devices: 22 us -> 31 us
  waiting for transfers between devices: 14.9 us -> 11.2 us
  local copies, waits for them, and re-layouts: 4.94 us -> 3.15 us
    pallas_call x2, Pallas kernels: 31.5 us -> 22.1 us  [call(): pl.pallas_call(kernel, in_specs=[smem] * scalars + [vmem] * (len(args) -...]
    ppermute x9 -> x10, starting transfers between devices: 22 us -> 31 us  [send(): return lax.ppermute(block, 'tile', route[name])]
    ppermute x9 -> x10, waiting for transfers between devices: 14.9 us -> 11.2 us  [send(): return lax.ppermute(block, 'tile', route[name])]
    unnamed x22 -> x10, local copies, waits for them, and re-layouts: 3.47 us -> 1.52 us
    concatenate x1 -> x0, other arithmetic: 0.99 us -> none  [on_device(): near_in = jnp.concatenate([frame_two, row_of(frame_one, side > 0)])]
  transfers between devices with their start and end apart: 9 -> 10, of which waited for: 5 -> 4; matrix products, arithmetic and copies ran while one was open for 4% -> 6% of each run, Pallas kernels for 4% -> 1%
where the time goes in v3:
time: 74 us; the launch traced here: 72.9 us
  starting transfers between devices  31 us (42%)
  Pallas kernels  22.1 us (30%)
  waiting for transfers between devices  11.2 us (15%)
  other arithmetic  3.88 us (5%)
  local copies, waits for them, and re-layouts  3.15 us (4%)
  between operations  1.53 us (2%)
    ppermute x10, starting transfers between devices, send(): return lax.ppermute(block, 'tile', route[name])  31 us
    pallas_call x2, Pallas kernels, call(): pl.pallas_call(kernel, in_specs=[smem] * scalars + [vmem] * (len(args) -...  22.1 us
    ppermute x10, waiting for transfers between devices, send(): return lax.ppermute(block, 'tile', route[name])  11.2 us
    dynamic_slice x3, local copies, waits for them, and re-layouts, row_of(): return lax.dynamic_slice_in_dim(frame, jnp.where(first, 0, TR - 1), 1, 0)  1.56 us
    unnamed x10, local copies, waits for them, and re-layouts  1.52 us
  transfers between devices with their start and end apart: 10, of which 4 were waited for; matrix products, arithmetic and copies ran while one was open for 6% of the time, Pallas kernels for 1%

profile of v3, /device:TPU:9, one launch (start us, length us, event | category | flops | bytes accessed | tf_op | source)
XLA Modules:
  0.0 72.9 jit_solution(7895657766285466031)
XLA Ops:
  0.6 3.2 %collective-permute-start.1 = (bf16[8,128,128]{2,1,0:T(8,128)(2,1)}, bf16[8,128,128]{2,1,0:T(8,128)(2,1)S(1)}, u32[]{:S(2)}, u32[]{:S(2)}) collective-permute-start(bf16[8,128,128]{2,1,0:T(8,128)(2,1)} %own_two.1), channel_id=1, source_target_pairs={{0,2},{2,4},{3,1},{4,6},{5,3},{6,8},{7,5},{8,10},{9,7},{10,12},{11... | collective-permute-start | bytes 786440 | tf_op jit(solution)/shard_map/ppermute | solution.py:302
  3.8 2.3 %collective-permute-start = (bf16[8,128,128]{2,1,0:T(8,128)(2,1)}, bf16[8,128,128]{2,1,0:T(8,128)(2,1)S(1)}, u32[]{:S(2)}, u32[]{:S(2)}) collective-permute-start(bf16[8,128,128]{2,1,0:T(8,128)(2,1)} %own_two.1), channel_id=1, source_target_pairs={{1,3},{2,0},{3,5},{4,2},{5,7},{6,4},{7,9},{8,6},{9,11},{10,8},{11,... | collective-permute-start | bytes 786440 | tf_op jit(solution)/shard_map/ppermute | solution.py:302
  6.1 0.7 subtract_bitcast_fusion
  6.7 0.7 and_select_fusion
  7.5 0.8 %constant_dynamic-slice_fusion.3 = bf16[1,128,128]{2,1,0:T(8,128)(2,1)S(1)} fusion(bf16[8,128,128]{2,1,0:T(8,128)(2,1)} %own_two.1, s32[]{:T(128)S(6)} %select_n.124), kind=kLoop, calls=%fused_computation.28 | loop fusion | bytes 65540 | tf_op jit(solution)/shard_map/dynamic_slice | solution.py:305
  9.1 1.0 %tables.1 = (bf16[384,1024]{1,0:T(8,128)(2,1)S(1)}, bf16[1024,384]{1,0:T(8,128)(2,1)S(1)}) custom-call(), custom_call_target="tpu_custom_call" | custom-call | tf_op jit(solution)/shard_map/tables/pallas_call | solution.py:270
  10.1 0.8 %constant_dynamic-slice_fusion.1 = (bf16[1,128,128]{2,1,0:T(8,128)(2,1)S(1)}, bf16[1,128,128]{2,1,0:T(8,128)(2,1)S(1)}) fusion(bf16[8,128,128]{2,1,0:T(8,128)(2,1)} %own_one.1, s32[]{:T(128)S(6)} %select_n.125, s32[]{:T(128)S(6)} %select_n.124), kind=kLoop, calls=%fused_computation.26 | loop fusion | bytes 131080 | tf_op jit(solution)/shard_map/dynamic_slice | solution.py:305
  10.9 5.2 %collective-permute-start.2 = (bf16[1,128,128]{2,1,0:T(8,128)(2,1)S(1)}, bf16[1,128,128]{2,1,0:T(8,128)(2,1)S(1)}, u32[]{:S(2)}, u32[]{:S(2)}) collective-permute-start(bf16[1,128,128]{2,1,0:T(8,128)(2,1)S(1)} %constant_dynamic-slice_fusion.3), channel_id=1, source_target_pairs={{1,4},{3,6},{4,1},{5,8},{6,3},{7,10},{8,5},{9,12},{10,7},{11,14},{... | collective-permute-start | bytes 98312 | tf_op jit(solution)/shard_map/ppermute | solution.py:302
  16.1 1.9 %collective-permute-start.3 = (bf16[1,128,128]{2,1,0:T(8,128)(2,1)S(1)}, bf16[1,128,128]{2,1,0:T(8,128)(2,1)S(1)}, u32[]{:S(2)}, u32[]{:S(2)}) collective-permute-start(bf16[1,128,128]{2,1,0:T(8,128)(2,1)S(1)} %get-tuple-element.23), channel_id=1, source_target_pairs={{1,2},{2,1},{3,4},{4,3},{5,6},{6,5},{7,8},{8,7},{9,10},{10,9},{11,... | collective-permute-start | bytes 98312 | tf_op jit(solution)/shard_map/ppermute | solution.py:302
  18.1 3.3 %collective-permute-done.3.cross = bf16[1,128,128]{2,1,0:T(8,128)(2,1)S(1)} collective-permute-done((bf16[1,128,128]{2,1,0:T(8,128)(2,1)S(1)}, bf16[1,128,128]{2,1,0:T(8,128)(2,1)S(1)}, u32[]{:S(2)}, u32[]{:S(2)}) %collective-permute-start.3) | collective-permute-done | bytes 32800 | tf_op jit(solution)/shard_map/ppermute | solution.py:302
  21.4 0.1 pad_maximum_fusion
  21.6 2.0 %collective-permute-done.4.from_sibling = bf16[18,128,128]{2,1,0:T(8,128)(2,1)S(1)} collective-permute-done((bf16[18,128,128]{2,1,0:T(8,128)(2,1)S(1)}, bf16[18,128,128]{2,1,0:T(8,128)(2,1)S(1)}, u32[]{:S(2)}, u32[]{:S(2)}) %collective-permute-start.4) | collective-permute-done | bytes 589856 | tf_op jit(solution)/shard_map/ppermute | solution.py:302
  23.6 21.1 %work.1 = (bf16[19,128,128]{2,1,0:T(8,128)(2,1)}, f32[8,128,128]{2,1,0:T(8,128)S(1)}, bf16[8,128,128]{2,1,0:T(8,128)(2,1)S(1)}, bf16[1,128,128]{2,1,0:T(8,128)(2...) custom-call(s32[8]{0:T(128)S(1)} %pad_add_fusion.plan, bf16[8,128,128]{2,1,0:T(8,128)(2,1)S(1)} %copy-done.3, ...), custom_call_target="tpu_custom_call" | custom-call | tf_op jit(solution)/shard_map/work/pallas_call | solution.py:270
  44.7 0.8 %copy-done.2 = f32[8,128,128]{2,1,0:T(8,128)} copy-done((f32[8,128,128]{2,1,0:T(8,128)}, f32[8,128,128]{2,1,0:T(8,128)S(1)}, u32[]{:S(2)}) %copy-start.2) | copy-done | bytes 524312
  45.5 0.7 copy-done.4
  46.2 0.1 collective-permute-start.5
  46.4 8.9 %collective-permute-start.8 = (bf16[1,128,128]{2,1,0:T(8,128)(2,1)S(1)}, bf16[1,128,128]{2,1,0:T(8,128)(2,1)S(1)}, u32[]{:S(2)}, u32[]{:S(2)}) collective-permute-start(bf16[1,128,128]{2,1,0:T(8,128)(2,1)S(1)} %get-tuple-element.35), channel_id=1, source_target_pairs={{1,4},{3,6},{4,1},{5,8},{6,3},{7,10},{8,5},{9,12},{10,7},{11,14},{... | collective-permute-start | bytes 98312 | tf_op jit(solution)/shard_map/ppermute | solution.py:302
  55.3 3.2 %collective-permute-start.7 = (bf16[8,128,128]{2,1,0:T(8,128)(2,1)}, bf16[8,128,128]{2,1,0:T(8,128)(2,1)S(1)}, u32[]{:S(2)}, u32[]{:S(2)}) collective-permute-start(bf16[8,128,128]{2,1,0:T(8,128)(2,1)} %copy-done.4), channel_id=1, source_target_pairs={{1,3},{2,0},{3,5},{4,2},{5,7},{6,4},{7,9},{8,6},{9,11},{10,8},{11,... | collective-permute-start | bytes 786440 | tf_op jit(solution)/shard_map/ppermute | solution.py:302
  58.5 1.9 %collective-permute-start.9 = (bf16[1,128,128]{2,1,0:T(8,128)(2,1)S(1)}, bf16[1,128,128]{2,1,0:T(8,128)(2,1)S(1)}, u32[]{:S(2)}, u32[]{:S(2)}) collective-permute-start(bf16[1,128,128]{2,1,0:T(8,128)(2,1)S(1)} %get-tuple-element.41), channel_id=1, source_target_pairs={{1,3},{2,0},{3,5},{4,2},{5,7},{6,4},{7,9},{8,6},{9,11},{10,8},{11,... | collective-permute-start | bytes 98312 | tf_op jit(solution)/shard_map/ppermute | solution.py:302
  60.4 1.1 %add_convert_fusion.2 = bf16[8,128,128]{2,1,0:T(8,128)(2,1)S(1)} fusion(f32[8,128,128]{2,1,0:T(8,128)} %copy-done.2, bf16[19,128,128]{2,1,0:T(8,128)(2,1)S(1)} %collective-permute-done.5), kind=kLoop, calls=%fused_computation.3 | loop fusion | flops 393216 | bytes 1048576 | tf_op jit(solution)/shard_map/convert_element_type | solution.py:371
  61.5 4.3 %collective-permute-start.6 = (bf16[9,128,128]{2,1,0:T(8,128)(2,1)S(1)}, bf16[9,128,128]{2,1,0:T(8,128)(2,1)S(1)}, u32[]{:S(2)}, u32[]{:S(2)}) collective-permute-start(bf16[9,128,128]{2,1,0:T(8,128)(2,1)S(1)} %pad_maximum_fusion.1), channel_id=1, source_target_pairs={{0,2},{2,4},{3,1},{4,6},{5,3},{6,8},{7,5},{8,10},{9,7},{10,12},{11... | collective-permute-start | bytes 884744 | tf_op jit(solution)/shard_map/ppermute | solution.py:302
  65.8 4.3 %collective-permute-done.9 = bf16[1,128,128]{2,1,0:T(8,128)(2,1)S(1)} collective-permute-done((bf16[1,128,128]{2,1,0:T(8,128)(2,1)S(1)}, bf16[1,128,128]{2,1,0:T(8,128)(2,1)S(1)}, u32[]{:S(2)}, u32[]{:S(2)}) %collective-permute-start.9) | collective-permute-done | bytes 32800 | tf_op jit(solution)/shard_map/ppermute | solution.py:302
  70.1 1.6 %collective-permute-done.6 = bf16[9,128,128]{2,1,0:T(8,128)(2,1)S(1)} collective-permute-done((bf16[9,128,128]{2,1,0:T(8,128)(2,1)S(1)}, bf16[9,128,128]{2,1,0:T(8,128)(2,1)S(1)}, u32[]{:S(2)}, u32[]{:S(2)}) %collective-permute-start.6) | collective-permute-done | bytes 294944 | tf_op jit(solution)/shard_map/ppermute | solution.py:302
  71.8 1.1 %add_convert_fusion = (bf16[8,128,128]{2,1,0:T(8,128)(2,1)}, bf16[8,128,128]{2,1,0:T(8,128)(2,1)}) fusion(bf16[8,128,128]{2,1,0:T(8,128)(2,1)S(1)} %collective-permute-done.7, f32[8,128,128]{2,1,0:T(8,128)S(1)} %get-tuple-element.33, bf16[9,128,128]{2,1,0:T(8,128)(2,1)S(1)} %collective-permute-done.6, bf16[19,128,128]{2,1,0:T(8,128)(2,1)S(1)} %collective-permute-done.5, ...), kind=kLoop, calls=%fused_computation.1 | loop fusion | flops 2097152 | bytes 2621456 | tf_op jit(solution)/shard_map/convert_element_type | solution.py:389
  (27 shorter events, 0.4 us)
Async XLA Ops:
  0.6 20.8 %copy-start = (bf16[8,128,128]{2,1,0:T(8,128)(2,1)S(1)}, bf16[8,128,128]{2,1,0:T(8,128)(2,1)}, u32[]{:S(2)}) copy-start(bf16[8,128,128]{2,1,0:T(8,128)(2,1)} %own_two.1) | copy-start | bytes 786436
  0.6 20.7 %collective-permute-start.1 = (bf16[8,128,128]{2,1,0:T(8,128)(2,1)}, bf16[8,128,128]{2,1,0:T(8,128)(2,1)S(1)}, u32[]{:S(2)}, u32[]{:S(2)}) collective-permute-start(bf16[8,128,128]{2,1,0:T(8,128)(2,1)} %own_two.1), channel_id=1, source_target_pairs={{0,2},{2,4},{3,1},{4,6},{5,3},{6,8},{7,5},{8,10},{9,7},{10,12},{11... | collective-permute-start | bytes 786440 | tf_op jit(solution)/shard_map/ppermute | solution.py:302
  3.8 17.6 %collective-permute-start = (bf16[8,128,128]{2,1,0:T(8,128)(2,1)}, bf16[8,128,128]{2,1,0:T(8,128)(2,1)S(1)}, u32[]{:S(2)}, u32[]{:S(2)}) collective-permute-start(bf16[8,128,128]{2,1,0:T(8,128)(2,1)} %own_two.1), channel_id=1, source_target_pairs={{1,3},{2,0},{3,5},{4,2},{5,7},{6,4},{7,9},{8,6},{9,11},{10,8},{11,... | collective-permute-start | bytes 786440 | tf_op jit(solution)/shard_map/ppermute | solution.py:302
  10.9 7.2 %collective-permute-start.2 = (bf16[1,128,128]{2,1,0:T(8,128)(2,1)S(1)}, bf16[1,128,128]{2,1,0:T(8,128)(2,1)S(1)}, u32[]{:S(2)}, u32[]{:S(2)}) collective-permute-start(bf16[1,128,128]{2,1,0:T(8,128)(2,1)S(1)} %constant_dynamic-slice_fusion.3), channel_id=1, source_target_pairs={{1,4},{3,6},{4,1},{5,8},{6,3},{7,10},{8,5},{9,12},{10,7},{11,14},{... | collective-permute-start | bytes 98312 | tf_op jit(solution)/shard_map/ppermute | solution.py:302
  16.1 5.2 %collective-permute-start.3 = (bf16[1,128,128]{2,1,0:T(8,128)(2,1)S(1)}, bf16[1,128,128]{2,1,0:T(8,128)(2,1)S(1)}, u32[]{:S(2)}, u32[]{:S(2)}) collective-permute-start(bf16[1,128,128]{2,1,0:T(8,128)(2,1)S(1)} %get-tuple-element.23), channel_id=1, source_target_pairs={{1,2},{2,1},{3,4},{4,3},{5,6},{6,5},{7,8},{8,7},{9,10},{10,9},{11,... | collective-permute-start | bytes 98312 | tf_op jit(solution)/shard_map/ppermute | solution.py:302
  21.4 2.2 %copy-start.1 = (bf16[3,3,128,256]{3,2,1,0:T(8,128)(2,1)S(1)}, bf16[3,3,128,256]{3,2,1,0:T(8,128)(2,1)}, u32[]{:S(2)}) copy-start(bf16[3,3,128,256]{3,2,1,0:T(8,128)(2,1)} %param.8) | copy-start | bytes 1769476
  21.4 2.2 %copy-start.3 = (bf16[8,128,128]{2,1,0:T(8,128)(2,1)S(1)}, bf16[8,128,128]{2,1,0:T(8,128)(2,1)}, u32[]{:S(2)}) copy-start(bf16[8,128,128]{2,1,0:T(8,128)(2,1)} %own_one.1) | copy-start | bytes 786436
  21.5 2.1 %collective-permute-start.4 = (bf16[18,128,128]{2,1,0:T(8,128)(2,1)S(1)}, bf16[18,128,128]{2,1,0:T(8,128)(2,1)S(1)}, u32[]{:S(2)}, u32[]{:S(2)}) collective-permute-start(bf16[18,128,128]{2,1,0:T(8,128)(2,1)S(1)} %pad_maximum_fusion), channel_id=1, source_target_pairs={{0,1},{1,0},{2,3},{3,2},{4,5},{5,4},{6,7},{7,6},{8,9},{9,8},{10,11... | collective-permute-start | bytes 1769480 | tf_op jit(solution)/shard_map/ppermute | solution.py:302
  44.7 0.8 %copy-start.2 = (f32[8,128,128]{2,1,0:T(8,128)}, f32[8,128,128]{2,1,0:T(8,128)S(1)}, u32[]{:S(2)}) copy-start(f32[8,128,128]{2,1,0:T(8,128)S(1)} %get-tuple-element.32) | copy-start | bytes 1572868
  45.5 0.7 copy-start.4
  46.2 12.2 %collective-permute-start.5 = (bf16[19,128,128]{2,1,0:T(8,128)(2,1)}, bf16[19,128,128]{2,1,0:T(8,128)(2,1)S(1)}, u32[]{:S(2)}, u32[]{:S(2)}) collective-permute-start(bf16[19,128,128]{2,1,0:T(8,128)(2,1)} %get-tuple-element.31), channel_id=1, source_target_pairs={{0,1},{1,0},{2,3},{3,2},{4,5},{5,4},{6,7},{7,6},{8,9},{9,8},{10,11... | collective-permute-start | bytes 1867784 | tf_op jit(solution)/shard_map/ppermute | solution.py:302
  46.4 19.4 %collective-permute-start.8 = (bf16[1,128,128]{2,1,0:T(8,128)(2,1)S(1)}, bf16[1,128,128]{2,1,0:T(8,128)(2,1)S(1)}, u32[]{:S(2)}, u32[]{:S(2)}) collective-permute-start(bf16[1,128,128]{2,1,0:T(8,128)(2,1)S(1)} %get-tuple-element.35), channel_id=1, source_target_pairs={{1,4},{3,6},{4,1},{5,8},{6,3},{7,10},{8,5},{9,12},{10,7},{11,14},{... | collective-permute-start | bytes 98312 | tf_op jit(solution)/shard_map/ppermute | solution.py:302
  55.3 16.5 %collective-permute-start.7 = (bf16[8,128,128]{2,1,0:T(8,128)(2,1)}, bf16[8,128,128]{2,1,0:T(8,128)(2,1)S(1)}, u32[]{:S(2)}, u32[]{:S(2)}) collective-permute-start(bf16[8,128,128]{2,1,0:T(8,128)(2,1)} %copy-done.4), channel_id=1, source_target_pairs={{1,3},{2,0},{3,5},{4,2},{5,7},{6,4},{7,9},{8,6},{9,11},{10,8},{11,... | collective-permute-start | bytes 786440 | tf_op jit(solution)/shard_map/ppermute | solution.py:302
  58.5 11.7 %collective-permute-start.9 = (bf16[1,128,128]{2,1,0:T(8,128)(2,1)S(1)}, bf16[1,128,128]{2,1,0:T(8,128)(2,1)S(1)}, u32[]{:S(2)}, u32[]{:S(2)}) collective-permute-start(bf16[1,128,128]{2,1,0:T(8,128)(2,1)S(1)} %get-tuple-element.41), channel_id=1, source_target_pairs={{1,3},{2,0},{3,5},{4,2},{5,7},{6,4},{7,9},{8,6},{9,11},{10,8},{11,... | collective-permute-start | bytes 98312 | tf_op jit(solution)/shard_map/ppermute | solution.py:302
  61.5 10.2 %collective-permute-start.6 = (bf16[9,128,128]{2,1,0:T(8,128)(2,1)S(1)}, bf16[9,128,128]{2,1,0:T(8,128)(2,1)S(1)}, u32[]{:S(2)}, u32[]{:S(2)}) collective-permute-start(bf16[9,128,128]{2,1,0:T(8,128)(2,1)S(1)} %pad_maximum_fusion.1), channel_id=1, source_target_pairs={{0,2},{2,4},{3,1},{4,6},{5,3},{6,8},{7,5},{8,10},{9,7},{10,12},{11... | collective-permute-start | bytes 884744 | tf_op jit(solution)/shard_map/ppermute | solution.py:302

commit v4 on v3

--- a/solution.py
+++ b/solution.py
@@ -19,7 +19,7 @@
 POOLED = PIX // 4 + PIX // 16 + PIX // 64
 PAD = 384
 CELLS = PIX + PAD
-LIMIT = 40
+LIMIT = 48
 WIN = 2 * RADIUS * TR + TR + 2
 
 NN = (((1,), (0,)), ((), ()))
@@ -237,7 +237,7 @@
     def out(n, block, target):
         return pltpu.make_async_copy(block, target, sems.at[n])
 
-    behind[...] = rows(total_two, at(-2 * side), TR).astype(jnp.bfloat16)
+    behind[...] = rows(total_two, at(-2 * side), TR)
     out(0, behind, behind_hbm).start()
     far_out[...] = rows(total_two, edge(-side)).astype(jnp.bfloat16)
     out(1, far_out, far_hbm).start()
@@ -320,12 +320,12 @@
         0,
         pltpu.VMEM,
     )
-    rims = row_of(frame_two, side > 0), row_of(frame_one, side > 0)
-    tables, labels, plan, rims = lax.optimization_barrier((tables, labels, plan, rims))
-    far = send(rims[0], "far")
-    cross = send(rims[1], "cross")
+    far = send(row_of(frame_two, side > 0), "far")
+    cross = send(row_of(frame_one, side > 0), "cross")
     inward = row_of(frame_one, side < 0)
-    inward, far, cross = lax.optimization_barrier((inward, far, cross))
+    inward, far, cross, tables, labels, plan = lax.optimization_barrier(
+        (inward, far, cross, tables, labels, plan)
+    )
     payload = jnp.concatenate([frame_two, near, inward, row_of(direct, side < 0)])
     from_sibling = send(payload, "swap")
 
@@ -334,7 +334,7 @@
     outs = [
         (pack, bf16),
         (tile, f32),
-        (tile, bf16),
+        (tile, f32),
         ((1, TC, CIN), bf16),
         (tile, f32),
         (tile, f32),
@@ -366,17 +366,16 @@
         1,
         pltpu.HBM,
     )
-    back_behind = send(behind, "behind")
-    back_sibling = send(to_sibling, "swap")
-    joined = (ahead + back_sibling[TR : 2 * TR].astype(f32)).astype(bf16)
-    ahead_in = jnp.concatenate([joined, back_sibling[2 * TR + 2 :]])
-    back_ahead = send(ahead_in, "ahead")
-    back_far = send(far_out, "far")
-    back_edge = send(back_sibling[2 * TR : 2 * TR + 1], "behind")
-
     row = lax.broadcasted_iota(jnp.int32, (TR, 1, 1), 0)
     facing = row == jnp.where(side > 0, TR - 1, 0)
     outer = row == jnp.where(side > 0, 0, TR - 1)
+    back_sibling = send(to_sibling, "swap")
+    ahead_in = (ahead + back_sibling[TR : 2 * TR].astype(f32)).astype(bf16)
+    edge = jnp.where(facing, back_sibling[2 * TR : 2 * TR + 1].astype(f32), 0.0)
+    behind_in = (behind + edge).astype(bf16)
+    back_ahead = send(jnp.concatenate([ahead_in, back_sibling[2 * TR + 2 :]]), "ahead")
+    back_behind = send(behind_in, "behind")
+    back_far = send(far_out, "far")
 
     def place(where, block):
         return jnp.where(where, block.astype(f32), 0.0)
@@ -385,7 +384,7 @@
     grad_one = grad_one + place(outer, back_ahead[TR:])
     grad_two = sum_two + back_sibling[:TR].astype(f32) + back_ahead[:TR].astype(f32)
     grad_two = grad_two + back_behind.astype(f32)
-    grad_two = grad_two + place(outer, back_far) + place(facing, back_edge)
+    grad_two = grad_two + place(outer, back_far)
     return grad_one.astype(bf16), grad_two.astype(bf16)
 
 

time: 74 us -> 71.8 us (0.970)
  starting transfers between devices: 31 us -> 22 us
  Pallas kernels: 22.1 us -> 28.2 us
  other arithmetic: 3.88 us -> 2.28 us
  local copies, waits for them, and re-layouts: 3.15 us -> 4.65 us
  waiting for transfers between devices: 11.2 us -> 12.6 us
    ppermute x10 -> x9, starting transfers between devices: 31 us -> 22 us  [send(): return lax.ppermute(block, 'tile', route[name])]
    pallas_call x2, Pallas kernels: 22.1 us -> 28.2 us  [call(): pl.pallas_call(kernel, in_specs=[smem] * scalars + [vmem] * (len(args) -...]
    unnamed x10 -> x14, local copies, waits for them, and re-layouts: 1.52 us -> 2.99 us
    ppermute x10 -> x9, waiting for transfers between devices: 11.2 us -> 12.6 us  [send(): return lax.ppermute(block, 'tile', route[name])]
    convert_element_type x1 -> x2, other arithmetic: 1.1 us -> 0.18 us  [the longest x1 0.12 us: on_device(): behind_in = (behind + edge).astype(bf16)]
  transfers between devices with their start and end apart: 10 -> 9, of which waited for: 4 -> 2; matrix products, arithmetic and copies ran while one was open for 6% -> 4% of each run, Pallas kernels for 1% -> 1%
where the time goes in v4:
time: 71.8 us; the launch traced here: 71.3 us
  Pallas kernels  28.2 us (39%)
  starting transfers between devices  22 us (31%)
  waiting for transfers between devices  12.6 us (18%)
  local copies, waits for them, and re-layouts  4.65 us (6%)
  other arithmetic  2.28 us (3%)
  between operations  1.59 us (2%)
    pallas_call x2, Pallas kernels, call(): pl.pallas_call(kernel, in_specs=[smem] * scalars + [vmem] * (len(args) -...  28.2 us
    ppermute x9, starting transfers between devices, send(): return lax.ppermute(block, 'tile', route[name])  22 us
    ppermute x9, waiting for transfers between devices, send(): return lax.ppermute(block, 'tile', route[name])  12.6 us
    unnamed x14, local copies, waits for them, and re-layouts  2.99 us
    dynamic_slice x3, local copies, waits for them, and re-layouts, row_of(): return lax.dynamic_slice_in_dim(frame, jnp.where(first, 0, TR - 1), 1, 0)  1.59 us
  transfers between devices with their start and end apart: 9, of which 2 were waited for; matrix products, arithmetic and copies ran while one was open for 4% of the time, Pallas kernels for 1%

profile of v4, /device:TPU:9, one launch (start us, length us, event | category | flops | bytes accessed | tf_op | source)
XLA Modules:
  0.0 71.3 jit_solution(182842792544516681)
XLA Ops:
  0.6 3.2 %collective-permute-start.3 = (bf16[8,128,128]{2,1,0:T(8,128)(2,1)}, bf16[8,128,128]{2,1,0:T(8,128)(2,1)S(1)}, u32[]{:S(2)}, u32[]{:S(2)}) collective-permute-start(bf16[8,128,128]{2,1,0:T(8,128)(2,1)} %own_two.1), channel_id=1, source_target_pairs={{0,2},{2,4},{3,1},{4,6},{5,3},{6,8},{7,5},{8,10},{9,7},{10,12},{11... | collective-permute-start | bytes 786440 | tf_op jit(solution)/shard_map/ppermute | solution.py:302
  3.8 2.2 %collective-permute-start.2 = (bf16[8,128,128]{2,1,0:T(8,128)(2,1)}, bf16[8,128,128]{2,1,0:T(8,128)(2,1)S(1)}, u32[]{:S(2)}, u32[]{:S(2)}) collective-permute-start(bf16[8,128,128]{2,1,0:T(8,128)(2,1)} %own_two.1), channel_id=1, source_target_pairs={{1,3},{2,0},{3,5},{4,2},{5,7},{6,4},{7,9},{8,6},{9,11},{10,8},{11,... | collective-permute-start | bytes 786440 | tf_op jit(solution)/shard_map/ppermute | solution.py:302
  6.1 0.8 %constant_dynamic-slice_fusion.2 = bf16[1,128,128]{2,1,0:T(8,128)(2,1)S(1)} fusion(bf16[8,128,128]{2,1,0:T(8,128)(2,1)} %own_two.1, s32[]{:T(128)S(6)} %select_n.121), kind=kLoop, calls=%fused_computation.29 | loop fusion | bytes 65540 | tf_op jit(solution)/shard_map/dynamic_slice | solution.py:305
  6.9 5.2 %collective-permute-start = (bf16[1,128,128]{2,1,0:T(8,128)(2,1)S(1)}, bf16[1,128,128]{2,1,0:T(8,128)(2,1)S(1)}, u32[]{:S(2)}, u32[]{:S(2)}) collective-permute-start(bf16[1,128,128]{2,1,0:T(8,128)(2,1)S(1)} %constant_dynamic-slice_fusion.2), channel_id=1, source_target_pairs={{1,4},{3,6},{4,1},{5,8},{6,3},{7,10},{8,5},{9,12},{10,7},{11,14},{... | collective-permute-start | bytes 98312 | tf_op jit(solution)/shard_map/ppermute | solution.py:302
  12.1 0.8 %constant_dynamic-slice_fusion.1 = (bf16[1,128,128]{2,1,0:T(8,128)(2,1)S(1)}, bf16[1,128,128]{2,1,0:T(8,128)(2,1)S(1)}) fusion(bf16[8,128,128]{2,1,0:T(8,128)(2,1)} %own_one.1, s32[]{:T(128)S(6)} %select_n.121, s32[]{:T(128)S(6)} %select_n.120), kind=kLoop, calls=%fused_computation.28 | loop fusion | bytes 131080 | tf_op jit(solution)/shard_map/dynamic_slice | solution.py:305
  12.9 1.9 %collective-permute-start.1 = (bf16[1,128,128]{2,1,0:T(8,128)(2,1)S(1)}, bf16[1,128,128]{2,1,0:T(8,128)(2,1)S(1)}, u32[]{:S(2)}, u32[]{:S(2)}) collective-permute-start(bf16[1,128,128]{2,1,0:T(8,128)(2,1)S(1)} %get-tuple-element.40), channel_id=1, source_target_pairs={{1,2},{2,1},{3,4},{4,3},{5,6},{6,5},{7,8},{8,7},{9,10},{10,9},{11,... | collective-permute-start | bytes 98312 | tf_op jit(solution)/shard_map/ppermute | solution.py:302
  14.8 0.7 and_select_fusion
  15.6 0.6 copy-done.6
  16.9 0.1 pad_add_fusion.plan
  17.0 1.0 %tables.1 = (bf16[384,1024]{1,0:T(8,128)(2,1)S(1)}, bf16[1024,384]{1,0:T(8,128)(2,1)S(1)}) custom-call(), custom_call_target="tpu_custom_call" | custom-call | tf_op jit(solution)/shard_map/tables/pallas_call | solution.py:270
  18.0 0.9 %copy-done.1 = bf16[1024,384]{1,0:T(8,128)(2,1)} copy-done((bf16[1024,384]{1,0:T(8,128)(2,1)}, bf16[1024,384]{1,0:T(8,128)(2,1)S(1)}, u32[]{:S(2)}) %copy-start.1) | copy-done | bytes 786456
  19.0 0.1 pad_maximum_fusion
  19.1 0.5 copy-done.4
  19.7 0.6 collective-permute-start.4
  20.3 1.6 %collective-permute-done.4.from_sibling = bf16[18,128,128]{2,1,0:T(8,128)(2,1)S(1)} collective-permute-done((bf16[18,128,128]{2,1,0:T(8,128)(2,1)S(1)}, bf16[18,128,128]{2,1,0:T(8,128)(2,1)S(1)}, u32[]{:S(2)}, u32[]{:S(2)}) %collective-permute-start.4) | collective-permute-done | bytes 589856 | tf_op jit(solution)/shard_map/ppermute | solution.py:302
  21.9 0.9 %copy-done.5 = bf16[8,128,128]{2,1,0:T(8,128)(2,1)S(1)} copy-done((bf16[8,128,128]{2,1,0:T(8,128)(2,1)S(1)}, bf16[8,128,128]{2,1,0:T(8,128)(2,1)}, u32[]{:S(2)}) %copy-start.5) | copy-done | bytes 262168
  22.9 27.2 %work.1 = (bf16[19,128,128]{2,1,0:T(8,128)(2,1)}, f32[8,128,128]{2,1,0:T(8,128)S(1)}, f32[8,128,128]{2,1,0:T(8,128)S(1)}, bf16[1,128,128]{2,1,0:T(8,128)(2,1)S(1...) custom-call(s32[8]{0:T(128)S(1)} %pad_add_fusion.plan, bf16[8,128,128]{2,1,0:T(8,128)(2,1)S(1)} %copy-done.3, ...), custom_call_target="tpu_custom_call" | custom-call | tf_op jit(solution)/shard_map/work/pallas_call | solution.py:270
  50.0 0.1 collective-permute-start.5
  50.2 3.5 %collective-permute-start.8 = (bf16[1,128,128]{2,1,0:T(8,128)(2,1)S(1)}, bf16[1,128,128]{2,1,0:T(8,128)(2,1)S(1)}, u32[]{:S(2)}, u32[]{:S(2)}) collective-permute-start(bf16[1,128,128]{2,1,0:T(8,128)(2,1)S(1)} %get-tuple-element.31), channel_id=1, source_target_pairs={{1,4},{3,6},{4,1},{5,8},{6,3},{7,10},{8,5},{9,12},{10,7},{11,14},{... | collective-permute-start | bytes 98312 | tf_op jit(solution)/shard_map/ppermute | solution.py:302
  53.8 3.1 %collective-permute-start.6 = (bf16[9,128,128]{2,1,0:T(8,128)(2,1)S(1)}, bf16[9,128,128]{2,1,0:T(8,128)(2,1)S(1)}, u32[]{:S(2)}, u32[]{:S(2)}) collective-permute-start(bf16[9,128,128]{2,1,0:T(8,128)(2,1)S(1)} %pad_maximum_fusion.1), channel_id=1, source_target_pairs={{0,2},{2,4},{3,1},{4,6},{5,3},{6,8},{7,5},{8,10},{9,7},{10,12},{11... | collective-permute-start | bytes 884744 | tf_op jit(solution)/shard_map/ppermute | solution.py:302
  56.9 0.1 add_convert_fusion.1
  57.0 2.2 %collective-permute-start.7 = (bf16[8,128,128]{2,1,0:T(8,128)(2,1)S(1)}, bf16[8,128,128]{2,1,0:T(8,128)(2,1)S(1)}, u32[]{:S(2)}, u32[]{:S(2)}) collective-permute-start(bf16[8,128,128]{2,1,0:T(8,128)(2,1)S(1)} %add_convert_fusion.1), channel_id=1, source_target_pairs={{1,3},{2,0},{3,5},{4,2},{5,7},{6,4},{7,9},{8,6},{9,11},{10,8},{11,... | collective-permute-start | bytes 786440 | tf_op jit(solution)/shard_map/ppermute | solution.py:302
  59.2 11.0 %collective-permute-done.6 = bf16[9,128,128]{2,1,0:T(8,128)(2,1)S(1)} collective-permute-done((bf16[9,128,128]{2,1,0:T(8,128)(2,1)S(1)}, bf16[9,128,128]{2,1,0:T(8,128)(2,1)S(1)}, u32[]{:S(2)}, u32[]{:S(2)}) %collective-permute-start.6) | collective-permute-done | bytes 294944 | tf_op jit(solution)/shard_map/ppermute | solution.py:302
  70.2 1.1 %add_convert_fusion = (bf16[8,128,128]{2,1,0:T(8,128)(2,1)}, bf16[8,128,128]{2,1,0:T(8,128)(2,1)}) fusion(bf16[8,128,128]{2,1,0:T(8,128)(2,1)S(1)} %collective-permute-done.7, f32[8,128,128]{2,1,0:T(8,128)S(1)} %get-tuple-element.29, bf16[9,128,128]{2,1,0:T(8,128)(2,1)S(1)} %collective-permute-done.6, bf16[19,128,128]{2,1,0:T(8,128)(2,1)S(1)} %collective-permute-done.5, ...), kind=kLoop, calls=%fused_computation.1 | loop fusion | flops 1835008 | bytes 2555920 | tf_op jit(solution)/shard_map/convert_element_type | solution.py:388
  (30 shorter events, 0.3 us)
Async XLA Ops:
  0.6 18.4 %copy-start = (bf16[8,128,128]{2,1,0:T(8,128)(2,1)S(1)}, bf16[8,128,128]{2,1,0:T(8,128)(2,1)}, u32[]{:S(2)}) copy-start(bf16[8,128,128]{2,1,0:T(8,128)(2,1)} %own_two.1) | copy-start | bytes 786436
  0.6 18.3 %collective-permute-start.3 = (bf16[8,128,128]{2,1,0:T(8,128)(2,1)}, bf16[8,128,128]{2,1,0:T(8,128)(2,1)S(1)}, u32[]{:S(2)}, u32[]{:S(2)}) collective-permute-start(bf16[8,128,128]{2,1,0:T(8,128)(2,1)} %own_two.1), channel_id=1, source_target_pairs={{0,2},{2,4},{3,1},{4,6},{5,3},{6,8},{7,5},{8,10},{9,7},{10,12},{11... | collective-permute-start | bytes 786440 | tf_op jit(solution)/shard_map/ppermute | solution.py:302
  3.8 15.2 %collective-permute-start.2 = (bf16[8,128,128]{2,1,0:T(8,128)(2,1)}, bf16[8,128,128]{2,1,0:T(8,128)(2,1)S(1)}, u32[]{:S(2)}, u32[]{:S(2)}) collective-permute-start(bf16[8,128,128]{2,1,0:T(8,128)(2,1)} %own_two.1), channel_id=1, source_target_pairs={{1,3},{2,0},{3,5},{4,2},{5,7},{6,4},{7,9},{8,6},{9,11},{10,8},{11,... | collective-permute-start | bytes 786440 | tf_op jit(solution)/shard_map/ppermute | solution.py:302
  6.9 12.0 %collective-permute-start = (bf16[1,128,128]{2,1,0:T(8,128)(2,1)S(1)}, bf16[1,128,128]{2,1,0:T(8,128)(2,1)S(1)}, u32[]{:S(2)}, u32[]{:S(2)}) collective-permute-start(bf16[1,128,128]{2,1,0:T(8,128)(2,1)S(1)} %constant_dynamic-slice_fusion.2), channel_id=1, source_target_pairs={{1,4},{3,6},{4,1},{5,8},{6,3},{7,10},{8,5},{9,12},{10,7},{11,14},{... | collective-permute-start | bytes 98312 | tf_op jit(solution)/shard_map/ppermute | solution.py:302
  12.9 6.0 %collective-permute-start.1 = (bf16[1,128,128]{2,1,0:T(8,128)(2,1)S(1)}, bf16[1,128,128]{2,1,0:T(8,128)(2,1)S(1)}, u32[]{:S(2)}, u32[]{:S(2)}) collective-permute-start(bf16[1,128,128]{2,1,0:T(8,128)(2,1)S(1)} %get-tuple-element.40), channel_id=1, source_target_pairs={{1,2},{2,1},{3,4},{4,3},{5,6},{6,5},{7,8},{8,7},{9,10},{10,9},{11,... | collective-permute-start | bytes 98312 | tf_op jit(solution)/shard_map/ppermute | solution.py:302
  15.6 0.7 copy-start.6
  18.0 0.9 %copy-start.1 = (bf16[1024,384]{1,0:T(8,128)(2,1)}, bf16[1024,384]{1,0:T(8,128)(2,1)S(1)}, u32[]{:S(2)}) copy-start(bf16[1024,384]{1,0:T(8,128)(2,1)S(1)} %get-tuple-element.24.unpool) | copy-start | bytes 2359300
  19.0 0.7 copy-start.4
  19.0 2.9 %copy-start.2 = (bf16[3,3,128,256]{3,2,1,0:T(8,128)(2,1)S(1)}, bf16[3,3,128,256]{3,2,1,0:T(8,128)(2,1)}, u32[]{:S(2)}) copy-start(bf16[3,3,128,256]{3,2,1,0:T(8,128)(2,1)} %param.8) | copy-start | bytes 1769476
  19.0 2.9 %copy-start.3 = (bf16[8,128,128]{2,1,0:T(8,128)(2,1)S(1)}, bf16[8,128,128]{2,1,0:T(8,128)(2,1)}, u32[]{:S(2)}) copy-start(bf16[8,128,128]{2,1,0:T(8,128)(2,1)} %own_one.1) | copy-start | bytes 786436
  19.7 2.2 %collective-permute-start.4 = (bf16[18,128,128]{2,1,0:T(8,128)(2,1)S(1)}, bf16[18,128,128]{2,1,0:T(8,128)(2,1)S(1)}, u32[]{:S(2)}, u32[]{:S(2)}) collective-permute-start(bf16[18,128,128]{2,1,0:T(8,128)(2,1)S(1)} %pad_maximum_fusion), channel_id=1, source_target_pairs={{0,1},{1,0},{2,3},{3,2},{4,5},{5,4},{6,7},{7,6},{8,9},{9,8},{10,11... | collective-permute-start | bytes 1769480 | tf_op jit(solution)/shard_map/ppermute | solution.py:302
  21.9 1.0 %copy-start.5 = (bf16[8,128,128]{2,1,0:T(8,128)(2,1)S(1)}, bf16[8,128,128]{2,1,0:T(8,128)(2,1)}, u32[]{:S(2)}) copy-start(bf16[8,128,128]{2,1,0:T(8,128)(2,1)} %copy-done.4) | copy-start | bytes 786436
  50.0 3.6 %collective-permute-start.5 = (bf16[19,128,128]{2,1,0:T(8,128)(2,1)}, bf16[19,128,128]{2,1,0:T(8,128)(2,1)S(1)}, u32[]{:S(2)}, u32[]{:S(2)}) collective-permute-start(bf16[19,128,128]{2,1,0:T(8,128)(2,1)} %get-tuple-element.27), channel_id=1, source_target_pairs={{0,1},{1,0},{2,3},{3,2},{4,5},{5,4},{6,7},{7,6},{8,9},{9,8},{10,11... | collective-permute-start | bytes 1867784 | tf_op jit(solution)/shard_map/ppermute | solution.py:302
  50.2 9.0 %collective-permute-start.8 = (bf16[1,128,128]{2,1,0:T(8,128)(2,1)S(1)}, bf16[1,128,128]{2,1,0:T(8,128)(2,1)S(1)}, u32[]{:S(2)}, u32[]{:S(2)}) collective-permute-start(bf16[1,128,128]{2,1,0:T(8,128)(2,1)S(1)} %get-tuple-element.31), channel_id=1, source_target_pairs={{1,4},{3,6},{4,1},{5,8},{6,3},{7,10},{8,5},{9,12},{10,7},{11,14},{... | collective-permute-start | bytes 98312 | tf_op jit(solution)/shard_map/ppermute | solution.py:302
  53.8 16.4 %collective-permute-start.6 = (bf16[9,128,128]{2,1,0:T(8,128)(2,1)S(1)}, bf16[9,128,128]{2,1,0:T(8,128)(2,1)S(1)}, u32[]{:S(2)}, u32[]{:S(2)}) collective-permute-start(bf16[9,128,128]{2,1,0:T(8,128)(2,1)S(1)} %pad_maximum_fusion.1), channel_id=1, source_target_pairs={{0,2},{2,4},{3,1},{4,6},{5,3},{6,8},{7,5},{8,10},{9,7},{10,12},{11... | collective-permute-start | bytes 884744 | tf_op jit(solution)/shard_map/ppermute | solution.py:302
  57.0 13.2 %collective-permute-start.7 = (bf16[8,128,128]{2,1,0:T(8,128)(2,1)S(1)}, bf16[8,128,128]{2,1,0:T(8,128)(2,1)S(1)}, u32[]{:S(2)}, u32[]{:S(2)}) collective-permute-start(bf16[8,128,128]{2,1,0:T(8,128)(2,1)S(1)} %add_convert_fusion.1), channel_id=1, source_target_pairs={{1,3},{2,0},{3,5},{4,2},{5,7},{6,4},{7,9},{8,6},{9,11},{10,8},{11,... | collective-permute-start | bytes 786440 | tf_op jit(solution)/shard_map/ppermute | solution.py:302

commit v5 on v4

--- a/solution.py
+++ b/solution.py
@@ -42,7 +42,6 @@
         ahead=keep((i, i + 2 * side[i]) for i in range(count)),
         behind=keep((i, i - 2 * side[i]) for i in range(count)),
         far=keep((i, i - 3 * side[i]) for i in range(count)),
-        cross=keep((i, i - side[i]) for i in range(count)),
     )
 
 
@@ -108,24 +107,59 @@
     return jnp.where(cell >= offset, fill, result)
 
 
+def tile_side():
+    return 1 - 2 * lax.rem(lax.axis_index("tile"), 2)
+
+
 def tables_kernel(pool, unpool):
     pool[...] = pool_matrix((PAD, PIX), 0, [1.0] * LEVELS)
     unpool[...] = pool_matrix((PIX, PAD), 1, [2.0**-level for level in range(LEVELS)])
 
 
+def rows_kernel(one, two, near, far, inward, sems):
+    side = tile_side()
+    facing = jnp.where(side > 0, TR - 1, 0)
+    outer = jnp.where(side > 0, 0, TR - 1)
+    copies = [
+        pltpu.make_async_copy(two, near.at[pl.ds(0, TR)], sems.at[0]),
+        pltpu.make_async_copy(one.at[pl.ds(outer, 1)], near.at[pl.ds(TR, 1)], sems.at[1]),
+        pltpu.make_async_copy(two.at[pl.ds(outer, 1)], far, sems.at[2]),
+        pltpu.make_async_copy(one.at[pl.ds(facing, 1)], inward, sems.at[3]),
+    ]
+    for copy in copies:
+        copy.start()
+    for copy in copies:
+        copy.wait()
+
+
+def write_labels(targets, labels):
+    value = targets[...]
+    inside = value % PIX
+    row, column = inside // TC, inside % TC
+    offset = 0
+    for level in range(LEVELS):
+        cells = offset + (row >> level) * (TC >> level) + (column >> level)
+        for r in range(TR):
+            labels[level : level + 1, r * TC : (r + 1) * TC] = cells[r : r + 1, :]
+        offset += PIX >> (2 * level)
+    slots = value // PIX
+    for r in range(TR):
+        labels[LEVELS : LEVELS + 1, r * TC : (r + 1) * TC] = slots[r : r + 1, :]
+
+
 def work_kernel(
-    plan,
+    partners,
+    counts,
     own_one,
     own_two,
     near,
     direct,
     far,
-    cross,
     from_sibling,
     weight,
     pool,
     unpool,
-    labels,
+    targets,
     to_sibling_hbm,
     ahead_hbm,
     behind_hbm,
@@ -140,6 +174,7 @@
     sum_two,
     sems,
     weight_back,
+    labels,
     window,
     spread_two,
     window_one,
@@ -153,8 +188,9 @@
     total_two,
     total_one,
 ):
-    side = plan[5]
-    count = plan[4]
+    index = lax.axis_index("tile")
+    side = tile_side()
+    count = counts[0]
 
     def at(offset):
         return 1 + TR * (offset + RADIUS)
@@ -169,10 +205,11 @@
         window[at(side) + r] = from_sibling[r]
         window[at(-side) + r] = from_sibling[TR + r]
         window_one[1 + r] = own_one[r]
-    window[edge(side)] = from_sibling[2 * TR + 1]
+    window[edge(side)] = from_sibling[2 * TR + 2]
     window[edge(-side)] = far[0]
-    window_one[jnp.where(side > 0, TR + 1, 0)] = from_sibling[2 * TR]
-    window_one[jnp.where(side > 0, 0, TR + 1)] = cross[0]
+    window_one[jnp.where(side > 0, TR + 1, 0)] = from_sibling[2 * TR + 1]
+    window_one[jnp.where(side > 0, 0, TR + 1)] = from_sibling[2 * TR]
+    write_labels(targets, labels)
 
     for a in range(3):
         for b in range(3):
@@ -192,41 +229,41 @@
     total_two[...] = jnp.zeros_like(total_two)
     total_one[...] = jnp.zeros_like(total_one)
 
+    def work_slot(k):
+        first = TR * (partners[0, k] - index + RADIUS)
+        feat_two = convolve(spread_two, first, weight)
+        pyramid[0:PIX, :] = feat_two * jnp.bfloat16(2.0**-5)
+        means = matmul(pool[...], feat_two, NN) * per_level(
+            [4.0**-level for level in range(LEVELS)], 0.0
+        )
+        scale = per_level([2.0 ** (level - 5) for level in range(LEVELS)], 0.0)
+        pyramid[PIX:CELLS, :] = (
+            means.astype(jnp.bfloat16).astype(jnp.float32) * scale
+        ).astype(jnp.bfloat16)
+        features = feat_one[...]
+        here = labels[LEVELS : LEVELS + 1, :] == k
+        columns = [jnp.where(here, labels[m : m + 1, :], -1) for m in range(LEVELS)]
+        for start in range(0, CELLS, 256):
+            size = min(256, CELLS - start)
+            half_score = matmul(pyramid[start : start + size, :], features, NT)
+            position = lax.broadcasted_iota(jnp.int32, half_score.shape, 0) + start
+            if start < PIX:
+                hit = position == columns[0]
+            elif start < PIX + PIX // 4:
+                hit = position == columns[1]
+            else:
+                hit = (position == columns[2]) | (position == columns[3])
+            value = jnp.tanh(half_score - 1.0) + jnp.where(hit, -1.0, 1.0)
+            dscore[start : start + size, :] = value.astype(jnp.bfloat16)
+        level_grad[...] = matmul(dscore[...], features, NN)
+        grad_rows[...] += matmul(dscore[...], pyramid[...], TN)
+        coarse = level_grad[PIX:CELLS, :].astype(jnp.bfloat16)
+        gradient = level_grad[0:PIX, :] + matmul(unpool[...], coarse, NN)
+        level_grad[0:PIX, :] = gradient * 2.0**-5
+        convolve_back(level_grad, weight_back, moved, total_two, first)
+
     def slot(k, carry):
-        @pl.when(k < count)
-        def _():
-            first = TR * (plan[k] + RADIUS)
-            feat_two = convolve(spread_two, first, weight)
-            pyramid[0:PIX, :] = feat_two * jnp.bfloat16(2.0**-5)
-            means = matmul(pool[...], feat_two, NN) * per_level(
-                [4.0**-level for level in range(LEVELS)], 0.0
-            )
-            scale = per_level([2.0 ** (level - 5) for level in range(LEVELS)], 0.0)
-            pyramid[PIX:CELLS, :] = (
-                means.astype(jnp.bfloat16).astype(jnp.float32) * scale
-            ).astype(jnp.bfloat16)
-            features = feat_one[...]
-            here = labels[4:5, :] == k
-            columns = [jnp.where(here, labels[n : n + 1, :], -1) for n in range(LEVELS)]
-            for start in range(0, CELLS, 256):
-                size = min(256, CELLS - start)
-                half_score = matmul(pyramid[start : start + size, :], features, NT)
-                position = lax.broadcasted_iota(jnp.int32, half_score.shape, 0) + start
-                if start < PIX:
-                    hit = position == columns[0]
-                elif start < PIX + PIX // 4:
-                    hit = position == columns[1]
-                else:
-                    hit = (position == columns[2]) | (position == columns[3])
-                value = jnp.tanh(half_score - 1.0) + jnp.where(hit, -1.0, 1.0)
-                dscore[start : start + size, :] = value.astype(jnp.bfloat16)
-            level_grad[...] = matmul(dscore[...], features, NN)
-            grad_rows[...] += matmul(dscore[...], pyramid[...], TN)
-            coarse = level_grad[PIX:CELLS, :].astype(jnp.bfloat16)
-            gradient = level_grad[0:PIX, :] + matmul(unpool[...], coarse, NN)
-            gradient = gradient * 2.0**-5
-            convolve_back(gradient, weight_back, moved, total_two, first)
-
+        pl.when(k < count)(lambda: work_slot(k))
         return carry
 
     lax.fori_loop(0, SLOTS, slot, 0)
@@ -248,7 +285,7 @@
     to_sibling[0:TR] = rows(total_two, at(side), TR).astype(jnp.bfloat16)
     to_sibling[TR : 2 * TR] = rows(total_two, at(-side), TR).astype(jnp.bfloat16)
     to_sibling[2 * TR : 2 * TR + 1] = rows(total_two, edge(side)).astype(jnp.bfloat16)
-    convolve_back(grad_rows[...], weight_back, moved, total_one, 0)
+    convolve_back(grad_rows, weight_back, moved, total_one, 0)
     facing = jnp.where(side > 0, TR + 1, 0)
     outer = jnp.where(side > 0, 0, TR + 1)
     to_sibling[2 * TR + 1 : 2 * TR + 2] = rows(total_one, facing).astype(jnp.bfloat16)
@@ -264,13 +301,11 @@
     out(5, sum_one, sum_one_hbm).wait()
 
 
-def call(kernel, outs, scratch, args, name, scalars, space):
-    smem = pl.BlockSpec(memory_space=pltpu.SMEM)
-    vmem = pl.BlockSpec(memory_space=pltpu.VMEM)
+def call(kernel, outs, scratch, args, name, in_spaces, out_spaces):
     return pl.pallas_call(
         kernel,
-        in_specs=[smem] * scalars + [vmem] * (len(args) - scalars),
-        out_specs=[pl.BlockSpec(memory_space=space)] * len(outs),
+        in_specs=[pl.BlockSpec(memory_space=space) for space in in_spaces],
+        out_specs=[pl.BlockSpec(memory_space=space) for space in out_spaces],
         out_shape=[jax.ShapeDtypeStruct(*out) for out in outs],
         scratch_shapes=scratch,
         compiler_params=pltpu.CompilerParams(vmem_limit_bytes=LIMIT << 20),
@@ -278,20 +313,6 @@
     )(*args)
 
 
-def label_rows(targets):
-    value = targets.reshape(PIX)
-    inside = value % PIX
-    row, column = inside // TC, inside % TC
-    rows = []
-    offset = 0
-    for level in range(LEVELS):
-        rows.append(offset + (row >> level) * (TC >> level) + (column >> level))
-        offset += PIX >> (2 * level)
-    rows.append(value // PIX)
-    rows += [rows[-1]] * 3
-    return jnp.stack(rows).astype(jnp.int32)
-
-
 def on_device(frame_one, frame_two, conv_weight, partners, counts, targets):
     route = routes(lax.axis_size("tile"))
     index = lax.axis_index("tile")
@@ -301,32 +322,33 @@
     def send(block, name):
         return lax.ppermute(block, "tile", route[name])
 
-    def row_of(frame, first):
-        return lax.dynamic_slice_in_dim(frame, jnp.where(first, 0, TR - 1), 1, 0)
-
-    plan = jnp.concatenate(
-        [partners[0] - index, counts, side[None], jnp.zeros((2,), jnp.int32)]
-    ).astype(jnp.int32)
-    labels = label_rows(targets)
+    row_block = (1, TC, CIN)
     weight = conv_weight.reshape(9 * CIN, CH)
-    near = send(frame_two, "behind")
     direct = send(frame_two, "ahead")
-    tables = call(
+    near_in, far_in, inward = call(
+        rows_kernel,
+        [((TR + 1, TC, CIN), bf16), (row_block, bf16), (row_block, bf16)],
+        [pltpu.SemaphoreType.DMA((4,))],
+        [frame_one, frame_two],
+        "rows",
+        [pltpu.HBM] * 2,
+        [pltpu.HBM] * 3,
+    )
+    near = send(near_in, "behind")
+    far = send(far_in, "far")
+    pool, unpool = call(
         tables_kernel,
         [((PAD, PIX), bf16), ((PIX, PAD), bf16)],
         [],
         [],
         "tables",
-        0,
-        pltpu.VMEM,
+        [],
+        [pltpu.VMEM] * 2,
     )
-    far = send(row_of(frame_two, side > 0), "far")
-    cross = send(row_of(frame_one, side > 0), "cross")
-    inward = row_of(frame_one, side < 0)
-    inward, far, cross, tables, labels, plan = lax.optimization_barrier(
-        (inward, far, cross, tables, labels, plan)
-    )
-    payload = jnp.concatenate([frame_two, near, inward, row_of(direct, side < 0)])
+    inward, far, pool, unpool = lax.optimization_barrier((inward, far, pool, unpool))
+    facing_row = jnp.where(side > 0, TR - 1, 0)
+    direct_row = lax.dynamic_slice_in_dim(direct, facing_row, 1, 0)
+    payload = jnp.concatenate([frame_two, near, inward, direct_row])
     from_sibling = send(payload, "swap")
 
     tile = (TR, TC, CIN)
@@ -341,6 +363,7 @@
     ]
     scratch = [
         ((3 * CIN, 3 * CH), bf16),
+        ((8, PIX), jnp.int32),
         ((WIN, TC, CIN), bf16),
         ((WIN * TC, 3 * CIN), bf16),
         ((TR + 2, TC, CIN), bf16),
@@ -360,11 +383,11 @@
         [pltpu.VMEM(*out) for out in outs]
         + [pltpu.SemaphoreType.DMA((len(outs),))]
         + [pltpu.VMEM(*item) for item in scratch],
-        [plan, frame_one, frame_two, near, direct, far, cross]
-        + [from_sibling, weight, *tables, labels],
+        [partners, counts, frame_one, frame_two, near, direct, far]
+        + [from_sibling, weight, pool, unpool, targets],
         "work",
-        1,
-        pltpu.HBM,
+        [pltpu.SMEM] * 2 + [pltpu.VMEM] * 10,
+        [pltpu.HBM] * len(outs),
     )
     row = lax.broadcasted_iota(jnp.int32, (TR, 1, 1), 0)
     facing = row == jnp.where(side > 0, TR - 1, 0)

time: 71.8 us -> 70 us (0.975)
  Pallas kernels: 28.2 us -> 23 us
  starting transfers between devices: 22 us -> 25.9 us
  waiting for transfers between devices: 12.6 us -> 14 us
  local copies, waits for them, and re-layouts: 4.65 us -> 3.77 us
  other arithmetic: 2.28 us -> 1.42 us
    pallas_call x2 -> x3, Pallas kernels: 28.2 us -> 23 us  [call(): pl.pallas_call(kernel, in_specs=[pl.BlockSpec(memory_space=space) for spa...]
    ppermute x9 -> x8, starting transfers between devices: 22 us -> 25.9 us  [send(): return lax.ppermute(block, 'tile', route[name])]
    dynamic_slice x3 -> x1, local copies, waits for them, and re-layouts: 1.59 us -> 0.01 us  [on_device(): direct_row = lax.dynamic_slice_in_dim(direct, facing_row, 1, 0)]
    ppermute x9 -> x8, waiting for transfers between devices: 12.6 us -> 14 us  [send(): return lax.ppermute(block, 'tile', route[name])]
    unnamed x14 -> x20, local copies, waits for them, and re-layouts: 2.99 us -> 3.76 us
  transfers between devices with their start and end apart: 9 -> 8, of which waited for: 2 -> 4; matrix products, arithmetic and copies ran while one was open for 4% -> 0% of each run, Pallas kernels for 1% -> 2%
where the time goes in v5:
time: 70 us; the launch traced here: 69.6 us
  starting transfers between devices  25.9 us (37%)
  Pallas kernels  23 us (33%)
  waiting for transfers between devices  14 us (20%)
  local copies, waits for them, and re-layouts  3.77 us (5%)
  between operations  1.49 us (2%)
  other arithmetic  1.42 us (2%)
    ppermute x8, starting transfers between devices, send(): return lax.ppermute(block, 'tile', route[name])  25.9 us
    pallas_call x3, Pallas kernels, call(): pl.pallas_call(kernel, in_specs=[pl.BlockSpec(memory_space=space) for spa...  23 us
    ppermute x8, waiting for transfers between devices, send(): return lax.ppermute(block, 'tile', route[name])  14 us
    unnamed x20, local copies, waits for them, and re-layouts  3.76 us
  transfers between devices with their start and end apart: 8, of which 4 were waited for; matrix products, arithmetic and copies ran while one was open for 0% of the time, Pallas kernels for 2%

profile of v5, /device:TPU:9, one launch (start us, length us, event | category | flops | bytes accessed | tf_op | source)
XLA Modules:
  0.0 69.6 jit_solution(3486188839790047074)
XLA Ops:
  0.6 3.0 %collective-permute-start.1 = (bf16[8,128,128]{2,1,0:T(8,128)(2,1)}, bf16[8,128,128]{2,1,0:T(8,128)(2,1)S(1)}, u32[]{:S(2)}, u32[]{:S(2)}) collective-permute-start(bf16[8,128,128]{2,1,0:T(8,128)(2,1)} %own_two.1), channel_id=1, source_target_pairs={{0,2},{2,4},{3,1},{4,6},{5,3},{6,8},{7,5},{8,10},{9,7},{10,12},{11... | collective-permute-start | bytes 786440 | tf_op jit(solution)/shard_map/ppermute | solution.py:323
  3.7 1.0 %copy-done = bf16[8,128,128]{2,1,0:T(8,128)(2,1)S(1)} copy-done((bf16[8,128,128]{2,1,0:T(8,128)(2,1)S(1)}, bf16[8,128,128]{2,1,0:T(8,128)(2,1)}, u32[]{:S(2)}) %copy-start) | copy-done | bytes 262168
  4.6 0.9 %copy-done.2 = bf16[8,128,128]{2,1,0:T(8,128)(2,1)S(1)} copy-done((bf16[8,128,128]{2,1,0:T(8,128)(2,1)S(1)}, bf16[8,128,128]{2,1,0:T(8,128)(2,1)}, u32[]{:S(2)}) %copy-start.2) | copy-done | bytes 262168
  5.6 0.2 rows.1
  5.8 2.2 %collective-permute-start = (bf16[9,128,128]{2,1,0:T(8,128)(2,1)S(1)}, bf16[9,128,128]{2,1,0:T(8,128)(2,1)S(1)}, u32[]{:S(2)}, u32[]{:S(2)}) collective-permute-start(bf16[9,128,128]{2,1,0:T(8,128)(2,1)S(1)} %get-tuple-element.17), channel_id=1, source_target_pairs={{1,3},{2,0},{3,5},{4,2},{5,7},{6,4},{7,9},{8,6},{9,11},{10,8},{11,... | collective-permute-start | bytes 884744 | tf_op jit(solution)/shard_map/ppermute | solution.py:323
  8.0 5.2 %collective-permute-start.2 = (bf16[1,128,128]{2,1,0:T(8,128)(2,1)S(1)}, bf16[1,128,128]{2,1,0:T(8,128)(2,1)S(1)}, u32[]{:S(2)}, u32[]{:S(2)}) collective-permute-start(bf16[1,128,128]{2,1,0:T(8,128)(2,1)S(1)} %get-tuple-element.19), channel_id=1, source_target_pairs={{1,4},{3,6},{4,1},{5,8},{6,3},{7,10},{8,5},{9,12},{10,7},{11,14},{... | collective-permute-start | bytes 98312 | tf_op jit(solution)/shard_map/ppermute | solution.py:323
  13.3 1.0 %tables.1 = (bf16[384,1024]{1,0:T(8,128)(2,1)S(1)}, bf16[1024,384]{1,0:T(8,128)(2,1)S(1)}) custom-call(), custom_call_target="tpu_custom_call" | custom-call | tf_op jit(solution)/shard_map/tables/pallas_call | solution.py:305
  14.3 0.9 %copy-done.4 = bf16[1024,384]{1,0:T(8,128)(2,1)} copy-done((bf16[1024,384]{1,0:T(8,128)(2,1)}, bf16[1024,384]{1,0:T(8,128)(2,1)S(1)}, u32[]{:S(2)}) %copy-start.4) | copy-done | bytes 786456
  15.2 1.3 %collective-permute-done.2.far = bf16[1,128,128]{2,1,0:T(8,128)(2,1)S(1)} collective-permute-done((bf16[1,128,128]{2,1,0:T(8,128)(2,1)S(1)}, bf16[1,128,128]{2,1,0:T(8,128)(2,1)S(1)}, u32[]{:S(2)}, u32[]{:S(2)}) %collective-permute-start.2) | collective-permute-done | bytes 32800 | tf_op jit(solution)/shard_map/ppermute | solution.py:323
  16.4 0.0 copy-start.3
  16.5 0.9 %collective-permute-done.near = bf16[9,128,128]{2,1,0:T(8,128)(2,1)S(1)} collective-permute-done((bf16[9,128,128]{2,1,0:T(8,128)(2,1)S(1)}, bf16[9,128,128]{2,1,0:T(8,128)(2,1)S(1)}, u32[]{:S(2)}, u32[]{:S(2)}) %collective-permute-start) | collective-permute-done | bytes 294944 | tf_op jit(solution)/shard_map/ppermute | solution.py:323
  17.3 0.1 pad_maximum_fusion
  17.4 0.7 %collective-permute-start.3 = (bf16[19,128,128]{2,1,0:T(8,128)(2,1)S(1)}, bf16[19,128,128]{2,1,0:T(8,128)(2,1)S(1)}, u32[]{:S(2)}, u32[]{:S(2)}) collective-permute-start(bf16[19,128,128]{2,1,0:T(8,128)(2,1)S(1)} %pad_maximum_fusion), channel_id=1, source_target_pairs={{0,1},{1,0},{2,3},{3,2},{4,5},{5,4},{6,7},{7,6},{8,9},{9,8},{10,11... | collective-permute-start | bytes 1867784 | tf_op jit(solution)/shard_map/ppermute | solution.py:323
  18.8 1.0 %collective-permute-done.3.from_sibling = bf16[19,128,128]{2,1,0:T(8,128)(2,1)S(1)} collective-permute-done((bf16[19,128,128]{2,1,0:T(8,128)(2,1)S(1)}, bf16[19,128,128]{2,1,0:T(8,128)(2,1)S(1)}, u32[]{:S(2)}, u32[]{:S(2)}) %collective-permute-start.3) | collective-permute-done | bytes 622624 | tf_op jit(solution)/shard_map/ppermute | solution.py:323
  19.9 0.9 %copy-done.7 = bf16[8,128,128]{2,1,0:T(8,128)(2,1)S(1)} copy-done((bf16[8,128,128]{2,1,0:T(8,128)(2,1)S(1)}, bf16[8,128,128]{2,1,0:T(8,128)(2,1)}, u32[]{:S(2)}) %copy-start.7) | copy-done | bytes 262168
  20.8 21.8 %work.1 = (bf16[19,128,128]{2,1,0:T(8,128)(2,1)}, f32[8,128,128]{2,1,0:T(8,128)S(1)}, f32[8,128,128]{2,1,0:T(8,128)S(1)}, bf16[1,128,128]{2,1,0:T(8,128)(2,1)S(1...) custom-call(s32[1,4]{1,0:T(1,128)S(1)} %copy-done.9, s32[1]{0:T(128)S(6)} %copy.8.counts, ...), custom_call_target="tpu_custom_call" | custom-call | tf_op jit(solution)/shard_map/work/pallas_call | solution.py:305
  42.6 5.9 %collective-permute-start.4 = (bf16[19,128,128]{2,1,0:T(8,128)(2,1)}, bf16[19,128,128]{2,1,0:T(8,128)(2,1)S(1)}, u32[]{:S(2)}, u32[]{:S(2)}) collective-permute-start(bf16[19,128,128]{2,1,0:T(8,128)(2,1)} %get-tuple-element.27), channel_id=1, source_target_pairs={{0,1},{1,0},{2,3},{3,2},{4,5},{5,4},{6,7},{7,6},{8,9},{9,8},{10,11... | collective-permute-start | bytes 1867784 | tf_op jit(solution)/shard_map/ppermute | solution.py:323
  48.5 3.2 %collective-permute-start.7 = (bf16[1,128,128]{2,1,0:T(8,128)(2,1)S(1)}, bf16[1,128,128]{2,1,0:T(8,128)(2,1)S(1)}, u32[]{:S(2)}, u32[]{:S(2)}) collective-permute-start(bf16[1,128,128]{2,1,0:T(8,128)(2,1)S(1)} %get-tuple-element.31), channel_id=1, source_target_pairs={{1,4},{3,6},{4,1},{5,8},{6,3},{7,10},{8,5},{9,12},{10,7},{11,14},{... | collective-permute-start | bytes 98312 | tf_op jit(solution)/shard_map/ppermute | solution.py:323
  51.7 0.1 add_convert_fusion.3
  51.8 3.5 %collective-permute-start.5 = (bf16[9,128,128]{2,1,0:T(8,128)(2,1)S(1)}, bf16[9,128,128]{2,1,0:T(8,128)(2,1)S(1)}, u32[]{:S(2)}, u32[]{:S(2)}) collective-permute-start(bf16[9,128,128]{2,1,0:T(8,128)(2,1)S(1)} %pad_maximum_fusion.1), channel_id=1, source_target_pairs={{0,2},{2,4},{3,1},{4,6},{5,3},{6,8},{7,5},{8,10},{9,7},{10,12},{11... | collective-permute-start | bytes 884744 | tf_op jit(solution)/shard_map/ppermute | solution.py:323
  55.3 0.1 add_convert_fusion.1
  55.4 2.1 %collective-permute-start.6 = (bf16[8,128,128]{2,1,0:T(8,128)(2,1)S(1)}, bf16[8,128,128]{2,1,0:T(8,128)(2,1)S(1)}, u32[]{:S(2)}, u32[]{:S(2)}) collective-permute-start(bf16[8,128,128]{2,1,0:T(8,128)(2,1)S(1)} %add_convert_fusion.1), channel_id=1, source_target_pairs={{1,3},{2,0},{3,5},{4,2},{5,7},{6,4},{7,9},{8,6},{9,11},{10,8},{11,... | collective-permute-start | bytes 786440 | tf_op jit(solution)/shard_map/ppermute | solution.py:323
  57.6 10.9 %collective-permute-done.5 = bf16[9,128,128]{2,1,0:T(8,128)(2,1)S(1)} collective-permute-done((bf16[9,128,128]{2,1,0:T(8,128)(2,1)S(1)}, bf16[9,128,128]{2,1,0:T(8,128)(2,1)S(1)}, u32[]{:S(2)}, u32[]{:S(2)}) %collective-permute-start.5) | collective-permute-done | bytes 294944 | tf_op jit(solution)/shard_map/ppermute | solution.py:323
  68.5 1.1 %add_convert_fusion = (bf16[8,128,128]{2,1,0:T(8,128)(2,1)}, bf16[8,128,128]{2,1,0:T(8,128)(2,1)}) fusion(bf16[8,128,128]{2,1,0:T(8,128)(2,1)S(1)} %collective-permute-done.6, f32[8,128,128]{2,1,0:T(8,128)S(1)} %get-tuple-element.29, bf16[9,128,128]{2,1,0:T(8,128)(2,1)S(1)} %collective-permute-done.5, bf16[19,128,128]{2,1,0:T(8,128)(2,1)S(1)} %collective-permute-done.4, ...), kind=kLoop, calls=%fused_computation.1 | loop fusion | flops 1835008 | bytes 2555920 | tf_op jit(solution)/shard_map/convert_element_type | solution.py:411
  (26 shorter events, 0.1 us)
Async XLA Ops:
  0.6 15.8 %collective-permute-start.1 = (bf16[8,128,128]{2,1,0:T(8,128)(2,1)}, bf16[8,128,128]{2,1,0:T(8,128)(2,1)S(1)}, u32[]{:S(2)}, u32[]{:S(2)}) collective-permute-start(bf16[8,128,128]{2,1,0:T(8,128)(2,1)} %own_two.1), channel_id=1, source_target_pairs={{0,2},{2,4},{3,1},{4,6},{5,3},{6,8},{7,5},{8,10},{9,7},{10,12},{11... | collective-permute-start | bytes 786440 | tf_op jit(solution)/shard_map/ppermute | solution.py:323
  3.7 1.0 %copy-start = (bf16[8,128,128]{2,1,0:T(8,128)(2,1)S(1)}, bf16[8,128,128]{2,1,0:T(8,128)(2,1)}, u32[]{:S(2)}) copy-start(bf16[8,128,128]{2,1,0:T(8,128)(2,1)} %own_two.1) | copy-start | bytes 786436
  4.6 0.9 %copy-start.2 = (bf16[8,128,128]{2,1,0:T(8,128)(2,1)S(1)}, bf16[8,128,128]{2,1,0:T(8,128)(2,1)}, u32[]{:S(2)}) copy-start(bf16[8,128,128]{2,1,0:T(8,128)(2,1)} %own_one.1) | copy-start | bytes 786436
  5.6 11.7 %copy-start.1 = (bf16[8,128,128]{2,1,0:T(8,128)(2,1)S(1)}, bf16[8,128,128]{2,1,0:T(8,128)(2,1)}, u32[]{:S(2)}) copy-start(bf16[8,128,128]{2,1,0:T(8,128)(2,1)} %own_two.1) | copy-start | bytes 786436
  5.8 11.5 %collective-permute-start = (bf16[9,128,128]{2,1,0:T(8,128)(2,1)S(1)}, bf16[9,128,128]{2,1,0:T(8,128)(2,1)S(1)}, u32[]{:S(2)}, u32[]{:S(2)}) collective-permute-start(bf16[9,128,128]{2,1,0:T(8,128)(2,1)S(1)} %get-tuple-element.17), channel_id=1, source_target_pairs={{1,3},{2,0},{3,5},{4,2},{5,7},{6,4},{7,9},{8,6},{9,11},{10,8},{11,... | collective-permute-start | bytes 884744 | tf_op jit(solution)/shard_map/ppermute | solution.py:323
  8.0 8.4 %collective-permute-start.2 = (bf16[1,128,128]{2,1,0:T(8,128)(2,1)S(1)}, bf16[1,128,128]{2,1,0:T(8,128)(2,1)S(1)}, u32[]{:S(2)}, u32[]{:S(2)}) collective-permute-start(bf16[1,128,128]{2,1,0:T(8,128)(2,1)S(1)} %get-tuple-element.19), channel_id=1, source_target_pairs={{1,4},{3,6},{4,1},{5,8},{6,3},{7,10},{8,5},{9,12},{10,7},{11,14},{... | collective-permute-start | bytes 98312 | tf_op jit(solution)/shard_map/ppermute | solution.py:323
  14.3 0.9 %copy-start.4 = (bf16[1024,384]{1,0:T(8,128)(2,1)}, bf16[1024,384]{1,0:T(8,128)(2,1)S(1)}, u32[]{:S(2)}) copy-start(bf16[1024,384]{1,0:T(8,128)(2,1)S(1)} %get-tuple-element.25.unpool) | copy-start | bytes 2359300
  16.4 1.0 %copy-start.6 = (bf16[8,128,128]{2,1,0:T(8,128)(2,1)}, bf16[8,128,128]{2,1,0:T(8,128)(2,1)S(1)}, u32[]{:S(2)}) copy-start(bf16[8,128,128]{2,1,0:T(8,128)(2,1)S(1)} %collective-permute-done.1.direct) | copy-start | bytes 786436
  16.4 3.4 %copy-start.3 = (bf16[8,128,128]{2,1,0:T(8,128)(2,1)S(1)}, bf16[8,128,128]{2,1,0:T(8,128)(2,1)}, u32[]{:S(2)}) copy-start(bf16[8,128,128]{2,1,0:T(8,128)(2,1)} %own_one.1) | copy-start | bytes 786436
  16.4 3.4 %copy-start.5 = (bf16[3,3,128,256]{3,2,1,0:T(8,128)(2,1)S(1)}, bf16[3,3,128,256]{3,2,1,0:T(8,128)(2,1)}, u32[]{:S(2)}) copy-start(bf16[3,3,128,256]{3,2,1,0:T(8,128)(2,1)} %param.8) | copy-start | bytes 1769476
  17.3 2.5 %copy-start.8 = (s32[8,128]{1,0:T(8,128)S(1)}, s32[8,128]{1,0:T(8,128)}, u32[]{:S(2)}) copy-start(s32[8,128]{1,0:T(8,128)} %targets.1) | copy-start | bytes 12292
  17.4 2.4 %collective-permute-start.3 = (bf16[19,128,128]{2,1,0:T(8,128)(2,1)S(1)}, bf16[19,128,128]{2,1,0:T(8,128)(2,1)S(1)}, u32[]{:S(2)}, u32[]{:S(2)}) collective-permute-start(bf16[19,128,128]{2,1,0:T(8,128)(2,1)S(1)} %pad_maximum_fusion), channel_id=1, source_target_pairs={{0,1},{1,0},{2,3},{3,2},{4,5},{5,4},{6,7},{7,6},{8,9},{9,8},{10,11... | collective-permute-start | bytes 1867784 | tf_op jit(solution)/shard_map/ppermute | solution.py:323
  18.8 1.0 %copy-start.9 = (s32[1,4]{1,0:T(1,128)S(1)}, s32[1,4]{1,0:T(1,128)}, u32[]{:S(2)}) copy-start(s32[1,4]{1,0:T(1,128)} %partners.1) | copy-start | bytes 52
  19.9 1.0 %copy-start.7 = (bf16[8,128,128]{2,1,0:T(8,128)(2,1)S(1)}, bf16[8,128,128]{2,1,0:T(8,128)(2,1)}, u32[]{:S(2)}) copy-start(bf16[8,128,128]{2,1,0:T(8,128)(2,1)} %copy-done.6) | copy-start | bytes 786436
  42.6 9.1 %collective-permute-start.4 = (bf16[19,128,128]{2,1,0:T(8,128)(2,1)}, bf16[19,128,128]{2,1,0:T(8,128)(2,1)S(1)}, u32[]{:S(2)}, u32[]{:S(2)}) collective-permute-start(bf16[19,128,128]{2,1,0:T(8,128)(2,1)} %get-tuple-element.27), channel_id=1, source_target_pairs={{0,1},{1,0},{2,3},{3,2},{4,5},{5,4},{6,7},{7,6},{8,9},{9,8},{10,11... | collective-permute-start | bytes 1867784 | tf_op jit(solution)/shard_map/ppermute | solution.py:323
  48.5 9.1 %collective-permute-start.7 = (bf16[1,128,128]{2,1,0:T(8,128)(2,1)S(1)}, bf16[1,128,128]{2,1,0:T(8,128)(2,1)S(1)}, u32[]{:S(2)}, u32[]{:S(2)}) collective-permute-start(bf16[1,128,128]{2,1,0:T(8,128)(2,1)S(1)} %get-tuple-element.31), channel_id=1, source_target_pairs={{1,4},{3,6},{4,1},{5,8},{6,3},{7,10},{8,5},{9,12},{10,7},{11,14},{... | collective-permute-start | bytes 98312 | tf_op jit(solution)/shard_map/ppermute | solution.py:323
  51.8 16.7 %collective-permute-start.5 = (bf16[9,128,128]{2,1,0:T(8,128)(2,1)S(1)}, bf16[9,128,128]{2,1,0:T(8,128)(2,1)S(1)}, u32[]{:S(2)}, u32[]{:S(2)}) collective-permute-start(bf16[9,128,128]{2,1,0:T(8,128)(2,1)S(1)} %pad_maximum_fusion.1), channel_id=1, source_target_pairs={{0,2},{2,4},{3,1},{4,6},{5,3},{6,8},{7,5},{8,10},{9,7},{10,12},{11... | collective-permute-start | bytes 884744 | tf_op jit(solution)/shard_map/ppermute | solution.py:323
  55.4 13.1 %collective-permute-start.6 = (bf16[8,128,128]{2,1,0:T(8,128)(2,1)S(1)}, bf16[8,128,128]{2,1,0:T(8,128)(2,1)S(1)}, u32[]{:S(2)}, u32[]{:S(2)}) collective-permute-start(bf16[8,128,128]{2,1,0:T(8,128)(2,1)S(1)} %add_convert_fusion.1), channel_id=1, source_target_pairs={{1,3},{2,0},{3,5},{4,2},{5,7},{6,4},{7,9},{8,6},{9,11},{10,8},{11,... | collective-permute-start | bytes 786440 | tf_op jit(solution)/shard_map/ppermute | solution.py:323

commit v6 on v5

--- a/solution.py
+++ b/solution.py
@@ -19,7 +19,8 @@
 POOLED = PIX // 4 + PIX // 16 + PIX // 64
 PAD = 384
 CELLS = PIX + PAD
-LIMIT = 48
+CHUNK = 256
+LIMIT = 50
 WIN = 2 * RADIUS * TR + TR + 2
 
 NN = (((1,), (0,)), ((), ()))
@@ -42,6 +43,7 @@
         ahead=keep((i, i + 2 * side[i]) for i in range(count)),
         behind=keep((i, i - 2 * side[i]) for i in range(count)),
         far=keep((i, i - 3 * side[i]) for i in range(count)),
+        cross=keep((i, i - side[i]) for i in range(count)),
     )
 
 
@@ -70,14 +72,17 @@
     return total.astype(jnp.bfloat16)
 
 
-def convolve_back(gradient, weight_back, moved, total, at):
+def spread_back(gradient, moved):
     for r in range(TR):
-        block = gradient[r * TC : (r + 1) * TC, :]
+        rows = slice(r * TC, (r + 1) * TC)
+        block = gradient[rows, :]
         down, up = shifted(block)
-        rows = slice(r * TC, (r + 1) * TC)
         moved[rows, 0:CH] = up.astype(jnp.bfloat16)
         moved[rows, CH : 2 * CH] = block.astype(jnp.bfloat16)
         moved[rows, 2 * CH : 3 * CH] = down.astype(jnp.bfloat16)
+
+
+def convolve_back(moved, weight_back, total, at):
     parts = matmul(moved[...], weight_back[...], NT)
     for a in range(3):
         where = pl.ds(pl.multiple_of((at + a) * TC, TC), PIX)
@@ -116,15 +121,14 @@
     unpool[...] = pool_matrix((PIX, PAD), 1, [2.0**-level for level in range(LEVELS)])
 
 
-def rows_kernel(one, two, near, far, inward, sems):
+def rows_kernel(one, two, cross, far, inward, sems):
     side = tile_side()
     facing = jnp.where(side > 0, TR - 1, 0)
     outer = jnp.where(side > 0, 0, TR - 1)
     copies = [
-        pltpu.make_async_copy(two, near.at[pl.ds(0, TR)], sems.at[0]),
-        pltpu.make_async_copy(one.at[pl.ds(outer, 1)], near.at[pl.ds(TR, 1)], sems.at[1]),
-        pltpu.make_async_copy(two.at[pl.ds(outer, 1)], far, sems.at[2]),
-        pltpu.make_async_copy(one.at[pl.ds(facing, 1)], inward, sems.at[3]),
+        pltpu.make_async_copy(one.at[pl.ds(outer, 1)], cross, sems.at[0]),
+        pltpu.make_async_copy(two.at[pl.ds(outer, 1)], far, sems.at[1]),
+        pltpu.make_async_copy(one.at[pl.ds(facing, 1)], inward, sems.at[2]),
     ]
     for copy in copies:
         copy.start()
@@ -155,6 +159,7 @@
     near,
     direct,
     far,
+    cross,
     from_sibling,
     weight,
     pool,
@@ -180,6 +185,7 @@
     window_one,
     spread_one,
     feat_one,
+    feat_two,
     pyramid,
     dscore,
     level_grad,
@@ -205,10 +211,10 @@
         window[at(side) + r] = from_sibling[r]
         window[at(-side) + r] = from_sibling[TR + r]
         window_one[1 + r] = own_one[r]
-    window[edge(side)] = from_sibling[2 * TR + 2]
+    window[edge(side)] = from_sibling[2 * TR + 1]
     window[edge(-side)] = far[0]
-    window_one[jnp.where(side > 0, TR + 1, 0)] = from_sibling[2 * TR + 1]
-    window_one[jnp.where(side > 0, 0, TR + 1)] = from_sibling[2 * TR]
+    window_one[jnp.where(side > 0, TR + 1, 0)] = from_sibling[2 * TR]
+    window_one[jnp.where(side > 0, 0, TR + 1)] = cross[0]
     write_labels(targets, labels)
 
     for a in range(3):
@@ -229,38 +235,47 @@
     total_two[...] = jnp.zeros_like(total_two)
     total_one[...] = jnp.zeros_like(total_one)
 
+    def first_row(k):
+        return TR * (partners[0, k] - index + RADIUS)
+
+    feat_two[...] = convolve(spread_two, first_row(0), weight)
+
     def work_slot(k):
-        first = TR * (partners[0, k] - index + RADIUS)
-        feat_two = convolve(spread_two, first, weight)
-        pyramid[0:PIX, :] = feat_two * jnp.bfloat16(2.0**-5)
-        means = matmul(pool[...], feat_two, NN) * per_level(
+        features = feat_one[...]
+        here = labels[LEVELS : LEVELS + 1, :] == k
+        columns = [jnp.where(here, labels[m : m + 1, :], -1) for m in range(LEVELS)]
+
+        def score(start, size, hits):
+            half_score = matmul(pyramid[start : start + size, :], features, NT)
+            position = lax.broadcasted_iota(jnp.int32, half_score.shape, 0) + start
+            hit = position == hits[0]
+            for more in hits[1:]:
+                hit = hit | (position == more)
+            value = jnp.tanh(half_score - 1.0) + jnp.where(hit, -1.0, 1.0)
+            dscore[start : start + size, :] = value.astype(jnp.bfloat16)
+
+        pyramid[0:PIX, :] = feat_two[...] * jnp.bfloat16(2.0**-5)
+        score(0, CHUNK, columns[:1])
+        means = matmul(pool[...], feat_two[...], NN) * per_level(
             [4.0**-level for level in range(LEVELS)], 0.0
         )
         scale = per_level([2.0 ** (level - 5) for level in range(LEVELS)], 0.0)
         pyramid[PIX:CELLS, :] = (
             means.astype(jnp.bfloat16).astype(jnp.float32) * scale
         ).astype(jnp.bfloat16)
-        features = feat_one[...]
-        here = labels[LEVELS : LEVELS + 1, :] == k
-        columns = [jnp.where(here, labels[m : m + 1, :], -1) for m in range(LEVELS)]
-        for start in range(0, CELLS, 256):
-            size = min(256, CELLS - start)
-            half_score = matmul(pyramid[start : start + size, :], features, NT)
-            position = lax.broadcasted_iota(jnp.int32, half_score.shape, 0) + start
-            if start < PIX:
-                hit = position == columns[0]
-            elif start < PIX + PIX // 4:
-                hit = position == columns[1]
-            else:
-                hit = (position == columns[2]) | (position == columns[3])
-            value = jnp.tanh(half_score - 1.0) + jnp.where(hit, -1.0, 1.0)
-            dscore[start : start + size, :] = value.astype(jnp.bfloat16)
-        level_grad[...] = matmul(dscore[...], features, NN)
-        grad_rows[...] += matmul(dscore[...], pyramid[...], TN)
+        for start in range(CHUNK, PIX, CHUNK):
+            score(start, CHUNK, columns[:1])
+        score(PIX, PIX // 4, columns[1:2])
+        score(PIX + PIX // 4, PAD - PIX // 4, columns[2:])
+        level_grad[PIX:CELLS, :] = matmul(dscore[PIX:CELLS, :], features, NN)
+        level_grad[0:PIX, :] = matmul(dscore[0:PIX, :], features, NN)
         coarse = level_grad[PIX:CELLS, :].astype(jnp.bfloat16)
         gradient = level_grad[0:PIX, :] + matmul(unpool[...], coarse, NN)
         level_grad[0:PIX, :] = gradient * 2.0**-5
-        convolve_back(level_grad, weight_back, moved, total_two, first)
+        spread_back(level_grad, moved)
+        feat_two[...] = convolve(spread_two, first_row(jnp.minimum(k + 1, SLOTS - 1)), weight)
+        grad_rows[...] += matmul(dscore[...], pyramid[...], TN)
+        convolve_back(moved, weight_back, total_two, first_row(k))
 
     def slot(k, carry):
         pl.when(k < count)(lambda: work_slot(k))
@@ -285,7 +300,8 @@
     to_sibling[0:TR] = rows(total_two, at(side), TR).astype(jnp.bfloat16)
     to_sibling[TR : 2 * TR] = rows(total_two, at(-side), TR).astype(jnp.bfloat16)
     to_sibling[2 * TR : 2 * TR + 1] = rows(total_two, edge(side)).astype(jnp.bfloat16)
-    convolve_back(grad_rows, weight_back, moved, total_one, 0)
+    spread_back(grad_rows, moved)
+    convolve_back(moved, weight_back, total_one, 0)
     facing = jnp.where(side > 0, TR + 1, 0)
     outer = jnp.where(side > 0, 0, TR + 1)
     to_sibling[2 * TR + 1 : 2 * TR + 2] = rows(total_one, facing).astype(jnp.bfloat16)
@@ -325,17 +341,18 @@
     row_block = (1, TC, CIN)
     weight = conv_weight.reshape(9 * CIN, CH)
     direct = send(frame_two, "ahead")
-    near_in, far_in, inward = call(
+    near = send(frame_two, "behind")
+    cross_in, far_in, inward = call(
         rows_kernel,
-        [((TR + 1, TC, CIN), bf16), (row_block, bf16), (row_block, bf16)],
-        [pltpu.SemaphoreType.DMA((4,))],
+        [(row_block, bf16)] * 3,
+        [pltpu.SemaphoreType.DMA((3,))],
         [frame_one, frame_two],
         "rows",
         [pltpu.HBM] * 2,
         [pltpu.HBM] * 3,
     )
-    near = send(near_in, "behind")
     far = send(far_in, "far")
+    cross = send(cross_in, "cross")
     pool, unpool = call(
         tables_kernel,
         [((PAD, PIX), bf16), ((PIX, PAD), bf16)],
@@ -345,7 +362,9 @@
         [],
         [pltpu.VMEM] * 2,
     )
-    inward, far, pool, unpool = lax.optimization_barrier((inward, far, pool, unpool))
+    inward, far, cross, pool, unpool = lax.optimization_barrier(
+        (inward, far, cross, pool, unpool)
+    )
     facing_row = jnp.where(side > 0, TR - 1, 0)
     direct_row = lax.dynamic_slice_in_dim(direct, facing_row, 1, 0)
     payload = jnp.concatenate([frame_two, near, inward, direct_row])
@@ -369,6 +388,7 @@
         ((TR + 2, TC, CIN), bf16),
         (((TR + 2) * TC, 3 * CIN), bf16),
         ((PIX, CH), bf16),
+        ((PIX, CH), bf16),
         ((CELLS, CH), bf16),
         ((CELLS, PIX), bf16),
         ((CELLS, CH), f32),
@@ -383,10 +403,10 @@
         [pltpu.VMEM(*out) for out in outs]
         + [pltpu.SemaphoreType.DMA((len(outs),))]
         + [pltpu.VMEM(*item) for item in scratch],
-        [partners, counts, frame_one, frame_two, near, direct, far]
+        [partners, counts, frame_one, frame_two, near, direct, far, cross]
         + [from_sibling, weight, pool, unpool, targets],
         "work",
-        [pltpu.SMEM] * 2 + [pltpu.VMEM] * 10,
+        [pltpu.SMEM] * 2 + [pltpu.VMEM] * 11,
         [pltpu.HBM] * len(outs),
     )
     row = lax.broadcasted_iota(jnp.int32, (TR, 1, 1), 0)

time: 70 us -> 71 us (1.014)
  other arithmetic: 1.42 us -> 4.11 us
  waiting for transfers between devices: 14 us -> 12.7 us
  Pallas kernels: 23 us -> 22.1 us
    ppermute x8 -> x9, waiting for transfers between devices: 14 us -> 12.7 us  [send(): return lax.ppermute(block, 'tile', route[name])]
    convert_element_type x1, other arithmetic: 0.06 us -> 1.01 us  [on_device(): ahead_in = (ahead + back_sibling[TR:2 * TR].astype(f32)).astype(bf16)]
    convert_element_type x1, other arithmetic: 1.07 us -> 2.02 us  [on_device(): return (grad_one.astype(bf16), grad_two.astype(bf16))]
    pallas_call x3, Pallas kernels: 23 us -> 22.1 us  [call(): pl.pallas_call(kernel, in_specs=[pl.BlockSpec(memory_space=space) for spa...]
    broadcast_in_dim x1, other arithmetic: 0.01 us -> 0.8 us  [on_device(): edge = jnp.where(facing, back_sibling[2 * TR:2 * TR + 1].astype(f32), 0.0)]
    ppermute x8 -> x9, starting transfers between devices: 25.9 us -> 26.3 us  [send(): return lax.ppermute(block, 'tile', route[name])]
    unnamed x20 -> x16, local copies, waits for them, and re-layouts: 3.76 us -> 3.71 us
  transfers between devices with their start and end apart: 8 -> 9, of which waited for: 4 -> 3; matrix products, arithmetic and copies ran while one was open for 0% -> 3% of each run, Pallas kernels for 2% -> 2%
where the time goes in v6:
time: 71 us; the launch traced here: 70.4 us
  starting transfers between devices  26.3 us (37%)
  Pallas kernels  22.1 us (31%)
  waiting for transfers between devices  12.7 us (18%)
  other arithmetic  4.11 us (6%)
  local copies, waits for them, and re-layouts  3.71 us (5%)
  between operations  1.49 us (2%)
    ppermute x9, starting transfers between devices, send(): return lax.ppermute(block, 'tile', route[name])  26.3 us
    pallas_call x3, Pallas kernels, call(): pl.pallas_call(kernel, in_specs=[pl.BlockSpec(memory_space=space) for spa...  22.1 us
    ppermute x9, waiting for transfers between devices, send(): return lax.ppermute(block, 'tile', route[name])  12.7 us
    unnamed x16, local copies, waits for them, and re-layouts  3.71 us
    convert_element_type x1, other arithmetic, on_device(): return (grad_one.astype(bf16), grad_two.astype(bf16))  2.02 us
  transfers between devices with their start and end apart: 9, of which 3 were waited for; matrix products, arithmetic and copies ran while one was open for 3% of the time, Pallas kernels for 2%

profile of v6, /device:TPU:9, one launch (start us, length us, event | category | flops | bytes accessed | tf_op | source)
XLA Modules:
  0.0 70.4 jit_solution(9463571155528671363)
XLA Ops:
  0.6 3.0 %collective-permute-start.1 = (bf16[8,128,128]{2,1,0:T(8,128)(2,1)}, bf16[8,128,128]{2,1,0:T(8,128)(2,1)S(1)}, u32[]{:S(2)}, u32[]{:S(2)}) collective-permute-start(bf16[8,128,128]{2,1,0:T(8,128)(2,1)} %own_two.1), channel_id=1, source_target_pairs={{0,2},{2,4},{3,1},{4,6},{5,3},{6,8},{7,5},{8,10},{9,7},{10,12},{11... | collective-permute-start | bytes 786440 | tf_op jit(solution)/shard_map/ppermute | solution.py:339
  3.7 2.2 %collective-permute-start = (bf16[8,128,128]{2,1,0:T(8,128)(2,1)}, bf16[8,128,128]{2,1,0:T(8,128)(2,1)S(1)}, u32[]{:S(2)}, u32[]{:S(2)}) collective-permute-start(bf16[8,128,128]{2,1,0:T(8,128)(2,1)} %own_two.1), channel_id=1, source_target_pairs={{1,3},{2,0},{3,5},{4,2},{5,7},{6,4},{7,9},{8,6},{9,11},{10,8},{11,... | collective-permute-start | bytes 786440 | tf_op jit(solution)/shard_map/ppermute | solution.py:339
  5.9 1.0 %copy-done = bf16[8,128,128]{2,1,0:T(8,128)(2,1)S(1)} copy-done((bf16[8,128,128]{2,1,0:T(8,128)(2,1)S(1)}, bf16[8,128,128]{2,1,0:T(8,128)(2,1)}, u32[]{:S(2)}) %copy-start) | copy-done | bytes 262168
  6.9 0.9 %copy-done.2 = bf16[8,128,128]{2,1,0:T(8,128)(2,1)S(1)} copy-done((bf16[8,128,128]{2,1,0:T(8,128)(2,1)S(1)}, bf16[8,128,128]{2,1,0:T(8,128)(2,1)}, u32[]{:S(2)}) %copy-start.2) | copy-done | bytes 262168
  7.8 0.1 rows.1
  8.0 5.2 %collective-permute-start.2 = (bf16[1,128,128]{2,1,0:T(8,128)(2,1)S(1)}, bf16[1,128,128]{2,1,0:T(8,128)(2,1)S(1)}, u32[]{:S(2)}, u32[]{:S(2)}) collective-permute-start(bf16[1,128,128]{2,1,0:T(8,128)(2,1)S(1)} %get-tuple-element.19), channel_id=1, source_target_pairs={{1,4},{3,6},{4,1},{5,8},{6,3},{7,10},{8,5},{9,12},{10,7},{11,14},{... | collective-permute-start | bytes 98312 | tf_op jit(solution)/shard_map/ppermute | solution.py:339
  13.2 1.9 %collective-permute-start.3 = (bf16[1,128,128]{2,1,0:T(8,128)(2,1)S(1)}, bf16[1,128,128]{2,1,0:T(8,128)(2,1)S(1)}, u32[]{:S(2)}, u32[]{:S(2)}) collective-permute-start(bf16[1,128,128]{2,1,0:T(8,128)(2,1)S(1)} %get-tuple-element.20), channel_id=1, source_target_pairs={{1,2},{2,1},{3,4},{4,3},{5,6},{6,5},{7,8},{8,7},{9,10},{10,9},{11,... | collective-permute-start | bytes 98312 | tf_op jit(solution)/shard_map/ppermute | solution.py:339
  15.1 1.0 %tables.1 = (bf16[384,1024]{1,0:T(8,128)(2,1)S(1)}, bf16[1024,384]{1,0:T(8,128)(2,1)S(1)}) custom-call(), custom_call_target="tpu_custom_call" | custom-call | tf_op jit(solution)/shard_map/tables/pallas_call | solution.py:321
  16.2 0.9 %copy-done.4 = bf16[384,1024]{1,0:T(8,128)(2,1)} copy-done((bf16[384,1024]{1,0:T(8,128)(2,1)}, bf16[384,1024]{1,0:T(8,128)(2,1)S(1)}, u32[]{:S(2)}) %copy-start.4) | copy-done | bytes 786456
  17.0 0.9 %copy-done.5 = bf16[1024,384]{1,0:T(8,128)(2,1)} copy-done((bf16[1024,384]{1,0:T(8,128)(2,1)}, bf16[1024,384]{1,0:T(8,128)(2,1)S(1)}, u32[]{:S(2)}) %copy-start.5) | copy-done | bytes 786456
  17.9 0.5 collective-permute-done.3.cross
  18.5 0.1 pad_maximum_fusion
  18.6 0.2 collective-permute-start.4
  19.5 1.2 %collective-permute-done.4.from_sibling = bf16[18,128,128]{2,1,0:T(8,128)(2,1)S(1)} collective-permute-done((bf16[18,128,128]{2,1,0:T(8,128)(2,1)S(1)}, bf16[18,128,128]{2,1,0:T(8,128)(2,1)S(1)}, u32[]{:S(2)}, u32[]{:S(2)}) %collective-permute-start.4) | collective-permute-done | bytes 589856 | tf_op jit(solution)/shard_map/ppermute | solution.py:339
  20.7 21.0 %work.1 = (bf16[19,128,128]{2,1,0:T(8,128)(2,1)}, f32[8,128,128]{2,1,0:T(8,128)S(1)}, f32[8,128,128]{2,1,0:T(8,128)S(1)}, bf16[1,128,128]{2,1,0:T(8,128)(2,1)S(1...) custom-call(s32[1,4]{1,0:T(1,128)S(1)} %copy-done.7, s32[1]{0:T(128)S(6)} %copy.8.counts, ...), custom_call_target="tpu_custom_call" | custom-call | tf_op jit(solution)/shard_map/work/pallas_call | solution.py:321
  41.6 5.0 %collective-permute-start.5 = (bf16[19,128,128]{2,1,0:T(8,128)(2,1)}, bf16[19,128,128]{2,1,0:T(8,128)(2,1)}, u32[]{:S(2)}, u32[]{:S(2)}) collective-permute-start(bf16[19,128,128]{2,1,0:T(8,128)(2,1)} %get-tuple-element.29), channel_id=1, source_target_pairs={{0,1},{1,0},{2,3},{3,2},{4,5},{5,4},{6,7},{7,6},{8,9},{9,8},{10,11... | collective-permute-start | bytes 1867784 | tf_op jit(solution)/shard_map/ppermute | solution.py:339
  46.6 3.5 %collective-permute-start.8 = (bf16[1,128,128]{2,1,0:T(8,128)(2,1)S(1)}, bf16[1,128,128]{2,1,0:T(8,128)(2,1)S(1)}, u32[]{:S(2)}, u32[]{:S(2)}) collective-permute-start(bf16[1,128,128]{2,1,0:T(8,128)(2,1)S(1)} %get-tuple-element.33), channel_id=1, source_target_pairs={{1,4},{3,6},{4,1},{5,8},{6,3},{7,10},{8,5},{9,12},{10,7},{11,14},{... | collective-permute-start | bytes 98312 | tf_op jit(solution)/shard_map/ppermute | solution.py:339
  50.1 0.8 %fusion = (f32[128,128]{1,0:T(8,128)S(1)}, bf16[1,128,128]{2,1,0:T(8,128)(2,1)S(1)}, f32[128,128]{1,0:T(8,128)S(1)}) fusion(bf16[19,128,128]{2,1,0:T(8,128)(2,1)} %collective-permute-done.5), kind=kLoop, calls=%fused_computation.7 | loop fusion | flops 32768 | bytes 262144 | tf_op jit(solution)/shard_map/jit(_where)/broadcast_in_dim | solution.py:417
  50.9 1.0 %add_convert_fusion.3 = bf16[8,128,128]{2,1,0:T(8,128)(2,1)S(1)} fusion(f32[8,128,128]{2,1,0:T(8,128)S(1)} %get-tuple-element.30, bf16[19,128,128]{2,1,0:T(8,128)(2,1)} %collective-permute-done.5), kind=kLoop, calls=%fused_computation.4 | loop fusion | flops 393216 | bytes 1048576 | tf_op jit(solution)/shard_map/convert_element_type | solution.py:416
  52.0 3.0 %collective-permute-start.6 = (bf16[9,128,128]{2,1,0:T(8,128)(2,1)S(1)}, bf16[9,128,128]{2,1,0:T(8,128)(2,1)S(1)}, u32[]{:S(2)}, u32[]{:S(2)}) collective-permute-start(bf16[9,128,128]{2,1,0:T(8,128)(2,1)S(1)} %pad_maximum_fusion.1), channel_id=1, source_target_pairs={{0,2},{2,4},{3,1},{4,6},{5,3},{6,8},{7,5},{8,10},{9,7},{10,12},{11... | collective-permute-start | bytes 884744 | tf_op jit(solution)/shard_map/ppermute | solution.py:339
  55.0 0.1 add_convert_fusion.1
  55.1 2.3 %collective-permute-start.7 = (bf16[8,128,128]{2,1,0:T(8,128)(2,1)S(1)}, bf16[8,128,128]{2,1,0:T(8,128)(2,1)S(1)}, u32[]{:S(2)}, u32[]{:S(2)}) collective-permute-start(bf16[8,128,128]{2,1,0:T(8,128)(2,1)S(1)} %add_convert_fusion.1), channel_id=1, source_target_pairs={{1,3},{2,0},{3,5},{4,2},{5,7},{6,4},{7,9},{8,6},{9,11},{10,8},{11,... | collective-permute-start | bytes 786440 | tf_op jit(solution)/shard_map/ppermute | solution.py:339
  57.4 11.0 %collective-permute-done.6 = bf16[9,128,128]{2,1,0:T(8,128)(2,1)S(1)} collective-permute-done((bf16[9,128,128]{2,1,0:T(8,128)(2,1)S(1)}, bf16[9,128,128]{2,1,0:T(8,128)(2,1)S(1)}, u32[]{:S(2)}, u32[]{:S(2)}) %collective-permute-start.6) | collective-permute-done | bytes 294944 | tf_op jit(solution)/shard_map/ppermute | solution.py:339
  68.4 2.0 %add_convert_fusion = (bf16[8,128,128]{2,1,0:T(8,128)(2,1)}, bf16[8,128,128]{2,1,0:T(8,128)(2,1)}) fusion(bf16[8,128,128]{2,1,0:T(8,128)(2,1)S(1)} %collective-permute-done.7, f32[8,128,128]{2,1,0:T(8,128)S(1)} %get-tuple-element.31, bf16[9,128,128]{2,1,0:T(8,128)(2,1)S(1)} %collective-permute-done.6, bf16[19,128,128]{2,1,0:T(8,128)(2,1)} %collective-permute-done.5, ...), kind=kLoop, calls=%fused_computation.1 | loop fusion | flops 1835008 | bytes 2555920 | tf_op jit(solution)/shard_map/convert_element_type | solution.py:431
  (24 shorter events, 0.1 us)
Async XLA Ops:
  0.6 17.8 %collective-permute-start.1 = (bf16[8,128,128]{2,1,0:T(8,128)(2,1)}, bf16[8,128,128]{2,1,0:T(8,128)(2,1)S(1)}, u32[]{:S(2)}, u32[]{:S(2)}) collective-permute-start(bf16[8,128,128]{2,1,0:T(8,128)(2,1)} %own_two.1), channel_id=1, source_target_pairs={{0,2},{2,4},{3,1},{4,6},{5,3},{6,8},{7,5},{8,10},{9,7},{10,12},{11... | collective-permute-start | bytes 786440 | tf_op jit(solution)/shard_map/ppermute | solution.py:339
  3.7 14.8 %collective-permute-start = (bf16[8,128,128]{2,1,0:T(8,128)(2,1)}, bf16[8,128,128]{2,1,0:T(8,128)(2,1)S(1)}, u32[]{:S(2)}, u32[]{:S(2)}) collective-permute-start(bf16[8,128,128]{2,1,0:T(8,128)(2,1)} %own_two.1), channel_id=1, source_target_pairs={{1,3},{2,0},{3,5},{4,2},{5,7},{6,4},{7,9},{8,6},{9,11},{10,8},{11,... | collective-permute-start | bytes 786440 | tf_op jit(solution)/shard_map/ppermute | solution.py:339
  5.9 1.0 %copy-start = (bf16[8,128,128]{2,1,0:T(8,128)(2,1)S(1)}, bf16[8,128,128]{2,1,0:T(8,128)(2,1)}, u32[]{:S(2)}) copy-start(bf16[8,128,128]{2,1,0:T(8,128)(2,1)} %own_two.1) | copy-start | bytes 786436
  6.9 0.9 %copy-start.2 = (bf16[8,128,128]{2,1,0:T(8,128)(2,1)S(1)}, bf16[8,128,128]{2,1,0:T(8,128)(2,1)}, u32[]{:S(2)}) copy-start(bf16[8,128,128]{2,1,0:T(8,128)(2,1)} %own_one.1) | copy-start | bytes 786436
  7.8 10.6 %copy-start.1 = (bf16[8,128,128]{2,1,0:T(8,128)(2,1)S(1)}, bf16[8,128,128]{2,1,0:T(8,128)(2,1)}, u32[]{:S(2)}) copy-start(bf16[8,128,128]{2,1,0:T(8,128)(2,1)} %own_two.1) | copy-start | bytes 786436
  8.0 10.0 %collective-permute-start.2 = (bf16[1,128,128]{2,1,0:T(8,128)(2,1)S(1)}, bf16[1,128,128]{2,1,0:T(8,128)(2,1)S(1)}, u32[]{:S(2)}, u32[]{:S(2)}) collective-permute-start(bf16[1,128,128]{2,1,0:T(8,128)(2,1)S(1)} %get-tuple-element.19), channel_id=1, source_target_pairs={{1,4},{3,6},{4,1},{5,8},{6,3},{7,10},{8,5},{9,12},{10,7},{11,14},{... | collective-permute-start | bytes 98312 | tf_op jit(solution)/shard_map/ppermute | solution.py:339
  13.2 5.2 %collective-permute-start.3 = (bf16[1,128,128]{2,1,0:T(8,128)(2,1)S(1)}, bf16[1,128,128]{2,1,0:T(8,128)(2,1)S(1)}, u32[]{:S(2)}, u32[]{:S(2)}) collective-permute-start(bf16[1,128,128]{2,1,0:T(8,128)(2,1)S(1)} %get-tuple-element.20), channel_id=1, source_target_pairs={{1,2},{2,1},{3,4},{4,3},{5,6},{6,5},{7,8},{8,7},{9,10},{10,9},{11,... | collective-permute-start | bytes 98312 | tf_op jit(solution)/shard_map/ppermute | solution.py:339
  16.1 0.9 %copy-start.4 = (bf16[384,1024]{1,0:T(8,128)(2,1)}, bf16[384,1024]{1,0:T(8,128)(2,1)S(1)}, u32[]{:S(2)}) copy-start(bf16[384,1024]{1,0:T(8,128)(2,1)S(1)} %get-tuple-element.26.pool) | copy-start | bytes 2359300
  17.0 0.9 %copy-start.5 = (bf16[1024,384]{1,0:T(8,128)(2,1)}, bf16[1024,384]{1,0:T(8,128)(2,1)S(1)}, u32[]{:S(2)}) copy-start(bf16[1024,384]{1,0:T(8,128)(2,1)S(1)} %get-tuple-element.27.unpool) | copy-start | bytes 2359300
  18.5 2.2 %copy-start.3 = (bf16[8,128,128]{2,1,0:T(8,128)(2,1)S(1)}, bf16[8,128,128]{2,1,0:T(8,128)(2,1)}, u32[]{:S(2)}) copy-start(bf16[8,128,128]{2,1,0:T(8,128)(2,1)} %own_one.1) | copy-start | bytes 786436
  18.5 2.2 %copy-start.6 = (s32[8,128]{1,0:T(8,128)S(1)}, s32[8,128]{1,0:T(8,128)}, u32[]{:S(2)}) copy-start(s32[8,128]{1,0:T(8,128)} %targets.1) | copy-start | bytes 12292
  18.6 2.1 %collective-permute-start.4 = (bf16[18,128,128]{2,1,0:T(8,128)(2,1)S(1)}, bf16[18,128,128]{2,1,0:T(8,128)(2,1)S(1)}, u32[]{:S(2)}, u32[]{:S(2)}) collective-permute-start(bf16[18,128,128]{2,1,0:T(8,128)(2,1)S(1)} %pad_maximum_fusion), channel_id=1, source_target_pairs={{0,1},{1,0},{2,3},{3,2},{4,5},{5,4},{6,7},{7,6},{8,9},{9,8},{10,11... | collective-permute-start | bytes 1769480 | tf_op jit(solution)/shard_map/ppermute | solution.py:339
  19.4 1.2 %copy-start.7 = (s32[1,4]{1,0:T(1,128)S(1)}, s32[1,4]{1,0:T(1,128)}, u32[]{:S(2)}) copy-start(s32[1,4]{1,0:T(1,128)} %partners.1) | copy-start | bytes 52
  41.6 8.4 %collective-permute-start.5 = (bf16[19,128,128]{2,1,0:T(8,128)(2,1)}, bf16[19,128,128]{2,1,0:T(8,128)(2,1)}, u32[]{:S(2)}, u32[]{:S(2)}) collective-permute-start(bf16[19,128,128]{2,1,0:T(8,128)(2,1)} %get-tuple-element.29), channel_id=1, source_target_pairs={{0,1},{1,0},{2,3},{3,2},{4,5},{5,4},{6,7},{7,6},{8,9},{9,8},{10,11... | collective-permute-start | bytes 1867784 | tf_op jit(solution)/shard_map/ppermute | solution.py:339
  46.6 10.8 %collective-permute-start.8 = (bf16[1,128,128]{2,1,0:T(8,128)(2,1)S(1)}, bf16[1,128,128]{2,1,0:T(8,128)(2,1)S(1)}, u32[]{:S(2)}, u32[]{:S(2)}) collective-permute-start(bf16[1,128,128]{2,1,0:T(8,128)(2,1)S(1)} %get-tuple-element.33), channel_id=1, source_target_pairs={{1,4},{3,6},{4,1},{5,8},{6,3},{7,10},{8,5},{9,12},{10,7},{11,14},{... | collective-permute-start | bytes 98312 | tf_op jit(solution)/shard_map/ppermute | solution.py:339
  52.0 16.5 %collective-permute-start.6 = (bf16[9,128,128]{2,1,0:T(8,128)(2,1)S(1)}, bf16[9,128,128]{2,1,0:T(8,128)(2,1)S(1)}, u32[]{:S(2)}, u32[]{:S(2)}) collective-permute-start(bf16[9,128,128]{2,1,0:T(8,128)(2,1)S(1)} %pad_maximum_fusion.1), channel_id=1, source_target_pairs={{0,2},{2,4},{3,1},{4,6},{5,3},{6,8},{7,5},{8,10},{9,7},{10,12},{11... | collective-permute-start | bytes 884744 | tf_op jit(solution)/shard_map/ppermute | solution.py:339
  55.1 13.3 %collective-permute-start.7 = (bf16[8,128,128]{2,1,0:T(8,128)(2,1)S(1)}, bf16[8,128,128]{2,1,0:T(8,128)(2,1)S(1)}, u32[]{:S(2)}, u32[]{:S(2)}) collective-permute-start(bf16[8,128,128]{2,1,0:T(8,128)(2,1)S(1)} %add_convert_fusion.1), channel_id=1, source_target_pairs={{1,3},{2,0},{3,5},{4,2},{5,7},{6,4},{7,9},{8,6},{9,11},{10,8},{11,... | collective-permute-start | bytes 786440 | tf_op jit(solution)/shard_map/ppermute | solution.py:339

commit v7 on v6

--- a/solution.py
+++ b/solution.py
@@ -20,7 +20,7 @@
 PAD = 384
 CELLS = PIX + PAD
 CHUNK = 256
-LIMIT = 50
+LIMIT = 49
 WIN = 2 * RADIUS * TR + TR + 2
 
 NN = (((1,), (0,)), ((), ()))
@@ -346,7 +346,7 @@
         rows_kernel,
         [(row_block, bf16)] * 3,
         [pltpu.SemaphoreType.DMA((3,))],
-        [frame_one, frame_two],
+        [pltpu.with_memory_space_constraint(x, pltpu.HBM) for x in (frame_one, frame_two)],
         "rows",
         [pltpu.HBM] * 2,
         [pltpu.HBM] * 3,

time: 71 us -> 70.3 us (level)
  Pallas kernels: 22.1 us -> 27.4 us
  starting transfers between devices: 26.3 us -> 22.3 us
  local copies, waits for them, and re-layouts: 3.71 us -> 1.82 us
    pallas_call x3, Pallas kernels: 22.1 us -> 27.4 us  [call(): pl.pallas_call(kernel, in_specs=[pl.BlockSpec(memory_space=space) for spa...]
    ppermute x9, starting transfers between devices: 26.3 us -> 22.3 us  [send(): return lax.ppermute(block, 'tile', route[name])]
    unnamed x16 -> x14, local copies, waits for them, and re-layouts: 3.71 us -> 1.82 us
    ppermute x9, waiting for transfers between devices: 12.7 us -> 12 us  [send(): return lax.ppermute(block, 'tile', route[name])]
  transfers between devices with their start and end apart: 9 -> 9, of which waited for: 3 -> 3; matrix products, arithmetic and copies ran while one was open for 3% -> 3% of each run, Pallas kernels for 2% -> 3%
where the time goes in v7:
time: 70.3 us; the launch traced here: 69.1 us
  Pallas kernels  27.4 us (39%)
  starting transfers between devices  22.3 us (32%)
  waiting for transfers between devices  12 us (17%)
  other arithmetic  4.1 us (6%)
  local copies, waits for them, and re-layouts  1.82 us (3%)
  between operations  1.5 us (2%)
    pallas_call x3, Pallas kernels, call(): pl.pallas_call(kernel, in_specs=[pl.BlockSpec(memory_space=space) for spa...  27.4 us
    ppermute x9, starting transfers between devices, send(): return lax.ppermute(block, 'tile', route[name])  22.3 us
    ppermute x9, waiting for transfers between devices, send(): return lax.ppermute(block, 'tile', route[name])  12 us
    convert_element_type x1, other arithmetic, on_device(): return (grad_one.astype(bf16), grad_two.astype(bf16))  2.01 us
    unnamed x14, local copies, waits for them, and re-layouts  1.82 us
  transfers between devices with their start and end apart: 9, of which 3 were waited for; matrix products, arithmetic and copies ran while one was open for 3% of the time, Pallas kernels for 3%

profile of v7, /device:TPU:9, one launch (start us, length us, event | category | flops | bytes accessed | tf_op | source)
XLA Modules:
  0.0 69.1 jit_solution(15363535074466626742)
XLA Ops:
  0.6 3.2 %collective-permute-start.1 = (bf16[8,128,128]{2,1,0:T(8,128)(2,1)}, bf16[8,128,128]{2,1,0:T(8,128)(2,1)S(1)}, u32[]{:S(2)}, u32[]{:S(2)}) collective-permute-start(bf16[8,128,128]{2,1,0:T(8,128)(2,1)} %own_two.1), channel_id=1, source_target_pairs={{0,2},{2,4},{3,1},{4,6},{5,3},{6,8},{7,5},{8,10},{9,7},{10,12},{11... | collective-permute-start | bytes 786440 | tf_op jit(solution)/shard_map/ppermute | solution.py:339
  3.8 2.2 %collective-permute-start = (bf16[8,128,128]{2,1,0:T(8,128)(2,1)}, bf16[8,128,128]{2,1,0:T(8,128)(2,1)S(1)}, u32[]{:S(2)}, u32[]{:S(2)}) collective-permute-start(bf16[8,128,128]{2,1,0:T(8,128)(2,1)} %own_two.1), channel_id=1, source_target_pairs={{1,3},{2,0},{3,5},{4,2},{5,7},{6,4},{7,9},{8,6},{9,11},{10,8},{11,... | collective-permute-start | bytes 786440 | tf_op jit(solution)/shard_map/ppermute | solution.py:339
  6.1 0.8 %rows.1 = (bf16[1,128,128]{2,1,0:T(8,128)(2,1)S(1)}, bf16[1,128,128]{2,1,0:T(8,128)(2,1)S(1)}, bf16[1,128,128]{2,1,0:T(8,128)(2,1)S(1)}) custom-call(bf16[8,128,128]{2,1,0:T(8,128)(2,1)} %own_one.1, bf16[8,128,128]{2,1,0:T(8,128)(2,1)} %own_two.1), custom_call_target="tpu_custom_call" | custom-call | tf_op jit(solution)/shard_map/rows/pallas_call | solution.py:321
  6.9 5.2 %collective-permute-start.2 = (bf16[1,128,128]{2,1,0:T(8,128)(2,1)S(1)}, bf16[1,128,128]{2,1,0:T(8,128)(2,1)S(1)}, u32[]{:S(2)}, u32[]{:S(2)}) collective-permute-start(bf16[1,128,128]{2,1,0:T(8,128)(2,1)S(1)} %get-tuple-element.19), channel_id=1, source_target_pairs={{1,4},{3,6},{4,1},{5,8},{6,3},{7,10},{8,5},{9,12},{10,7},{11,14},{... | collective-permute-start | bytes 98312 | tf_op jit(solution)/shard_map/ppermute | solution.py:339
  12.1 1.9 %collective-permute-start.3 = (bf16[1,128,128]{2,1,0:T(8,128)(2,1)S(1)}, bf16[1,128,128]{2,1,0:T(8,128)(2,1)S(1)}, u32[]{:S(2)}, u32[]{:S(2)}) collective-permute-start(bf16[1,128,128]{2,1,0:T(8,128)(2,1)S(1)} %get-tuple-element.20), channel_id=1, source_target_pairs={{1,2},{2,1},{3,4},{4,3},{5,6},{6,5},{7,8},{8,7},{9,10},{10,9},{11,... | collective-permute-start | bytes 98312 | tf_op jit(solution)/shard_map/ppermute | solution.py:339
  14.1 1.0 %tables.1 = (bf16[384,1024]{1,0:T(8,128)(2,1)S(1)}, bf16[1024,384]{1,0:T(8,128)(2,1)S(1)}) custom-call(), custom_call_target="tpu_custom_call" | custom-call | tf_op jit(solution)/shard_map/tables/pallas_call | solution.py:321
  15.1 0.9 %copy-done.2 = bf16[384,1024]{1,0:T(8,128)(2,1)} copy-done((bf16[384,1024]{1,0:T(8,128)(2,1)}, bf16[384,1024]{1,0:T(8,128)(2,1)S(1)}, u32[]{:S(2)}) %copy-start.2) | copy-done | bytes 786456
  16.0 0.9 %copy-done.3 = bf16[1024,384]{1,0:T(8,128)(2,1)} copy-done((bf16[1024,384]{1,0:T(8,128)(2,1)}, bf16[1024,384]{1,0:T(8,128)(2,1)S(1)}, u32[]{:S(2)}) %copy-start.3) | copy-done | bytes 786456
  16.9 0.6 collective-permute-done.3.cross
  17.5 0.0 copy-start.4
  17.5 0.1 pad_maximum_fusion
  17.6 0.1 collective-permute-start.4
  18.4 1.3 %collective-permute-done.4.from_sibling = bf16[18,128,128]{2,1,0:T(8,128)(2,1)S(1)} collective-permute-done((bf16[18,128,128]{2,1,0:T(8,128)(2,1)S(1)}, bf16[18,128,128]{2,1,0:T(8,128)(2,1)S(1)}, u32[]{:S(2)}, u32[]{:S(2)}) %collective-permute-start.4) | collective-permute-done | bytes 589856 | tf_op jit(solution)/shard_map/ppermute | solution.py:339
  19.7 25.6 %work.1 = (bf16[19,128,128]{2,1,0:T(8,128)(2,1)}, f32[8,128,128]{2,1,0:T(8,128)S(1)}, f32[8,128,128]{2,1,0:T(8,128)S(1)}, bf16[1,128,128]{2,1,0:T(8,128)(2,1)S(1...) custom-call(s32[1,4]{1,0:T(1,128)S(1)} %copy-done.6, s32[1]{0:T(128)S(6)} %copy.8.counts, ...), custom_call_target="tpu_custom_call" | custom-call | tf_op jit(solution)/shard_map/work/pallas_call | solution.py:321
  45.3 0.2 collective-permute-start.5
  45.5 3.1 %collective-permute-start.8 = (bf16[1,128,128]{2,1,0:T(8,128)(2,1)S(1)}, bf16[1,128,128]{2,1,0:T(8,128)(2,1)S(1)}, u32[]{:S(2)}, u32[]{:S(2)}) collective-permute-start(bf16[1,128,128]{2,1,0:T(8,128)(2,1)S(1)} %get-tuple-element.33), channel_id=1, source_target_pairs={{1,4},{3,6},{4,1},{5,8},{6,3},{7,10},{8,5},{9,12},{10,7},{11,14},{... | collective-permute-start | bytes 98312 | tf_op jit(solution)/shard_map/ppermute | solution.py:339
  48.6 0.8 %fusion = (f32[128,128]{1,0:T(8,128)S(1)}, bf16[1,128,128]{2,1,0:T(8,128)(2,1)S(1)}, f32[128,128]{1,0:T(8,128)S(1)}) fusion(bf16[19,128,128]{2,1,0:T(8,128)(2,1)} %collective-permute-done.5), kind=kLoop, calls=%fused_computation.7 | loop fusion | flops 32768 | bytes 262144 | tf_op jit(solution)/shard_map/jit(_where)/broadcast_in_dim | solution.py:417
  49.4 1.0 %add_convert_fusion.3 = bf16[8,128,128]{2,1,0:T(8,128)(2,1)S(1)} fusion(f32[8,128,128]{2,1,0:T(8,128)S(1)} %get-tuple-element.30, bf16[19,128,128]{2,1,0:T(8,128)(2,1)} %collective-permute-done.5), kind=kLoop, calls=%fused_computation.4 | loop fusion | flops 393216 | bytes 1048576 | tf_op jit(solution)/shard_map/convert_element_type | solution.py:416
  50.5 4.3 %collective-permute-start.6 = (bf16[9,128,128]{2,1,0:T(8,128)(2,1)S(1)}, bf16[9,128,128]{2,1,0:T(8,128)(2,1)S(1)}, u32[]{:S(2)}, u32[]{:S(2)}) collective-permute-start(bf16[9,128,128]{2,1,0:T(8,128)(2,1)S(1)} %pad_maximum_fusion.1), channel_id=1, source_target_pairs={{0,2},{2,4},{3,1},{4,6},{5,3},{6,8},{7,5},{8,10},{9,7},{10,12},{11... | collective-permute-start | bytes 884744 | tf_op jit(solution)/shard_map/ppermute | solution.py:339
  54.8 0.1 add_convert_fusion.1
  54.9 2.0 %collective-permute-start.7 = (bf16[8,128,128]{2,1,0:T(8,128)(2,1)S(1)}, bf16[8,128,128]{2,1,0:T(8,128)(2,1)S(1)}, u32[]{:S(2)}, u32[]{:S(2)}) collective-permute-start(bf16[8,128,128]{2,1,0:T(8,128)(2,1)S(1)} %add_convert_fusion.1), channel_id=1, source_target_pairs={{1,3},{2,0},{3,5},{4,2},{5,7},{6,4},{7,9},{8,6},{9,11},{10,8},{11,... | collective-permute-start | bytes 786440 | tf_op jit(solution)/shard_map/ppermute | solution.py:339
  57.0 10.1 %collective-permute-done.6 = bf16[9,128,128]{2,1,0:T(8,128)(2,1)S(1)} collective-permute-done((bf16[9,128,128]{2,1,0:T(8,128)(2,1)S(1)}, bf16[9,128,128]{2,1,0:T(8,128)(2,1)S(1)}, u32[]{:S(2)}, u32[]{:S(2)}) %collective-permute-start.6) | collective-permute-done | bytes 294944 | tf_op jit(solution)/shard_map/ppermute | solution.py:339
  67.1 0.0 collective-permute-done.7
  67.1 2.0 %add_convert_fusion = (bf16[8,128,128]{2,1,0:T(8,128)(2,1)}, bf16[8,128,128]{2,1,0:T(8,128)(2,1)}) fusion(bf16[8,128,128]{2,1,0:T(8,128)(2,1)S(1)} %collective-permute-done.7, f32[8,128,128]{2,1,0:T(8,128)S(1)} %get-tuple-element.31, bf16[9,128,128]{2,1,0:T(8,128)(2,1)S(1)} %collective-permute-done.6, bf16[19,128,128]{2,1,0:T(8,128)(2,1)} %collective-permute-done.5, ...), kind=kLoop, calls=%fused_computation.1 | loop fusion | flops 1835008 | bytes 2555920 | tf_op jit(solution)/shard_map/convert_element_type | solution.py:431
  (22 shorter events, 0.1 us)
Async XLA Ops:
  0.6 16.9 %copy-start = (bf16[8,128,128]{2,1,0:T(8,128)(2,1)S(1)}, bf16[8,128,128]{2,1,0:T(8,128)(2,1)}, u32[]{:S(2)}) copy-start(bf16[8,128,128]{2,1,0:T(8,128)(2,1)} %own_two.1) | copy-start | bytes 786436
  0.6 16.8 %collective-permute-start.1 = (bf16[8,128,128]{2,1,0:T(8,128)(2,1)}, bf16[8,128,128]{2,1,0:T(8,128)(2,1)S(1)}, u32[]{:S(2)}, u32[]{:S(2)}) collective-permute-start(bf16[8,128,128]{2,1,0:T(8,128)(2,1)} %own_two.1), channel_id=1, source_target_pairs={{0,2},{2,4},{3,1},{4,6},{5,3},{6,8},{7,5},{8,10},{9,7},{10,12},{11... | collective-permute-start | bytes 786440 | tf_op jit(solution)/shard_map/ppermute | solution.py:339
  3.8 13.7 %collective-permute-start = (bf16[8,128,128]{2,1,0:T(8,128)(2,1)}, bf16[8,128,128]{2,1,0:T(8,128)(2,1)S(1)}, u32[]{:S(2)}, u32[]{:S(2)}) collective-permute-start(bf16[8,128,128]{2,1,0:T(8,128)(2,1)} %own_two.1), channel_id=1, source_target_pairs={{1,3},{2,0},{3,5},{4,2},{5,7},{6,4},{7,9},{8,6},{9,11},{10,8},{11,... | collective-permute-start | bytes 786440 | tf_op jit(solution)/shard_map/ppermute | solution.py:339
  6.9 10.0 %collective-permute-start.2 = (bf16[1,128,128]{2,1,0:T(8,128)(2,1)S(1)}, bf16[1,128,128]{2,1,0:T(8,128)(2,1)S(1)}, u32[]{:S(2)}, u32[]{:S(2)}) collective-permute-start(bf16[1,128,128]{2,1,0:T(8,128)(2,1)S(1)} %get-tuple-element.19), channel_id=1, source_target_pairs={{1,4},{3,6},{4,1},{5,8},{6,3},{7,10},{8,5},{9,12},{10,7},{11,14},{... | collective-permute-start | bytes 98312 | tf_op jit(solution)/shard_map/ppermute | solution.py:339
  12.1 5.3 %collective-permute-start.3 = (bf16[1,128,128]{2,1,0:T(8,128)(2,1)S(1)}, bf16[1,128,128]{2,1,0:T(8,128)(2,1)S(1)}, u32[]{:S(2)}, u32[]{:S(2)}) collective-permute-start(bf16[1,128,128]{2,1,0:T(8,128)(2,1)S(1)} %get-tuple-element.20), channel_id=1, source_target_pairs={{1,2},{2,1},{3,4},{4,3},{5,6},{6,5},{7,8},{8,7},{9,10},{10,9},{11,... | collective-permute-start | bytes 98312 | tf_op jit(solution)/shard_map/ppermute | solution.py:339
  15.1 0.9 %copy-start.2 = (bf16[384,1024]{1,0:T(8,128)(2,1)}, bf16[384,1024]{1,0:T(8,128)(2,1)S(1)}, u32[]{:S(2)}) copy-start(bf16[384,1024]{1,0:T(8,128)(2,1)S(1)} %get-tuple-element.26.pool) | copy-start | bytes 2359300
  16.0 0.9 %copy-start.3 = (bf16[1024,384]{1,0:T(8,128)(2,1)}, bf16[1024,384]{1,0:T(8,128)(2,1)S(1)}, u32[]{:S(2)}) copy-start(bf16[1024,384]{1,0:T(8,128)(2,1)S(1)} %get-tuple-element.27.unpool) | copy-start | bytes 2359300
  17.5 2.2 %copy-start.1 = (bf16[8,128,128]{2,1,0:T(8,128)(2,1)S(1)}, bf16[8,128,128]{2,1,0:T(8,128)(2,1)}, u32[]{:S(2)}) copy-start(bf16[8,128,128]{2,1,0:T(8,128)(2,1)} %own_one.1) | copy-start | bytes 786436
  17.5 2.2 %copy-start.4 = (bf16[3,3,128,256]{3,2,1,0:T(8,128)(2,1)S(1)}, bf16[3,3,128,256]{3,2,1,0:T(8,128)(2,1)}, u32[]{:S(2)}) copy-start(bf16[3,3,128,256]{3,2,1,0:T(8,128)(2,1)} %param.8) | copy-start | bytes 1769476
  17.5 2.2 %copy-start.5 = (s32[8,128]{1,0:T(8,128)S(1)}, s32[8,128]{1,0:T(8,128)}, u32[]{:S(2)}) copy-start(s32[8,128]{1,0:T(8,128)} %targets.1) | copy-start | bytes 12292
  17.6 2.1 %collective-permute-start.4 = (bf16[18,128,128]{2,1,0:T(8,128)(2,1)S(1)}, bf16[18,128,128]{2,1,0:T(8,128)(2,1)S(1)}, u32[]{:S(2)}, u32[]{:S(2)}) collective-permute-start(bf16[18,128,128]{2,1,0:T(8,128)(2,1)S(1)} %pad_maximum_fusion), channel_id=1, source_target_pairs={{0,1},{1,0},{2,3},{3,2},{4,5},{5,4},{6,7},{7,6},{8,9},{9,8},{10,11... | collective-permute-start | bytes 1769480 | tf_op jit(solution)/shard_map/ppermute | solution.py:339
  18.4 1.3 %copy-start.6 = (s32[1,4]{1,0:T(1,128)S(1)}, s32[1,4]{1,0:T(1,128)}, u32[]{:S(2)}) copy-start(s32[1,4]{1,0:T(1,128)} %partners.1) | copy-start | bytes 52
  45.3 3.3 %collective-permute-start.5 = (bf16[19,128,128]{2,1,0:T(8,128)(2,1)}, bf16[19,128,128]{2,1,0:T(8,128)(2,1)}, u32[]{:S(2)}, u32[]{:S(2)}) collective-permute-start(bf16[19,128,128]{2,1,0:T(8,128)(2,1)} %get-tuple-element.29), channel_id=1, source_target_pairs={{0,1},{1,0},{2,3},{3,2},{4,5},{5,4},{6,7},{7,6},{8,9},{9,8},{10,11... | collective-permute-start | bytes 1867784 | tf_op jit(solution)/shard_map/ppermute | solution.py:339
  45.5 11.4 %collective-permute-start.8 = (bf16[1,128,128]{2,1,0:T(8,128)(2,1)S(1)}, bf16[1,128,128]{2,1,0:T(8,128)(2,1)S(1)}, u32[]{:S(2)}, u32[]{:S(2)}) collective-permute-start(bf16[1,128,128]{2,1,0:T(8,128)(2,1)S(1)} %get-tuple-element.33), channel_id=1, source_target_pairs={{1,4},{3,6},{4,1},{5,8},{6,3},{7,10},{8,5},{9,12},{10,7},{11,14},{... | collective-permute-start | bytes 98312 | tf_op jit(solution)/shard_map/ppermute | solution.py:339
  50.5 16.6 %collective-permute-start.6 = (bf16[9,128,128]{2,1,0:T(8,128)(2,1)S(1)}, bf16[9,128,128]{2,1,0:T(8,128)(2,1)S(1)}, u32[]{:S(2)}, u32[]{:S(2)}) collective-permute-start(bf16[9,128,128]{2,1,0:T(8,128)(2,1)S(1)} %pad_maximum_fusion.1), channel_id=1, source_target_pairs={{0,2},{2,4},{3,1},{4,6},{5,3},{6,8},{7,5},{8,10},{9,7},{10,12},{11... | collective-permute-start | bytes 884744 | tf_op jit(solution)/shard_map/ppermute | solution.py:339
  54.9 12.2 %collective-permute-start.7 = (bf16[8,128,128]{2,1,0:T(8,128)(2,1)S(1)}, bf16[8,128,128]{2,1,0:T(8,128)(2,1)S(1)}, u32[]{:S(2)}, u32[]{:S(2)}) collective-permute-start(bf16[8,128,128]{2,1,0:T(8,128)(2,1)S(1)} %add_convert_fusion.1), channel_id=1, source_target_pairs={{1,3},{2,0},{3,5},{4,2},{5,7},{6,4},{7,9},{8,6},{9,11},{10,8},{11,... | collective-permute-start | bytes 786440 | tf_op jit(solution)/shard_map/ppermute | solution.py:339

commit v8 on v7

--- a/solution.py
+++ b/solution.py
@@ -20,7 +20,7 @@
 PAD = 384
 CELLS = PIX + PAD
 CHUNK = 256
-LIMIT = 49
+LIMIT = 193 << 18
 WIN = 2 * RADIUS * TR + TR + 2
 
 NN = (((1,), (0,)), ((), ()))
@@ -178,6 +178,7 @@
     sum_one,
     sum_two,
     sems,
+    move_sems,
     weight_back,
     labels,
     window,
@@ -204,17 +205,33 @@
     def edge(sign):
         return jnp.where(sign > 0, WIN - 1, 0)
 
-    for r in range(TR):
-        window[at(0) + r] = own_two[r]
-        window[at(2 * side) + r] = near[r]
-        window[at(-2 * side) + r] = direct[r]
-        window[at(side) + r] = from_sibling[r]
-        window[at(-side) + r] = from_sibling[TR + r]
-        window_one[1 + r] = own_one[r]
-    window[edge(side)] = from_sibling[2 * TR + 1]
-    window[edge(-side)] = far[0]
-    window_one[jnp.where(side > 0, TR + 1, 0)] = from_sibling[2 * TR]
-    window_one[jnp.where(side > 0, 0, TR + 1)] = cross[0]
+    def block(row):
+        return window.at[pl.ds(row, TR)]
+
+    def single(target, row):
+        return target.at[pl.ds(row, 1)]
+
+    def arrived(first, size=1):
+        return from_sibling.at[pl.ds(first, size)]
+
+    moves = [
+        (own_two, block(at(0))),
+        (near, block(at(2 * side))),
+        (direct, block(at(-2 * side))),
+        (arrived(0, TR), block(at(side))),
+        (arrived(TR, TR), block(at(-side))),
+        (arrived(2 * TR + 1), single(window, edge(side))),
+        (far, single(window, edge(-side))),
+        (own_one, window_one.at[pl.ds(1, TR)]),
+        (arrived(2 * TR), single(window_one, jnp.where(side > 0, TR + 1, 0))),
+        (cross, single(window_one, jnp.where(side > 0, 0, TR + 1))),
+    ]
+    moves = [
+        pltpu.make_async_copy(source, target, move_sems.at[n])
+        for n, (source, target) in enumerate(moves)
+    ]
+    for move in moves:
+        move.start()
     write_labels(targets, labels)
 
     for a in range(3):
@@ -223,6 +240,12 @@
                 (3 * a + b) * CIN : (3 * a + b + 1) * CIN, :
             ]
 
+    grad_rows[...] = jnp.zeros_like(grad_rows)
+    total_two[...] = jnp.zeros_like(total_two)
+    total_one[...] = jnp.zeros_like(total_one)
+    for move in moves:
+        move.wait()
+
     def spread(r, carry):
         spread_columns(window, r, spread_two, r)
         return carry
@@ -231,9 +254,6 @@
     for r in range(TR + 2):
         spread_columns(window_one, r, spread_one, r)
     feat_one[...] = convolve(spread_one, 0, weight)
-    grad_rows[...] = jnp.zeros_like(grad_rows)
-    total_two[...] = jnp.zeros_like(total_two)
-    total_one[...] = jnp.zeros_like(total_one)
 
     def first_row(k):
         return TR * (partners[0, k] - index + RADIUS)
@@ -324,7 +344,7 @@
         out_specs=[pl.BlockSpec(memory_space=space) for space in out_spaces],
         out_shape=[jax.ShapeDtypeStruct(*out) for out in outs],
         scratch_shapes=scratch,
-        compiler_params=pltpu.CompilerParams(vmem_limit_bytes=LIMIT << 20),
+        compiler_params=pltpu.CompilerParams(vmem_limit_bytes=LIMIT),
         name=name,
     )(*args)
 
@@ -339,6 +359,9 @@
         return lax.ppermute(block, "tile", route[name])
 
     row_block = (1, TC, CIN)
+    frames = [
+        pltpu.with_memory_space_constraint(frame, pltpu.HBM) for frame in (frame_one, frame_two)
+    ]
     weight = conv_weight.reshape(9 * CIN, CH)
     direct = send(frame_two, "ahead")
     near = send(frame_two, "behind")
@@ -346,7 +369,7 @@
         rows_kernel,
         [(row_block, bf16)] * 3,
         [pltpu.SemaphoreType.DMA((3,))],
-        [pltpu.with_memory_space_constraint(x, pltpu.HBM) for x in (frame_one, frame_two)],
+        frames,
         "rows",
         [pltpu.HBM] * 2,
         [pltpu.HBM] * 3,
@@ -401,12 +424,12 @@
         work_kernel,
         outs,
         [pltpu.VMEM(*out) for out in outs]
-        + [pltpu.SemaphoreType.DMA((len(outs),))]
+        + [pltpu.SemaphoreType.DMA((len(outs),)), pltpu.SemaphoreType.DMA((10,))]
         + [pltpu.VMEM(*item) for item in scratch],
-        [partners, counts, frame_one, frame_two, near, direct, far, cross]
+        [partners, counts, *frames, near, direct, far, cross]
         + [from_sibling, weight, pool, unpool, targets],
         "work",
-        [pltpu.SMEM] * 2 + [pltpu.VMEM] * 11,
+        [pltpu.SMEM] * 2 + [pl.ANY] * 7 + [pltpu.VMEM] * 4,
         [pltpu.HBM] * len(outs),
     )
     row = lax.broadcasted_iota(jnp.int32, (TR, 1, 1), 0)

time: 70.3 us -> 68 us (0.967)
  starting transfers between devices: 22.3 us -> 27 us
  Pallas kernels: 27.4 us -> 23.2 us
  other arithmetic: 4.1 us -> 1.42 us
  local copies, waits for them, and re-layouts: 1.82 us -> 0.91 us
  waiting for transfers between devices: 12 us -> 12.9 us
    ppermute x9, starting transfers between devices: 22.3 us -> 27 us  [send(): return lax.ppermute(block, 'tile', route[name])]
    pallas_call x3, Pallas kernels: 27.4 us -> 23.2 us  [call(): pl.pallas_call(kernel, in_specs=[pl.BlockSpec(memory_space=space) for spa...]
    convert_element_type x1, other arithmetic: 1.01 us -> 0.06 us  [on_device(): ahead_in = (ahead + back_sibling[TR:2 * TR].astype(f32)).astype(bf16)]
    convert_element_type x1, other arithmetic: 2.01 us -> 1.07 us  [on_device(): return (grad_one.astype(bf16), grad_two.astype(bf16))]
    unnamed x14 -> x10, local copies, waits for them, and re-layouts: 1.82 us -> 0.91 us
    ppermute x9, waiting for transfers between devices: 12 us -> 12.9 us  [send(): return lax.ppermute(block, 'tile', route[name])]
    broadcast_in_dim x1, other arithmetic: 0.8 us -> 0.01 us  [on_device(): edge = jnp.where(facing, back_sibling[2 * TR:2 * TR + 1].astype(f32), 0.0)]
  transfers between devices with their start and end apart: 9 -> 9, of which waited for: 3 -> 3; matrix products, arithmetic and copies ran while one was open for 3% -> 0% of each run, Pallas kernels for 3% -> 3%
where the time goes in v8:
time: 68 us; the launch traced here: 66.9 us
  starting transfers between devices  27 us (40%)
  Pallas kernels  23.2 us (34%)
  waiting for transfers between devices  12.9 us (19%)
  between operations  1.49 us (2%)
  other arithmetic  1.42 us (2%)
  local copies, waits for them, and re-layouts  0.91 us (1%)
    ppermute x9, starting transfers between devices, send(): return lax.ppermute(block, 'tile', route[name])  27 us
    pallas_call x3, Pallas kernels, call(): pl.pallas_call(kernel, in_specs=[pl.BlockSpec(memory_space=space) for spa...  23.2 us
    ppermute x9, waiting for transfers between devices, send(): return lax.ppermute(block, 'tile', route[name])  12.9 us
  transfers between devices with their start and end apart: 9, of which 3 were waited for; matrix products, arithmetic and copies ran while one was open for 0% of the time, Pallas kernels for 3%

profile of v8, /device:TPU:9, one launch (start us, length us, event | category | flops | bytes accessed | tf_op | source)
XLA Modules:
  0.0 66.9 jit_solution(9125567461150453613)
XLA Ops:
  0.6 0.0 copy-start.4
  0.6 3.2 %collective-permute-start.1 = (bf16[8,128,128]{2,1,0:T(8,128)(2,1)}, bf16[8,128,128]{2,1,0:T(8,128)(2,1)S(1)}, u32[]{:S(2)}, u32[]{:S(2)}) collective-permute-start(bf16[8,128,128]{2,1,0:T(8,128)(2,1)} %own_two.1), channel_id=1, source_target_pairs={{0,2},{2,4},{3,1},{4,6},{5,3},{6,8},{7,5},{8,10},{9,7},{10,12},{11... | collective-permute-start | bytes 786440 | tf_op jit(solution)/shard_map/ppermute | solution.py:359
  3.8 2.3 %collective-permute-start = (bf16[8,128,128]{2,1,0:T(8,128)(2,1)}, bf16[8,128,128]{2,1,0:T(8,128)(2,1)S(1)}, u32[]{:S(2)}, u32[]{:S(2)}) collective-permute-start(bf16[8,128,128]{2,1,0:T(8,128)(2,1)} %own_two.1), channel_id=1, source_target_pairs={{1,3},{2,0},{3,5},{4,2},{5,7},{6,4},{7,9},{8,6},{9,11},{10,8},{11,... | collective-permute-start | bytes 786440 | tf_op jit(solution)/shard_map/ppermute | solution.py:359
  6.1 0.8 %rows.1 = (bf16[1,128,128]{2,1,0:T(8,128)(2,1)S(1)}, bf16[1,128,128]{2,1,0:T(8,128)(2,1)S(1)}, bf16[1,128,128]{2,1,0:T(8,128)(2,1)S(1)}) custom-call(bf16[8,128,128]{2,1,0:T(8,128)(2,1)} %own_one.1, bf16[8,128,128]{2,1,0:T(8,128)(2,1)} %own_two.1), custom_call_target="tpu_custom_call" | custom-call | tf_op jit(solution)/shard_map/rows/pallas_call | solution.py:341
  6.9 5.2 %collective-permute-start.2 = (bf16[1,128,128]{2,1,0:T(8,128)(2,1)S(1)}, bf16[1,128,128]{2,1,0:T(8,128)(2,1)S(1)}, u32[]{:S(2)}, u32[]{:S(2)}) collective-permute-start(bf16[1,128,128]{2,1,0:T(8,128)(2,1)S(1)} %get-tuple-element.19), channel_id=1, source_target_pairs={{1,4},{3,6},{4,1},{5,8},{6,3},{7,10},{8,5},{9,12},{10,7},{11,14},{... | collective-permute-start | bytes 98312 | tf_op jit(solution)/shard_map/ppermute | solution.py:359
  12.2 1.9 %collective-permute-start.3 = (bf16[1,128,128]{2,1,0:T(8,128)(2,1)S(1)}, bf16[1,128,128]{2,1,0:T(8,128)(2,1)S(1)}, u32[]{:S(2)}, u32[]{:S(2)}) collective-permute-start(bf16[1,128,128]{2,1,0:T(8,128)(2,1)S(1)} %get-tuple-element.20), channel_id=1, source_target_pairs={{1,2},{2,1},{3,4},{4,3},{5,6},{6,5},{7,8},{8,7},{9,10},{10,9},{11,... | collective-permute-start | bytes 98312 | tf_op jit(solution)/shard_map/ppermute | solution.py:359
  14.1 1.0 %tables.1 = (bf16[384,1024]{1,0:T(8,128)(2,1)S(1)}, bf16[1024,384]{1,0:T(8,128)(2,1)S(1)}) custom-call(), custom_call_target="tpu_custom_call" | custom-call | tf_op jit(solution)/shard_map/tables/pallas_call | solution.py:341
  15.1 0.9 %copy-done = bf16[1024,384]{1,0:T(8,128)(2,1)} copy-done((bf16[1024,384]{1,0:T(8,128)(2,1)}, bf16[1024,384]{1,0:T(8,128)(2,1)S(1)}, u32[]{:S(2)}) %copy-start) | copy-done | bytes 786456
  16.0 0.0 collective-permute-done.2.far
  16.0 1.5 %collective-permute-done.3.cross = bf16[1,128,128]{2,1,0:T(8,128)(2,1)S(1)} collective-permute-done((bf16[1,128,128]{2,1,0:T(8,128)(2,1)S(1)}, bf16[1,128,128]{2,1,0:T(8,128)(2,1)S(1)}, u32[]{:S(2)}, u32[]{:S(2)}) %collective-permute-start.3) | collective-permute-done | bytes 32800 | tf_op jit(solution)/shard_map/ppermute | solution.py:359
  17.5 0.0 copy-start.2
  17.5 0.1 pad_maximum_fusion
  17.6 0.1 collective-permute-start.4
  18.4 0.0 copy-start.3
  18.4 1.3 %collective-permute-done.4.from_sibling = bf16[18,128,128]{2,1,0:T(8,128)(2,1)S(1)} collective-permute-done((bf16[18,128,128]{2,1,0:T(8,128)(2,1)S(1)}, bf16[18,128,128]{2,1,0:T(8,128)(2,1)S(1)}, u32[]{:S(2)}, u32[]{:S(2)}) %collective-permute-start.4) | collective-permute-done | bytes 589856 | tf_op jit(solution)/shard_map/ppermute | solution.py:359
  19.7 21.4 %work.1 = (bf16[19,128,128]{2,1,0:T(8,128)(2,1)}, f32[8,128,128]{2,1,0:T(8,128)S(1)}, f32[8,128,128]{2,1,0:T(8,128)S(1)}, bf16[1,128,128]{2,1,0:T(8,128)(2,1)S(1...) custom-call(s32[1,4]{1,0:T(1,128)S(1)} %copy-done.3, s32[1]{0:T(128)S(6)} %copy.8.counts, ...), custom_call_target="tpu_custom_call" | custom-call | tf_op jit(solution)/shard_map/work/pallas_call | solution.py:341
  41.1 4.9 %collective-permute-start.5 = (bf16[19,128,128]{2,1,0:T(8,128)(2,1)}, bf16[19,128,128]{2,1,0:T(8,128)(2,1)S(1)}, u32[]{:S(2)}, u32[]{:S(2)}) collective-permute-start(bf16[19,128,128]{2,1,0:T(8,128)(2,1)} %get-tuple-element.29), channel_id=1, source_target_pairs={{0,1},{1,0},{2,3},{3,2},{4,5},{5,4},{6,7},{7,6},{8,9},{9,8},{10,11... | collective-permute-start | bytes 1867784 | tf_op jit(solution)/shard_map/ppermute | solution.py:359
  46.0 3.5 %collective-permute-start.8 = (bf16[1,128,128]{2,1,0:T(8,128)(2,1)S(1)}, bf16[1,128,128]{2,1,0:T(8,128)(2,1)S(1)}, u32[]{:S(2)}, u32[]{:S(2)}) collective-permute-start(bf16[1,128,128]{2,1,0:T(8,128)(2,1)S(1)} %get-tuple-element.33), channel_id=1, source_target_pairs={{1,4},{3,6},{4,1},{5,8},{6,3},{7,10},{8,5},{9,12},{10,7},{11,14},{... | collective-permute-start | bytes 98312 | tf_op jit(solution)/shard_map/ppermute | solution.py:359
  49.6 0.1 add_convert_fusion.3
  49.7 4.0 %collective-permute-start.6 = (bf16[9,128,128]{2,1,0:T(8,128)(2,1)S(1)}, bf16[9,128,128]{2,1,0:T(8,128)(2,1)S(1)}, u32[]{:S(2)}, u32[]{:S(2)}) collective-permute-start(bf16[9,128,128]{2,1,0:T(8,128)(2,1)S(1)} %pad_maximum_fusion.1), channel_id=1, source_target_pairs={{0,2},{2,4},{3,1},{4,6},{5,3},{6,8},{7,5},{8,10},{9,7},{10,12},{11... | collective-permute-start | bytes 884744 | tf_op jit(solution)/shard_map/ppermute | solution.py:359
  53.7 0.1 add_convert_fusion.1
  53.8 1.9 %collective-permute-start.7 = (bf16[8,128,128]{2,1,0:T(8,128)(2,1)S(1)}, bf16[8,128,128]{2,1,0:T(8,128)(2,1)S(1)}, u32[]{:S(2)}, u32[]{:S(2)}) collective-permute-start(bf16[8,128,128]{2,1,0:T(8,128)(2,1)S(1)} %add_convert_fusion.1), channel_id=1, source_target_pairs={{1,3},{2,0},{3,5},{4,2},{5,7},{6,4},{7,9},{8,6},{9,11},{10,8},{11,... | collective-permute-start | bytes 786440 | tf_op jit(solution)/shard_map/ppermute | solution.py:359
  55.7 10.1 %collective-permute-done.6 = bf16[9,128,128]{2,1,0:T(8,128)(2,1)S(1)} collective-permute-done((bf16[9,128,128]{2,1,0:T(8,128)(2,1)S(1)}, bf16[9,128,128]{2,1,0:T(8,128)(2,1)S(1)}, u32[]{:S(2)}, u32[]{:S(2)}) %collective-permute-start.6) | collective-permute-done | bytes 294944 | tf_op jit(solution)/shard_map/ppermute | solution.py:359
  65.8 1.1 %add_convert_fusion = (bf16[8,128,128]{2,1,0:T(8,128)(2,1)}, bf16[8,128,128]{2,1,0:T(8,128)(2,1)}) fusion(bf16[8,128,128]{2,1,0:T(8,128)(2,1)S(1)} %collective-permute-done.7, f32[8,128,128]{2,1,0:T(8,128)S(1)} %get-tuple-element.31, bf16[9,128,128]{2,1,0:T(8,128)(2,1)S(1)} %collective-permute-done.6, bf16[19,128,128]{2,1,0:T(8,128)(2,1)S(1)} %collective-permute-done.5, ...), kind=kLoop, calls=%fused_computation.1 | loop fusion | flops 1835008 | bytes 2555920 | tf_op jit(solution)/shard_map/convert_element_type | solution.py:454
  (18 shorter events, 0.1 us)
Async XLA Ops:
  0.6 16.9 %copy-start.4 = (bf16[8,128,128]{2,1,0:T(8,128)(2,1)S(1)}, bf16[8,128,128]{2,1,0:T(8,128)(2,1)}, u32[]{:S(2)}) copy-start(bf16[8,128,128]{2,1,0:T(8,128)(2,1)} %own_two.1) | copy-start | bytes 786436
  0.6 16.8 %collective-permute-start.1 = (bf16[8,128,128]{2,1,0:T(8,128)(2,1)}, bf16[8,128,128]{2,1,0:T(8,128)(2,1)S(1)}, u32[]{:S(2)}, u32[]{:S(2)}) collective-permute-start(bf16[8,128,128]{2,1,0:T(8,128)(2,1)} %own_two.1), channel_id=1, source_target_pairs={{0,2},{2,4},{3,1},{4,6},{5,3},{6,8},{7,5},{8,10},{9,7},{10,12},{11... | collective-permute-start | bytes 786440 | tf_op jit(solution)/shard_map/ppermute | solution.py:359
  3.8 13.7 %collective-permute-start = (bf16[8,128,128]{2,1,0:T(8,128)(2,1)}, bf16[8,128,128]{2,1,0:T(8,128)(2,1)S(1)}, u32[]{:S(2)}, u32[]{:S(2)}) collective-permute-start(bf16[8,128,128]{2,1,0:T(8,128)(2,1)} %own_two.1), channel_id=1, source_target_pairs={{1,3},{2,0},{3,5},{4,2},{5,7},{6,4},{7,9},{8,6},{9,11},{10,8},{11,... | collective-permute-start | bytes 786440 | tf_op jit(solution)/shard_map/ppermute | solution.py:359
  6.9 9.1 %collective-permute-start.2 = (bf16[1,128,128]{2,1,0:T(8,128)(2,1)S(1)}, bf16[1,128,128]{2,1,0:T(8,128)(2,1)S(1)}, u32[]{:S(2)}, u32[]{:S(2)}) collective-permute-start(bf16[1,128,128]{2,1,0:T(8,128)(2,1)S(1)} %get-tuple-element.19), channel_id=1, source_target_pairs={{1,4},{3,6},{4,1},{5,8},{6,3},{7,10},{8,5},{9,12},{10,7},{11,14},{... | collective-permute-start | bytes 98312 | tf_op jit(solution)/shard_map/ppermute | solution.py:359
  12.2 5.3 %collective-permute-start.3 = (bf16[1,128,128]{2,1,0:T(8,128)(2,1)S(1)}, bf16[1,128,128]{2,1,0:T(8,128)(2,1)S(1)}, u32[]{:S(2)}, u32[]{:S(2)}) collective-permute-start(bf16[1,128,128]{2,1,0:T(8,128)(2,1)S(1)} %get-tuple-element.20), channel_id=1, source_target_pairs={{1,2},{2,1},{3,4},{4,3},{5,6},{6,5},{7,8},{8,7},{9,10},{10,9},{11,... | collective-permute-start | bytes 98312 | tf_op jit(solution)/shard_map/ppermute | solution.py:359
  15.1 0.9 %copy-start = (bf16[1024,384]{1,0:T(8,128)(2,1)}, bf16[1024,384]{1,0:T(8,128)(2,1)S(1)}, u32[]{:S(2)}) copy-start(bf16[1024,384]{1,0:T(8,128)(2,1)S(1)} %get-tuple-element.27.unpool) | copy-start | bytes 2359300
  17.5 2.2 %copy-start.1 = (bf16[3,3,128,256]{3,2,1,0:T(8,128)(2,1)S(1)}, bf16[3,3,128,256]{3,2,1,0:T(8,128)(2,1)}, u32[]{:S(2)}) copy-start(bf16[3,3,128,256]{3,2,1,0:T(8,128)(2,1)} %param.8) | copy-start | bytes 1769476
  17.5 2.2 %copy-start.2 = (s32[8,128]{1,0:T(8,128)S(1)}, s32[8,128]{1,0:T(8,128)}, u32[]{:S(2)}) copy-start(s32[8,128]{1,0:T(8,128)} %targets.1) | copy-start | bytes 12292
  17.6 2.1 %collective-permute-start.4 = (bf16[18,128,128]{2,1,0:T(8,128)(2,1)S(1)}, bf16[18,128,128]{2,1,0:T(8,128)(2,1)S(1)}, u32[]{:S(2)}, u32[]{:S(2)}) collective-permute-start(bf16[18,128,128]{2,1,0:T(8,128)(2,1)S(1)} %pad_maximum_fusion), channel_id=1, source_target_pairs={{0,1},{1,0},{2,3},{3,2},{4,5},{5,4},{6,7},{7,6},{8,9},{9,8},{10,11... | collective-permute-start | bytes 1769480 | tf_op jit(solution)/shard_map/ppermute | solution.py:359
  18.4 1.3 %copy-start.3 = (s32[1,4]{1,0:T(1,128)S(1)}, s32[1,4]{1,0:T(1,128)}, u32[]{:S(2)}) copy-start(s32[1,4]{1,0:T(1,128)} %partners.1) | copy-start | bytes 52
  41.1 8.5 %collective-permute-start.5 = (bf16[19,128,128]{2,1,0:T(8,128)(2,1)}, bf16[19,128,128]{2,1,0:T(8,128)(2,1)S(1)}, u32[]{:S(2)}, u32[]{:S(2)}) collective-permute-start(bf16[19,128,128]{2,1,0:T(8,128)(2,1)} %get-tuple-element.29), channel_id=1, source_target_pairs={{0,1},{1,0},{2,3},{3,2},{4,5},{5,4},{6,7},{7,6},{8,9},{9,8},{10,11... | collective-permute-start | bytes 1867784 | tf_op jit(solution)/shard_map/ppermute | solution.py:359
  46.0 9.7 %collective-permute-start.8 = (bf16[1,128,128]{2,1,0:T(8,128)(2,1)S(1)}, bf16[1,128,128]{2,1,0:T(8,128)(2,1)S(1)}, u32[]{:S(2)}, u32[]{:S(2)}) collective-permute-start(bf16[1,128,128]{2,1,0:T(8,128)(2,1)S(1)} %get-tuple-element.33), channel_id=1, source_target_pairs={{1,4},{3,6},{4,1},{5,8},{6,3},{7,10},{8,5},{9,12},{10,7},{11,14},{... | collective-permute-start | bytes 98312 | tf_op jit(solution)/shard_map/ppermute | solution.py:359
  49.7 16.2 %collective-permute-start.6 = (bf16[9,128,128]{2,1,0:T(8,128)(2,1)S(1)}, bf16[9,128,128]{2,1,0:T(8,128)(2,1)S(1)}, u32[]{:S(2)}, u32[]{:S(2)}) collective-permute-start(bf16[9,128,128]{2,1,0:T(8,128)(2,1)S(1)} %pad_maximum_fusion.1), channel_id=1, source_target_pairs={{0,2},{2,4},{3,1},{4,6},{5,3},{6,8},{7,5},{8,10},{9,7},{10,12},{11... | collective-permute-start | bytes 884744 | tf_op jit(solution)/shard_map/ppermute | solution.py:359
  53.8 12.0 %collective-permute-start.7 = (bf16[8,128,128]{2,1,0:T(8,128)(2,1)S(1)}, bf16[8,128,128]{2,1,0:T(8,128)(2,1)S(1)}, u32[]{:S(2)}, u32[]{:S(2)}) collective-permute-start(bf16[8,128,128]{2,1,0:T(8,128)(2,1)S(1)} %add_convert_fusion.1), channel_id=1, source_target_pairs={{1,3},{2,0},{3,5},{4,2},{5,7},{6,4},{7,9},{8,6},{9,11},{10,8},{11,... | collective-permute-start | bytes 786440 | tf_op jit(solution)/shard_map/ppermute | solution.py:359

commit v9 on v8

--- a/solution.py
+++ b/solution.py
@@ -169,12 +169,14 @@
     ahead_hbm,
     behind_hbm,
     far_hbm,
+    edge_hbm,
     sum_one_hbm,
     sum_two_hbm,
     to_sibling,
     ahead,
     behind,
     far_out,
+    edge_out,
     sum_one,
     sum_two,
     sems,
@@ -309,28 +311,30 @@
     def out(n, block, target):
         return pltpu.make_async_copy(block, target, sems.at[n])
 
-    behind[...] = rows(total_two, at(-2 * side), TR)
+    behind[...] = rows(total_two, at(-2 * side), TR).astype(jnp.bfloat16)
     out(0, behind, behind_hbm).start()
     far_out[...] = rows(total_two, edge(-side)).astype(jnp.bfloat16)
     out(1, far_out, far_hbm).start()
+    edge_out[...] = rows(total_two, edge(side)).astype(jnp.bfloat16)
+    out(6, edge_out, edge_hbm).start()
     ahead[...] = rows(total_two, at(2 * side), TR)
     out(2, ahead, ahead_hbm).start()
     sum_two[...] = rows(total_two, at(0), TR)
     out(3, sum_two, sum_two_hbm).start()
     to_sibling[0:TR] = rows(total_two, at(side), TR).astype(jnp.bfloat16)
     to_sibling[TR : 2 * TR] = rows(total_two, at(-side), TR).astype(jnp.bfloat16)
-    to_sibling[2 * TR : 2 * TR + 1] = rows(total_two, edge(side)).astype(jnp.bfloat16)
     spread_back(grad_rows, moved)
     convolve_back(moved, weight_back, total_one, 0)
     facing = jnp.where(side > 0, TR + 1, 0)
     outer = jnp.where(side > 0, 0, TR + 1)
-    to_sibling[2 * TR + 1 : 2 * TR + 2] = rows(total_one, facing).astype(jnp.bfloat16)
-    to_sibling[2 * TR + 2 : 2 * TR + 3] = rows(total_one, outer).astype(jnp.bfloat16)
+    to_sibling[2 * TR : 2 * TR + 1] = rows(total_one, facing).astype(jnp.bfloat16)
+    to_sibling[2 * TR + 1 : 2 * TR + 2] = rows(total_one, outer).astype(jnp.bfloat16)
     out(4, to_sibling, to_sibling_hbm).start()
     sum_one[...] = rows(total_one, 1, TR)
     out(5, sum_one, sum_one_hbm).start()
     out(0, behind, behind_hbm).wait()
     out(1, far_out, far_hbm).wait()
+    out(6, edge_out, edge_hbm).wait()
     out(2, ahead, ahead_hbm).wait()
     out(3, sum_two, sum_two_hbm).wait()
     out(4, to_sibling, to_sibling_hbm).wait()
@@ -394,11 +398,12 @@
     from_sibling = send(payload, "swap")
 
     tile = (TR, TC, CIN)
-    pack = (2 * TR + 3, TC, CIN)
+    pack = (2 * TR + 2, TC, CIN)
     outs = [
         (pack, bf16),
         (tile, f32),
-        (tile, f32),
+        (tile, bf16),
+        ((1, TC, CIN), bf16),
         ((1, TC, CIN), bf16),
         (tile, f32),
         (tile, f32),
@@ -420,7 +425,7 @@
         ((WIN * TC, CIN), f32),
         (((TR + 2) * TC, CIN), f32),
     ]
-    to_sibling, ahead, behind, far_out, sum_one, sum_two = call(
+    to_sibling, ahead, behind, far_out, edge, sum_one, sum_two = call(
         work_kernel,
         outs,
         [pltpu.VMEM(*out) for out in outs]
@@ -437,20 +442,20 @@
     outer = row == jnp.where(side > 0, 0, TR - 1)
     back_sibling = send(to_sibling, "swap")
     ahead_in = (ahead + back_sibling[TR : 2 * TR].astype(f32)).astype(bf16)
-    edge = jnp.where(facing, back_sibling[2 * TR : 2 * TR + 1].astype(f32), 0.0)
-    behind_in = (behind + edge).astype(bf16)
-    back_ahead = send(jnp.concatenate([ahead_in, back_sibling[2 * TR + 2 :]]), "ahead")
-    back_behind = send(behind_in, "behind")
+    back_behind = send(behind, "behind")
+    ahead_in = jnp.concatenate([ahead_in, back_sibling[2 * TR + 1 :], edge])
+    back_ahead = send(ahead_in, "ahead")
+    back_edge = send(back_ahead[TR + 1 :], "swap")
     back_far = send(far_out, "far")
 
     def place(where, block):
         return jnp.where(where, block.astype(f32), 0.0)
 
-    grad_one = sum_one + place(facing, back_sibling[2 * TR + 1 : 2 * TR + 2])
-    grad_one = grad_one + place(outer, back_ahead[TR:])
+    grad_one = sum_one + place(facing, back_sibling[2 * TR : 2 * TR + 1])
+    grad_one = grad_one + place(outer, back_ahead[TR : TR + 1])
     grad_two = sum_two + back_sibling[:TR].astype(f32) + back_ahead[:TR].astype(f32)
     grad_two = grad_two + back_behind.astype(f32)
-    grad_two = grad_two + place(outer, back_far)
+    grad_two = grad_two + place(outer, back_far) + place(facing, back_edge)
     return grad_one.astype(bf16), grad_two.astype(bf16)
 
 

time: 68 us -> 68.8 us (1.012)
  the two profiles are of different devices: /device:TPU:9 before, /device:TPU:23 now
where the time goes in v9:
time: 68.8 us; the launch traced here: 68.4 us
  Pallas kernels  26.8 us (39%)
  starting transfers between devices  26.3 us (38%)
  waiting for transfers between devices  12.5 us (18%)
  between operations  1.46 us (2%)
  other arithmetic  1.35 us (2%)
    pallas_call x3, Pallas kernels, call(): pl.pallas_call(kernel, in_specs=[pl.BlockSpec(memory_space=space) for spa...  26.8 us
    ppermute x10, starting transfers between devices, send(): return lax.ppermute(block, 'tile', route[name])  26.3 us
    ppermute x10, waiting for transfers between devices, send(): return lax.ppermute(block, 'tile', route[name])  12.5 us
  transfers between devices with their start and end apart: 10, of which 6 were waited for; matrix products, arithmetic and copies ran while one was open for 0% of the time, Pallas kernels for 3%

profile of v9, /device:TPU:23, one launch (start us, length us, event | category | flops | bytes accessed | tf_op | source)
XLA Modules:
  0.0 68.4 jit_solution(15819903205588475093)
XLA Ops:
  0.6 0.0 copy-start.3
  0.6 2.3 %collective-permute-start.1 = (bf16[8,128,128]{2,1,0:T(8,128)(2,1)}, bf16[8,128,128]{2,1,0:T(8,128)(2,1)S(1)}, u32[]{:S(2)}, u32[]{:S(2)}) collective-permute-start(bf16[8,128,128]{2,1,0:T(8,128)(2,1)} %own_two.1), channel_id=1, source_target_pairs={{0,2},{2,4},{3,1},{4,6},{5,3},{6,8},{7,5},{8,10},{9,7},{10,12},{11... | collective-permute-start | bytes 786440 | tf_op jit(solution)/shard_map/ppermute | solution.py:363
  2.9 4.0 %collective-permute-start = (bf16[8,128,128]{2,1,0:T(8,128)(2,1)}, bf16[8,128,128]{2,1,0:T(8,128)(2,1)S(1)}, u32[]{:S(2)}, u32[]{:S(2)}) collective-permute-start(bf16[8,128,128]{2,1,0:T(8,128)(2,1)} %own_two.1), channel_id=1, source_target_pairs={{1,3},{2,0},{3,5},{4,2},{5,7},{6,4},{7,9},{8,6},{9,11},{10,8},{11,... | collective-permute-start | bytes 786440 | tf_op jit(solution)/shard_map/ppermute | solution.py:363
  7.0 0.8 %rows.1 = (bf16[1,128,128]{2,1,0:T(8,128)(2,1)S(1)}, bf16[1,128,128]{2,1,0:T(8,128)(2,1)S(1)}, bf16[1,128,128]{2,1,0:T(8,128)(2,1)S(1)}) custom-call(bf16[8,128,128]{2,1,0:T(8,128)(2,1)} %own_one.1, bf16[8,128,128]{2,1,0:T(8,128)(2,1)} %own_two.1), custom_call_target="tpu_custom_call" | custom-call | tf_op jit(solution)/shard_map/rows/pallas_call | solution.py:345
  7.8 3.4 %collective-permute-start.2 = (bf16[1,128,128]{2,1,0:T(8,128)(2,1)S(1)}, bf16[1,128,128]{2,1,0:T(8,128)(2,1)S(1)}, u32[]{:S(2)}, u32[]{:S(2)}) collective-permute-start(bf16[1,128,128]{2,1,0:T(8,128)(2,1)S(1)} %get-tuple-element.20), channel_id=1, source_target_pairs={{1,4},{3,6},{4,1},{5,8},{6,3},{7,10},{8,5},{9,12},{10,7},{11,14},{... | collective-permute-start | bytes 98312 | tf_op jit(solution)/shard_map/ppermute | solution.py:363
  11.3 2.8 %collective-permute-start.3 = (bf16[1,128,128]{2,1,0:T(8,128)(2,1)S(1)}, bf16[1,128,128]{2,1,0:T(8,128)(2,1)S(1)}, u32[]{:S(2)}, u32[]{:S(2)}) collective-permute-start(bf16[1,128,128]{2,1,0:T(8,128)(2,1)S(1)} %get-tuple-element.21), channel_id=1, source_target_pairs={{1,2},{2,1},{3,4},{4,3},{5,6},{6,5},{7,8},{8,7},{9,10},{10,9},{11,... | collective-permute-start | bytes 98312 | tf_op jit(solution)/shard_map/ppermute | solution.py:363
  14.0 1.0 %tables.1 = (bf16[384,1024]{1,0:T(8,128)(2,1)S(1)}, bf16[1024,384]{1,0:T(8,128)(2,1)S(1)}) custom-call(), custom_call_target="tpu_custom_call" | custom-call | tf_op jit(solution)/shard_map/tables/pallas_call | solution.py:345
  15.1 2.4 %collective-permute-done.3.cross = bf16[1,128,128]{2,1,0:T(8,128)(2,1)S(1)} collective-permute-done((bf16[1,128,128]{2,1,0:T(8,128)(2,1)S(1)}, bf16[1,128,128]{2,1,0:T(8,128)(2,1)S(1)}, u32[]{:S(2)}, u32[]{:S(2)}) %collective-permute-start.3) | collective-permute-done | bytes 32800 | tf_op jit(solution)/shard_map/ppermute | solution.py:363
  17.5 0.5 collective-permute-done.near
  18.0 0.1 pad_maximum_fusion
  18.1 1.0 %collective-permute-start.4 = (bf16[18,128,128]{2,1,0:T(8,128)(2,1)S(1)}, bf16[18,128,128]{2,1,0:T(8,128)(2,1)S(1)}, u32[]{:S(2)}, u32[]{:S(2)}) collective-permute-start(bf16[18,128,128]{2,1,0:T(8,128)(2,1)S(1)} %pad_maximum_fusion), channel_id=1, source_target_pairs={{0,1},{1,0},{2,3},{3,2},{4,5},{5,4},{6,7},{7,6},{8,9},{9,8},{10,11... | collective-permute-start | bytes 1769480 | tf_op jit(solution)/shard_map/ppermute | solution.py:363
  19.7 0.0 copy-start.2
  19.7 1.0 %collective-permute-done.4.from_sibling = bf16[18,128,128]{2,1,0:T(8,128)(2,1)S(1)} collective-permute-done((bf16[18,128,128]{2,1,0:T(8,128)(2,1)S(1)}, bf16[18,128,128]{2,1,0:T(8,128)(2,1)S(1)}, u32[]{:S(2)}, u32[]{:S(2)}) %collective-permute-start.4) | collective-permute-done | bytes 589856 | tf_op jit(solution)/shard_map/ppermute | solution.py:363
  20.7 25.0 %work.1 = (bf16[18,128,128]{2,1,0:T(8,128)(2,1)S(1)}, f32[8,128,128]{2,1,0:T(8,128)S(1)}, bf16[8,128,128]{2,1,0:T(8,128)(2,1)S(1)}, bf16[1,128,128]{2,1,0:T(8,12...) custom-call(s32[1,4]{1,0:T(1,128)S(1)} %copy-done.2, ...), custom_call_target="tpu_custom_call" | custom-call | tf_op jit(solution)/shard_map/work/pallas_call | solution.py:345
  45.7 0.4 collective-permute-start.5
  46.1 1.6 %collective-permute-done.5 = bf16[18,128,128]{2,1,0:T(8,128)(2,1)S(1)} collective-permute-done((bf16[18,128,128]{2,1,0:T(8,128)(2,1)S(1)}, bf16[18,128,128]{2,1,0:T(8,128)(2,1)S(1)}, u32[]{:S(2)}, u32[]{:S(2)}) %collective-permute-start.5) | collective-permute-done | bytes 589856 | tf_op jit(solution)/shard_map/ppermute | solution.py:363
  47.7 0.1 add_convert_fusion.2
  47.9 1.9 %collective-permute-start.6 = (bf16[10,128,128]{2,1,0:T(8,128)(2,1)S(1)}, bf16[10,128,128]{2,1,0:T(8,128)(2,1)S(1)}, u32[]{:S(2)}, u32[]{:S(2)}) collective-permute-start(bf16[10,128,128]{2,1,0:T(8,128)(2,1)S(1)} %pad_maximum_fusion.1), channel_id=1, source_target_pairs={{0,2},{2,4},{3,1},{4,6},{5,3},{6,8},{7,5},{8,10},{9,7},{10,12},{11... | collective-permute-start | bytes 983048 | tf_op jit(solution)/shard_map/ppermute | solution.py:363
  49.8 1.9 %collective-permute-start.8 = (bf16[1,128,128]{2,1,0:T(8,128)(2,1)S(1)}, bf16[1,128,128]{2,1,0:T(8,128)(2,1)S(1)}, u32[]{:S(2)}, u32[]{:S(2)}) collective-permute-start(bf16[1,128,128]{2,1,0:T(8,128)(2,1)S(1)} %get-tuple-element.35), channel_id=1, source_target_pairs={{1,4},{3,6},{4,1},{5,8},{6,3},{7,10},{8,5},{9,12},{10,7},{11,14},{... | collective-permute-start | bytes 98312 | tf_op jit(solution)/shard_map/ppermute | solution.py:363
  51.7 3.0 %collective-permute-start.7 = (bf16[8,128,128]{2,1,0:T(8,128)(2,1)S(1)}, bf16[8,128,128]{2,1,0:T(8,128)(2,1)S(1)}, u32[]{:S(2)}, u32[]{:S(2)}) collective-permute-start(bf16[8,128,128]{2,1,0:T(8,128)(2,1)S(1)} %get-tuple-element.34), channel_id=1, source_target_pairs={{1,3},{2,0},{3,5},{4,2},{5,7},{6,4},{7,9},{8,6},{9,11},{10,8},{11,... | collective-permute-start | bytes 786440 | tf_op jit(solution)/shard_map/ppermute | solution.py:363
  54.8 6.1 %collective-permute-done.6 = bf16[10,128,128]{2,1,0:T(8,128)(2,1)S(1)} collective-permute-done((bf16[10,128,128]{2,1,0:T(8,128)(2,1)S(1)}, bf16[10,128,128]{2,1,0:T(8,128)(2,1)S(1)}, u32[]{:S(2)}, u32[]{:S(2)}) %collective-permute-start.6) | collective-permute-done | bytes 327712 | tf_op jit(solution)/shard_map/ppermute | solution.py:363
  60.9 5.5 %collective-permute-start.9 = (bf16[1,128,128]{2,1,0:T(8,128)(2,1)S(1)}, bf16[1,128,128]{2,1,0:T(8,128)(2,1)S(1)}, u32[]{:S(2)}, u32[]{:S(2)}) collective-permute-start(bf16[1,128,128]{2,1,0:T(8,128)(2,1)S(1)} %get-tuple-element.38), channel_id=1, source_target_pairs={{0,1},{1,0},{2,3},{3,2},{4,5},{5,4},{6,7},{7,6},{8,9},{9,8},{10,11... | collective-permute-start | bytes 98312 | tf_op jit(solution)/shard_map/ppermute | solution.py:363
  66.4 0.8 %collective-permute-done.9 = bf16[1,128,128]{2,1,0:T(8,128)(2,1)S(1)} collective-permute-done((bf16[1,128,128]{2,1,0:T(8,128)(2,1)S(1)}, bf16[1,128,128]{2,1,0:T(8,128)(2,1)S(1)}, u32[]{:S(2)}, u32[]{:S(2)}) %collective-permute-start.9) | collective-permute-done | bytes 32800 | tf_op jit(solution)/shard_map/ppermute | solution.py:363
  67.3 1.1 %add_convert_fusion = (bf16[8,128,128]{2,1,0:T(8,128)(2,1)}, bf16[8,128,128]{2,1,0:T(8,128)(2,1)}) fusion(bf16[8,128,128]{2,1,0:T(8,128)(2,1)S(1)} %collective-permute-done.7, f32[8,128,128]{2,1,0:T(8,128)S(1)} %get-tuple-element.33, bf16[10,128,128]{2,1,0:T(8,128)(2,1)S(1)} %collective-permute-done.6, bf16[18,128,128]{2,1,0:T(8,128)(2,1)S(1)} %collective-permute-done.5, ...), kind=kLoop, calls=%fused_computation.1 | loop fusion | flops 2097152 | bytes 2621456 | tf_op jit(solution)/shard_map/convert_element_type | solution.py:459
  (17 shorter events, 0.1 us)
Async XLA Ops:
  0.6 17.3 %copy-start.3 = (bf16[8,128,128]{2,1,0:T(8,128)(2,1)S(1)}, bf16[8,128,128]{2,1,0:T(8,128)(2,1)}, u32[]{:S(2)}) copy-start(bf16[8,128,128]{2,1,0:T(8,128)(2,1)} %own_two.1) | copy-start | bytes 786436
  0.6 16.9 %collective-permute-start.1 = (bf16[8,128,128]{2,1,0:T(8,128)(2,1)}, bf16[8,128,128]{2,1,0:T(8,128)(2,1)S(1)}, u32[]{:S(2)}, u32[]{:S(2)}) collective-permute-start(bf16[8,128,128]{2,1,0:T(8,128)(2,1)} %own_two.1), channel_id=1, source_target_pairs={{0,2},{2,4},{3,1},{4,6},{5,3},{6,8},{7,5},{8,10},{9,7},{10,12},{11... | collective-permute-start | bytes 786440 | tf_op jit(solution)/shard_map/ppermute | solution.py:363
  2.9 15.1 %collective-permute-start = (bf16[8,128,128]{2,1,0:T(8,128)(2,1)}, bf16[8,128,128]{2,1,0:T(8,128)(2,1)S(1)}, u32[]{:S(2)}, u32[]{:S(2)}) collective-permute-start(bf16[8,128,128]{2,1,0:T(8,128)(2,1)} %own_two.1), channel_id=1, source_target_pairs={{1,3},{2,0},{3,5},{4,2},{5,7},{6,4},{7,9},{8,6},{9,11},{10,8},{11,... | collective-permute-start | bytes 786440 | tf_op jit(solution)/shard_map/ppermute | solution.py:363
  7.8 7.2 %collective-permute-start.2 = (bf16[1,128,128]{2,1,0:T(8,128)(2,1)S(1)}, bf16[1,128,128]{2,1,0:T(8,128)(2,1)S(1)}, u32[]{:S(2)}, u32[]{:S(2)}) collective-permute-start(bf16[1,128,128]{2,1,0:T(8,128)(2,1)S(1)} %get-tuple-element.20), channel_id=1, source_target_pairs={{1,4},{3,6},{4,1},{5,8},{6,3},{7,10},{8,5},{9,12},{10,7},{11,14},{... | collective-permute-start | bytes 98312 | tf_op jit(solution)/shard_map/ppermute | solution.py:363
  11.3 6.2 %collective-permute-start.3 = (bf16[1,128,128]{2,1,0:T(8,128)(2,1)S(1)}, bf16[1,128,128]{2,1,0:T(8,128)(2,1)S(1)}, u32[]{:S(2)}, u32[]{:S(2)}) collective-permute-start(bf16[1,128,128]{2,1,0:T(8,128)(2,1)S(1)} %get-tuple-element.21), channel_id=1, source_target_pairs={{1,2},{2,1},{3,4},{4,3},{5,6},{6,5},{7,8},{8,7},{9,10},{10,9},{11,... | collective-permute-start | bytes 98312 | tf_op jit(solution)/shard_map/ppermute | solution.py:363
  17.5 3.2 %copy-start = (bf16[3,3,128,256]{3,2,1,0:T(8,128)(2,1)S(1)}, bf16[3,3,128,256]{3,2,1,0:T(8,128)(2,1)}, u32[]{:S(2)}) copy-start(bf16[3,3,128,256]{3,2,1,0:T(8,128)(2,1)} %param.8) | copy-start | bytes 1769476
  18.0 2.7 %copy-start.1 = (s32[8,128]{1,0:T(8,128)S(1)}, s32[8,128]{1,0:T(8,128)}, u32[]{:S(2)}) copy-start(s32[8,128]{1,0:T(8,128)} %targets.1) | copy-start | bytes 12292
  18.1 2.6 %collective-permute-start.4 = (bf16[18,128,128]{2,1,0:T(8,128)(2,1)S(1)}, bf16[18,128,128]{2,1,0:T(8,128)(2,1)S(1)}, u32[]{:S(2)}, u32[]{:S(2)}) collective-permute-start(bf16[18,128,128]{2,1,0:T(8,128)(2,1)S(1)} %pad_maximum_fusion), channel_id=1, source_target_pairs={{0,1},{1,0},{2,3},{3,2},{4,5},{5,4},{6,7},{7,6},{8,9},{9,8},{10,11... | collective-permute-start | bytes 1769480 | tf_op jit(solution)/shard_map/ppermute | solution.py:363
  19.7 1.0 %copy-start.2 = (s32[1,4]{1,0:T(1,128)S(1)}, s32[1,4]{1,0:T(1,128)}, u32[]{:S(2)}) copy-start(s32[1,4]{1,0:T(1,128)} %partners.1) | copy-start | bytes 52
  45.7 2.1 %collective-permute-start.5 = (bf16[18,128,128]{2,1,0:T(8,128)(2,1)S(1)}, bf16[18,128,128]{2,1,0:T(8,128)(2,1)S(1)}, u32[]{:S(2)}, u32[]{:S(2)}) collective-permute-start(bf16[18,128,128]{2,1,0:T(8,128)(2,1)S(1)} %get-tuple-element.30), channel_id=1, source_target_pairs={{0,1},{1,0},{2,3},{3,2},{4,5},{5,4},{6,7},{7,6},{8,9},{9,8},{10,11... | collective-permute-start | bytes 1769480 | tf_op jit(solution)/shard_map/ppermute | solution.py:363
  47.9 13.0 %collective-permute-start.6 = (bf16[10,128,128]{2,1,0:T(8,128)(2,1)S(1)}, bf16[10,128,128]{2,1,0:T(8,128)(2,1)S(1)}, u32[]{:S(2)}, u32[]{:S(2)}) collective-permute-start(bf16[10,128,128]{2,1,0:T(8,128)(2,1)S(1)} %pad_maximum_fusion.1), channel_id=1, source_target_pairs={{0,2},{2,4},{3,1},{4,6},{5,3},{6,8},{7,5},{8,10},{9,7},{10,12},{11... | collective-permute-start | bytes 983048 | tf_op jit(solution)/shard_map/ppermute | solution.py:363
  49.8 16.6 %collective-permute-start.8 = (bf16[1,128,128]{2,1,0:T(8,128)(2,1)S(1)}, bf16[1,128,128]{2,1,0:T(8,128)(2,1)S(1)}, u32[]{:S(2)}, u32[]{:S(2)}) collective-permute-start(bf16[1,128,128]{2,1,0:T(8,128)(2,1)S(1)} %get-tuple-element.35), channel_id=1, source_target_pairs={{1,4},{3,6},{4,1},{5,8},{6,3},{7,10},{8,5},{9,12},{10,7},{11,14},{... | collective-permute-start | bytes 98312 | tf_op jit(solution)/shard_map/ppermute | solution.py:363
  51.7 15.5 %collective-permute-start.7 = (bf16[8,128,128]{2,1,0:T(8,128)(2,1)S(1)}, bf16[8,128,128]{2,1,0:T(8,128)(2,1)S(1)}, u32[]{:S(2)}, u32[]{:S(2)}) collective-permute-start(bf16[8,128,128]{2,1,0:T(8,128)(2,1)S(1)} %get-tuple-element.34), channel_id=1, source_target_pairs={{1,3},{2,0},{3,5},{4,2},{5,7},{6,4},{7,9},{8,6},{9,11},{10,8},{11,... | collective-permute-start | bytes 786440 | tf_op jit(solution)/shard_map/ppermute | solution.py:363
  60.9 6.4 %collective-permute-start.9 = (bf16[1,128,128]{2,1,0:T(8,128)(2,1)S(1)}, bf16[1,128,128]{2,1,0:T(8,128)(2,1)S(1)}, u32[]{:S(2)}, u32[]{:S(2)}) collective-permute-start(bf16[1,128,128]{2,1,0:T(8,128)(2,1)S(1)} %get-tuple-element.38), channel_id=1, source_target_pairs={{0,1},{1,0},{2,3},{3,2},{4,5},{5,4},{6,7},{7,6},{8,9},{9,8},{10,11... | collective-permute-start | bytes 98312 | tf_op jit(solution)/shard_map/ppermute | solution.py:363
